TPU v7x, 32 devices: a whole 2x2x4 slice. The times are simulated.
32 devices in a mesh: row: 2 (over x), col: 16 (over z, y, core).
Axes of the slice: x: 2, y: 2, z: 4, core: 2. Of those that a mesh axis runs over, the one named last changes fastest.
Arguments:
- hidden_in: bfloat16 [8192, 768], P('col', 'row'), may hold values from -6 to 6
- cotangent: bfloat16 [8192, 768], P('col', 'row'), may hold values from -6 to 6
- lengths: int32 [2], replicated, may hold values from 1024 to 4096, as said below
- w_query: bfloat16 [768, 768], P('col', 'row'), may hold values from -0.21875 to 0.21875
- w_key: bfloat16 [768, 768], P('col', 'row'), may hold values from -0.21875 to 0.21875
- w_value: bfloat16 [768, 768], P('col', 'row'), may hold values from -0.21875 to 0.21875
- w_output: bfloat16 [768, 768], P('row', 'col'), may hold values from -1.75 to 1.75
- w_inner: bfloat16 [768, 3072], P('col', 'row'), may hold values from -0.21875 to 0.21875
- w_outer: bfloat16 [3072, 768], P('row', 'col'), may hold values from -0.109375 to 0.109375
- b_query: bfloat16 [768], P(('row', 'col')), may hold values from -1.796875 to 1.796875
- b_value: bfloat16 [768], P(('row', 'col')), may hold values from -0.29882812 to 0.29882812
- b_output: bfloat16 [768], P(('row', 'col')), may hold values from -1.796875 to 1.796875
- b_inner: bfloat16 [3072], P(('row', 'col')), may hold values from -1.796875 to 1.796875
- b_outer: bfloat16 [768], P(('row', 'col')), may hold values from -1.796875 to 1.796875
- gain_one: bfloat16 [768], P(('row', 'col')), may hold values from 0.099609375 to 1.8984375
- shift_one: bfloat16 [768], P(('row', 'col')), may hold values from -1.796875 to 1.796875
- gain_two: bfloat16 [768], P(('row', 'col')), may hold values from 0.099609375 to 1.8984375
- shift_two: bfloat16 [768], P(('row', 'col')), may hold values from -1.796875 to 1.796875
Outputs:
- layer_out: bfloat16 [8192, 768], P('col', 'row')
- grad_in: float32 [8192, 768], P('col', 'row')
- grad_w_query: float32 [768, 768], P('col', 'row')
- grad_w_key: float32 [768, 768], P('col', 'row')
- grad_w_value: float32 [768, 768], P('col', 'row')
- grad_w_output: float32 [768, 768], P('row', 'col')
- grad_w_inner: float32 [768, 3072], P('col', 'row')
- grad_w_outer: float32 [3072, 768], P('row', 'col')
- grad_b_query: float32 [768], P(('row', 'col'))
- grad_b_value: float32 [768], P(('row', 'col'))
- grad_b_output: float32 [768], P(('row', 'col'))
- grad_b_inner: float32 [3072], P(('row', 'col'))
- grad_b_outer: float32 [768], P(('row', 'col'))
- grad_gain_one: float32 [768], P(('row', 'col'))
- grad_shift_one: float32 [768], P(('row', 'col'))
- grad_gain_two: float32 [768], P(('row', 'col'))
- grad_shift_two: float32 [768], P(('row', 'col'))
Inputs may be any that keep to these rules, and one draw needn't show every extreme that they name: Sequence s occupies token slots s * 4096 to s * 4096 + lengths[s] - 1; the last sequence has exactly 4096 tokens in every draw.
All inputs are finite; a program needn't handle non-finite values.
Results may differ from a plain program's by a relative error of at most 0.014.
The roundings to bfloat16 on the way count: a program that leaves them out, or rounds other values in their place, can miss the bound.
Values may be sent and summed in bfloat16 or wider, within the bound.
A program may use at most 128 MiB of HBM per device.

v0:
```python
import jax
import jax.numpy as jnp
from jax import lax
from jax.sharding import PartitionSpec as P

D = 768
HEAD_DIM = 64
SPAN = 8


EPSILON = 1e-12
MASKED = -1e30


def as_sent(value):
    return jax.tree.map(lambda a: a.astype(jnp.bfloat16) if a.dtype == jnp.float32 else a, value)


def partner_2(value, axis, bit):
    mask = 2**bit
    pairs = [(source, source ^ mask) for source in range(lax.axis_size(axis))]
    return lax.ppermute(value, axis, pairs)


def widen(operand):
    return lax.all_gather(operand, "row", axis=1, tiled=True)


def narrow(operand):
    return lax.psum_scatter(operand, "row", scatter_dimension=1, tiled=True)


def row_totals(first, second):
    return lax.psum((first, second), "row")


def kv_partner(pair, bit):
    return jax.tree.map(
        lambda part, own: part.astype(own.dtype), partner_2(as_sent(pair), "col", bit), pair
    )


def query_partner(pair, bit):
    return jax.tree.map(
        lambda part, own: part.astype(own.dtype), partner_2(as_sent(pair), "col", bit), pair
    )


def stats_partner(pair, bit):
    return partner_2(pair, "col", bit)


def group_collect(pair, partner):
    position = lax.axis_index("col")
    current = (pair[0][None], pair[1][None])
    for bit in range(SPAN.bit_length() - 1):
        other = partner(current, bit)
        upper = position // (1 << bit) % 2 == 1
        current = tuple(
            (
                jnp.where(
                    upper,
                    jnp.concatenate([theirs, mine], axis=0),
                    jnp.concatenate([mine, theirs], axis=0),
                )
                for mine, theirs in zip(current, other)
            )
        )
    return current


def gelu(argument):
    return 0.5 * argument * (1.0 + jax.scipy.special.erf(argument * 0.7071067811865476))


def norm_forward(resid, gain, shift):
    totals, squares = row_totals(jnp.sum(resid, axis=1), jnp.sum(resid * resid, axis=1))
    center = totals / D
    spread = squares / D - center * center
    scale = lax.rsqrt(spread + EPSILON)
    normal = (resid - center[:, None]) * scale[:, None]
    return (normal * gain + shift, normal, scale)


def norm_backward(incoming, normal, scale, gain):
    scaled = incoming * gain
    first, second = row_totals(jnp.sum(scaled, axis=1), jnp.sum(scaled * normal, axis=1))
    result = scale[:, None] * (scaled - first[:, None] / D - normal * (second[:, None] / D))
    return (result, jnp.sum(incoming * normal, axis=0), jnp.sum(incoming, axis=0))


def split_heads(operand):
    return operand.reshape(operand.shape[0], operand.shape[1] // HEAD_DIM, HEAD_DIM)


def split_stack(operand):
    return operand.reshape(
        operand.shape[0], operand.shape[1], operand.shape[2] // HEAD_DIM, HEAD_DIM
    )


def masked_scores(query_heads, key_heads, allowed):
    scores = (
        jnp.einsum("qhd,khd->hqk", query_heads, key_heads, preferred_element_type=jnp.float32)
        * 0.125
    )
    return jnp.where(allowed[None, None, :], scores, MASKED)


def probabilities(query_heads, key_heads, allowed, log_total):
    scores = masked_scores(query_heads, key_heads, allowed)
    return jnp.where(allowed[None, None, :], jnp.exp(scores - log_total[:, :, None]), 0.0)


def log_totals(query_heads, key_stack, allow_stack):
    head_count, row_count = (query_heads.shape[1], query_heads.shape[0])

    def log_step(state_pair, element):
        highest, denominator = state_pair
        key_heads, allowed = element
        scores = masked_scores(query_heads, key_heads, allowed)
        new_high = jnp.maximum(highest, jnp.max(scores, axis=2))
        weights = jnp.where(allowed[None, None, :], jnp.exp(scores - new_high[:, :, None]), 0.0)
        denominator = denominator * jnp.exp(highest - new_high) + jnp.sum(weights, axis=2)
        return ((new_high, denominator), None)

    start = (
        jnp.full((head_count, row_count), MASKED, jnp.float32),
        jnp.zeros((head_count, row_count), jnp.float32),
    )
    (highest, denominator), _ = lax.scan(log_step, start, (key_stack, allow_stack))
    return highest + jnp.log(denominator)


def attend(query_heads, key_stack, value_stack, allow_stack, log_total):

    def attend_step(running, element):
        key_heads, value_heads, allowed = element
        probs = probabilities(query_heads, key_heads, allowed, log_total)
        return (
            running
            + jnp.einsum(
                "hqk,khd->qhd",
                probs.astype(jnp.bfloat16),
                value_heads,
                preferred_element_type=jnp.float32,
            ),
            None,
        )

    start = jnp.zeros(query_heads.shape, jnp.float32)
    running, _ = lax.scan(attend_step, start, (key_stack, value_stack, allow_stack))
    return running


def softmax_delta(query_heads, dctx_heads, log_total, key_stack, value_stack, allow_stack):

    def softmax_step(running, element):
        key_heads, value_heads, allowed = element
        probs = probabilities(query_heads, key_heads, allowed, log_total)
        d_probs = jnp.einsum(
            "qhd,khd->hqk", dctx_heads, value_heads, preferred_element_type=jnp.float32
        )
        return (running + jnp.sum(probs * d_probs, axis=2), None)

    start = jnp.zeros(log_total.shape, jnp.float32)
    running, _ = lax.scan(softmax_step, start, (key_stack, value_stack, allow_stack))
    return running


def query_grads(query_heads, dctx_heads, log_total, row_delta, key_stack, value_stack, allow_stack):

    def query_step(running, element):
        key_heads, value_heads, allowed = element
        probs = probabilities(query_heads, key_heads, allowed, log_total)
        d_probs = jnp.einsum(
            "qhd,khd->hqk", dctx_heads, value_heads, preferred_element_type=jnp.float32
        )
        d_scores = (probs * (d_probs - row_delta[:, :, None])).astype(jnp.bfloat16)
        running = running + jnp.einsum(
            "hqk,khd->qhd", d_scores, key_heads, preferred_element_type=jnp.float32
        )
        return (running, None)

    start = jnp.zeros(query_heads.shape, jnp.float32)
    return lax.scan(query_step, start, (key_stack, value_stack, allow_stack))


def key_grads(own_keys, own_values, query_stack, dctx_stack, log_stack, delta_stack, own_allowed):

    def key_step(state_pair, element):
        key_running, value_running = state_pair
        query_heads, dctx_heads, log_total, row_delta = element
        probs = probabilities(query_heads, own_keys, own_allowed, log_total)
        d_probs = jnp.einsum(
            "qhd,khd->hqk", dctx_heads, own_values, preferred_element_type=jnp.float32
        )
        d_scores = (probs * (d_probs - row_delta[:, :, None])).astype(jnp.bfloat16)
        key_running = key_running + jnp.einsum(
            "hqk,qhd->khd", d_scores, query_heads, preferred_element_type=jnp.float32
        )
        value_running = value_running + jnp.einsum(
            "hqk,qhd->khd",
            probs.astype(jnp.bfloat16),
            dctx_heads,
            preferred_element_type=jnp.float32,
        )
        return ((key_running, value_running), None)

    zeros_like = jnp.zeros(own_keys.shape, jnp.float32)
    (key_running, value_running), _ = lax.scan(
        key_step, (zeros_like, zeros_like), (query_stack, dctx_stack, log_stack, delta_stack)
    )
    return (key_running * 0.125, value_running)


def per_device(
    hidden_in,
    cotangent,
    lengths,
    w_query,
    w_key,
    w_value,
    w_output,
    w_inner,
    w_outer,
    b_query,
    b_value,
    b_output,
    b_inner,
    b_outer,
    gain_one,
    shift_one,
    gain_two,
    shift_two,
):
    row_count = hidden_in.shape[0]
    position = lax.axis_index("col")
    slot_ids = jnp.arange(lengths.shape[0], dtype=jnp.int32)
    slot_length = jnp.sum(jnp.where(slot_ids == position // SPAN, lengths, 0))
    local_rows = jnp.arange(row_count, dtype=jnp.int32)
    block_ids = jnp.arange(SPAN, dtype=jnp.int32)
    allow_stack = block_ids[:, None] * row_count + local_rows[None, :] < slot_length
    own_keep = position % SPAN * row_count + local_rows < slot_length
    keep_mask = own_keep.astype(jnp.float32)[:, None]
    gathered = (
        lax.all_gather(w_query, "col", axis=0, tiled=True),
        lax.all_gather(w_key, "col", axis=0, tiled=True),
        lax.all_gather(w_value, "col", axis=0, tiled=True),
        lax.all_gather(w_output, "col", axis=1, tiled=True),
        lax.all_gather(w_inner, "col", axis=0, tiled=True),
        lax.all_gather(w_outer, "col", axis=1, tiled=True),
        lax.all_gather(b_query, "col", axis=0, tiled=True),
        lax.all_gather(b_value, "col", axis=0, tiled=True),
        lax.all_gather(b_output, "col", axis=0, tiled=True),
        lax.all_gather(b_inner, "col", axis=0, tiled=True),
        lax.all_gather(b_outer, "col", axis=0, tiled=True),
        lax.all_gather(gain_one, "col", axis=0, tiled=True),
        lax.all_gather(shift_one, "col", axis=0, tiled=True),
        lax.all_gather(gain_two, "col", axis=0, tiled=True),
        lax.all_gather(shift_two, "col", axis=0, tiled=True),
    )
    full_query, full_key, full_value, full_output, full_inner, full_outer = (
        gathered[0],
        gathered[1],
        gathered[2],
        gathered[3],
        gathered[4],
        gathered[5],
    )
    (
        bias_query,
        bias_value,
        bias_output,
        bias_inner,
        bias_outer,
        gain_first,
        shift_first,
        gain_second,
        shift_second,
    ) = [vector.astype(jnp.float32) for vector in gathered[6:]]
    wide_in = widen(hidden_in)
    queries = (
        jnp.dot(wide_in, full_query, preferred_element_type=jnp.float32) + bias_query
    ).astype(jnp.bfloat16)
    keys = jnp.dot(wide_in, full_key, preferred_element_type=jnp.float32).astype(jnp.bfloat16)
    values = (jnp.dot(wide_in, full_value, preferred_element_type=jnp.float32) + bias_value).astype(
        jnp.bfloat16
    )
    key_rows, value_rows = group_collect((keys, values), kv_partner)
    key_stack = split_stack(key_rows)
    value_stack = split_stack(value_rows)
    query_heads = split_heads(queries)
    log_total = log_totals(query_heads, key_stack, allow_stack)
    context = attend(query_heads, key_stack, value_stack, allow_stack, log_total)
    context = (context.reshape(row_count, -1) * keep_mask).astype(jnp.bfloat16)
    attn = narrow(jnp.dot(context, full_output, preferred_element_type=jnp.float32)) + bias_output
    normed, normal_one, scale_one = norm_forward(
        hidden_in.astype(jnp.float32) + attn, gain_first, shift_first
    )
    wide_normed = widen(normed.astype(jnp.bfloat16))
    inner = jnp.dot(wide_normed, full_inner, preferred_element_type=jnp.float32) + bias_inner
    activated = gelu(inner).astype(jnp.bfloat16)
    outer = narrow(jnp.dot(activated, full_outer, preferred_element_type=jnp.float32)) + bias_outer
    result, normal_two, scale_two = norm_forward(normed + outer, gain_second, shift_second)
    seed = cotangent.astype(jnp.float32) * keep_mask
    d_res_two, grad_gain_two, grad_shift_two = norm_backward(
        seed, normal_two, scale_two, gain_second
    )
    d_outer = d_res_two.astype(jnp.bfloat16)
    wide_d_outer = widen(d_outer)
    grad_w_outer = jnp.einsum(
        "tf,td->fd", activated, wide_d_outer, preferred_element_type=jnp.float32
    )
    d_activated = jnp.einsum(
        "td,fd->tf", wide_d_outer, full_outer, preferred_element_type=jnp.float32
    )
    _, gelu_pull = jax.vjp(gelu, inner)
    d_inner = gelu_pull(d_activated)[0].astype(jnp.bfloat16)
    grad_w_inner = jnp.einsum("td,tf->df", wide_normed, d_inner, preferred_element_type=jnp.float32)
    d_normed = d_res_two + narrow(
        jnp.einsum("tf,df->td", d_inner, full_inner, preferred_element_type=jnp.float32)
    )
    d_res_one, grad_gain_one, grad_shift_one = norm_backward(
        d_normed, normal_one, scale_one, gain_first
    )
    d_attn = d_res_one.astype(jnp.bfloat16)
    wide_d_attn = widen(d_attn)
    grad_w_output = jnp.einsum(
        "te,td->ed", context, wide_d_attn, preferred_element_type=jnp.float32
    )
    d_context = (
        jnp.einsum("td,ed->te", wide_d_attn, full_output, preferred_element_type=jnp.float32)
        * keep_mask
    ).astype(jnp.bfloat16)
    dctx_heads = split_heads(d_context)
    row_delta = softmax_delta(
        query_heads, dctx_heads, log_total, key_stack, value_stack, allow_stack
    )
    query_running, _ = query_grads(
        query_heads, dctx_heads, log_total, row_delta, key_stack, value_stack, allow_stack
    )
    query_rows, dctx_rows = group_collect((queries, d_context), query_partner)
    log_stack, delta_stack = group_collect((log_total, row_delta), stats_partner)
    key_total, value_total = key_grads(
        split_heads(keys),
        split_heads(values),
        split_stack(query_rows),
        split_stack(dctx_rows),
        log_stack,
        delta_stack,
        own_keep,
    )
    d_query = (query_running * 0.125).reshape(row_count, -1).astype(jnp.bfloat16)
    d_key = key_total.reshape(row_count, -1).astype(jnp.bfloat16)
    d_value = value_total.reshape(row_count, -1).astype(jnp.bfloat16)
    grad_w_query = jnp.einsum("td,te->de", wide_in, d_query, preferred_element_type=jnp.float32)
    grad_w_key = jnp.einsum("td,te->de", wide_in, d_key, preferred_element_type=jnp.float32)
    grad_w_value = jnp.einsum("td,te->de", wide_in, d_value, preferred_element_type=jnp.float32)
    input_terms = jnp.einsum("te,de->td", d_query, full_query, preferred_element_type=jnp.float32)
    input_terms = input_terms + jnp.einsum(
        "te,de->td", d_key, full_key, preferred_element_type=jnp.float32
    )
    input_terms = input_terms + jnp.einsum(
        "te,de->td", d_value, full_value, preferred_element_type=jnp.float32
    )
    grad_in = d_res_one + narrow(input_terms)
    summed = (
        lax.psum_scatter(grad_w_query, "col", scatter_dimension=0, tiled=True),
        lax.psum_scatter(grad_w_key, "col", scatter_dimension=0, tiled=True),
        lax.psum_scatter(grad_w_value, "col", scatter_dimension=0, tiled=True),
        lax.psum_scatter(grad_w_output, "col", scatter_dimension=1, tiled=True),
        lax.psum_scatter(grad_w_inner, "col", scatter_dimension=0, tiled=True),
        lax.psum_scatter(grad_w_outer, "col", scatter_dimension=1, tiled=True),
        lax.psum_scatter(
            jnp.sum(d_query.astype(jnp.float32), axis=0), "col", scatter_dimension=0, tiled=True
        ),
        lax.psum_scatter(
            jnp.sum(d_value.astype(jnp.float32), axis=0), "col", scatter_dimension=0, tiled=True
        ),
        lax.psum_scatter(
            jnp.sum(d_attn.astype(jnp.float32), axis=0), "col", scatter_dimension=0, tiled=True
        ),
        lax.psum_scatter(
            jnp.sum(d_inner.astype(jnp.float32), axis=0), "col", scatter_dimension=0, tiled=True
        ),
        lax.psum_scatter(
            jnp.sum(d_outer.astype(jnp.float32), axis=0), "col", scatter_dimension=0, tiled=True
        ),
        lax.psum_scatter(grad_gain_one, "col", scatter_dimension=0, tiled=True),
        lax.psum_scatter(grad_shift_one, "col", scatter_dimension=0, tiled=True),
        lax.psum_scatter(grad_gain_two, "col", scatter_dimension=0, tiled=True),
        lax.psum_scatter(grad_shift_two, "col", scatter_dimension=0, tiled=True),
    )
    return (
        result.astype(jnp.bfloat16),
        grad_in,
        summed[0],
        summed[1],
        summed[2],
        summed[3],
        summed[4],
        summed[5],
        summed[6],
        summed[7],
        summed[8],
        summed[9],
        summed[10],
        summed[11],
        summed[12],
        summed[13],
        summed[14],
    )


def solution(mesh):
    placed = (
        P("col", "row"),
        P("col", "row"),
        P(),
        P("col", "row"),
        P("col", "row"),
        P("col", "row"),
        P("row", "col"),
        P("col", "row"),
        P("row", "col"),
        P(("row", "col")),
        P(("row", "col")),
        P(("row", "col")),
        P(("row", "col")),
        P(("row", "col")),
        P(("row", "col")),
        P(("row", "col")),
        P(("row", "col")),
        P(("row", "col")),
    )
    return jax.shard_map(
        per_device,
        mesh=mesh,
        in_specs=placed,
        out_specs=(
            P("col", "row"),
            P("col", "row"),
            P("col", "row"),
            P("col", "row"),
            P("col", "row"),
            P("row", "col"),
            P("col", "row"),
            P("row", "col"),
            P(("row", "col")),
            P(("row", "col")),
            P(("row", "col")),
            P(("row", "col")),
            P(("row", "col")),
            P(("row", "col")),
            P(("row", "col")),
            P(("row", "col")),
            P(("row", "col")),
        ),
        check_vma=False,
    )
```

profile of v0, /device:TPU:0, one launch (start us, length us, event | category | flops | bytes accessed | tf_op | source)
XLA Modules:
  0.0 1324.5 jit_solution(16205717023281383789)
XLA Ops:
  8.2 13.1 all_gather.57
  21.3 23.9 %all_gather.60 = bf16[768,384]{1,0:T(8,128)(2,1)S(1)} all-gather(bf16[48,384]{1,0:T(8,128)(2,1)} %param.32), channel_id=1, replica_groups=mesh['row'=2,'col'=16] {'col'}, dimensions={0}, use_global_device_ids=true | all-gather | bytes 626688 | tf_op jit(solution)/shard_map/all_gather | solution.py:248
  50.3 57.7 %all-reduce.23 = (bf16[384]{0:T(512)(128)(2,1)S(1)}, bf16[384]{0:T(512)(128)(2,1)S(1)}, bf16[384]{0:T(512)(128)(2,1)S(1)}, bf16[384]{0:T(512)(128)(2,1)S(1)}, bf...) all-reduce(bf16[384]{0:T(512)(128)(2,1)S(1)} %dynamic-update-slice,, ...), channel_id=1, replica_groups=mesh['row'=2,'col'=16] {'col'}, use_global_device_ids=true, to_apply=%add | all-reduce | flops 4608 | bytes 18432
  108.0 18.9 %all_gather.58 = bf16[768,384]{1,0:T(8,128)(2,1)S(1)} all-gather(bf16[48,384]{1,0:T(8,128)(2,1)S(1)} %copy-done.30), channel_id=1, replica_groups=mesh['row'=2,'col'=16] {'col'}, dimensions={0}, use_global_device_ids=true | all-gather | bytes 626688 | tf_op jit(solution)/shard_map/all_gather | solution.py:249
  129.7 32.9 %all_gather.61 = bf16[768,384]{1,0:T(8,128)(2,1)S(1)} all-gather(bf16[48,384]{1,0:T(8,128)(2,1)S(1)} %copy-done.31), channel_id=1, replica_groups=mesh['row'=2,'col'=16] {'col'}, dimensions={0}, use_global_device_ids=true | all-gather | bytes 626688 | tf_op jit(solution)/shard_map/all_gather | solution.py:247
  171.0 50.0 %all_gather.63 = bf16[384,768]{0,1:T(8,128)(2,1)} all-gather(bf16[384,48]{0,1:T(8,128)(2,1)S(1)} %copy-done.32), channel_id=1, replica_groups=mesh['row'=2,'col'=16] {'col'}, dimensions={1}, use_global_device_ids=true | all-gather | bytes 626688 | tf_op jit(solution)/shard_map/all_gather | solution.py:250
  233.0 71.5 %while.59 = (s32[]{:T(128)}, f32[6,512]{1,0:T(8,128)S(1)}, f32[6,512]{1,0:T(8,128)S(1)}, pred[8,512]{1,0:T(8,128)(4,1)S(1)}, bf16[8,512,6,64]{1,3,2,0:T(8,128)(2...) while((s32[]{:T(128)}, f32[6,512]{1,0:T(8,128)S(1)}, f32[6,512]{1,0:T(8,128)S(1)}, ...), condition=%wide.region_4.5_spmd.clone, body=%wide.region_1.4_spmd.clone.sunk | while | flops 213924864 | bytes 13531248 | solution.py:131
  233.0 5.1 bitcast_reduce_fusion.2
  242.0 5.1 bitcast_reduce_fusion.2
  250.9 5.1 bitcast_reduce_fusion.2
  259.9 5.1 bitcast_reduce_fusion.2
  268.8 5.1 bitcast_reduce_fusion.2
  277.8 5.1 bitcast_reduce_fusion.2
  286.7 5.1 bitcast_reduce_fusion.2
  295.6 5.1 bitcast_reduce_fusion.2
  309.0 36.2 %while.60 = (s32[]{:T(128)}, f32[512,6,64]{0,2,1:T(8,128)}, bf16[8,512,6,64]{1,3,2,0:T(8,128)(2,1)}, pred[8,512]{1,0:T(8,128)(4,1)S(1)}, bf16[8,512,6,64]{1,3,2,...) while((s32[]{:T(128)}, f32[512,6,64]{0,2,1:T(8,128)}, ...), condition=%wide.region_6.7_spmd.clone, body=%wide.region_5.6_spmd.clone.sunk | while | flops 410910720 | bytes 2767986 | solution.py:152
  350.4 23.5 %reduce-scatter.17.cloned.1.call-done = f32[512,384]{0,1:T(8,128)} async-done(((f32[512,768]{0,1:T(8,128)}), f32[512,384]{0,1:T(8,128)}) %reduce-scatter.17.cloned.1.call-update) | async-done | bytes 786448 | tf_op jit(solution)/shard_map/reduce_scatter | solution.py:30
  375.3 4.9 all-reduce.22
  380.4 10.6 all_gather.67
  392.8 4.9 multiply_convert_fusion.12
  397.7 38.2 %all-gather.5.cloned.1.call-done = bf16[1536,768]{0,1:T(8,128)(2,1)} async-done(((bf16[1536,48]{0,1:T(8,128)(2,1)}), bf16[1536,768]{0,1:T(8,128)(2,1)}) %all-gather.5.cloned.1.call-update) | async-done | bytes 2359312 | tf_op jit(solution)/shard_map/all_gather | solution.py:252
  441.7 23.7 %reduce-scatter.19.cloned.1.call-done = f32[512,384]{0,1:T(8,128)} async-done(((f32[512,768]{0,1:T(8,128)}), f32[512,384]{0,1:T(8,128)}) %reduce-scatter.19.cloned.1.call-update) | async-done | bytes 786448 | tf_op jit(solution)/shard_map/reduce_scatter | solution.py:30
  466.8 4.9 all-reduce.21
  473.8 4.9 all-reduce.20
  480.7 9.4 all_gather.74
  490.1 5.8 convert_reduce_fusion
  509.5 13.7 %collective-permute-done.7 = bf16[2,512,384]{1,2,0:T(8,128)(2,1)} collective-permute-done((bf16[2,512,384]{1,2,0:T(8,128)(2,1)}, bf16[2,512,384]{1,2,0:T(8,128)(2,1)}, u32[]{:S(2)}, u32[]{:S(2)}) %collective-permute-start.7) | collective-permute-done | bytes 786464 | tf_op jit(solution)/shard_map/ppermute | solution.py:22
  536.4 4.9 all-reduce.19
  543.6 9.4 all_gather.75
  553.8 9.3 collective-permute-done.8
  570.5 53.6 %while.61 = (s32[]{:T(128)}, f32[6,512]{1,0:T(8,128)}, pred[8,512]{1,0:T(8,128)(4,1)S(1)}, bf16[8,512,6,64]{1,3,2,0:T(8,128)(2,1)}, bf16[512,6,64]{0,2,1:T(8,128...) while((s32[]{:T(128)}, f32[6,512]{1,0:T(8,128)}, ...), condition=%wide.region_28.29_spmd.clone, body=%wide.region_26.28_spmd.clone.sunk | while | flops 412093440 | bytes 14218883 | solution.py:167
  630.6 95.6 %while.62 = (s32[]{:T(128)}, f32[512,6,64]{0,2,1:T(8,128)}, bf16[8,512,6,64]{1,3,2,0:T(8,128)(2,1)}, pred[8,512]{1,0:T(8,128)(4,1)S(1)}, bf16[512,6,64]{2,1,0:T(...) while((s32[]{:T(128)}, f32[512,6,64]{0,2,1:T(8,128)}, ...), condition=%wide.region_30.31_spmd.clone, body=%wide.region_29.30_spmd.clone.sunk | while | flops 615383040 | bytes 16809092 | solution.py:186
  635.3 7.1 fusion.214
  647.1 7.3 fusion.214
  659.0 7.3 fusion.214
  671.0 7.3 fusion.214
  683.0 7.3 fusion.214
  695.0 7.3 fusion.214
  706.9 7.3 fusion.214
  718.9 7.3 fusion.214
  740.5 141.1 %while.63 = (s32[]{:T(128)}, f32[512,6,64]{0,2,1:T(8,128)S(1)}, f32[512,6,64]{0,2,1:T(8,128)}, bf16[8,512,6,64]{1,3,2,0:T(8,128)(2,1)}, bf16[512,6,64]{0,2,1:T(8...) while((s32[]{:T(128)}, f32[512,6,64]{0,2,1:T(8,128)S(1)}, ...), condition=%wide.region_32.33_spmd.clone, body=%wide.region_31.32_spmd.clone.sunk | while | flops 824968192 | bytes 25124000 | solution.py:211
  746.7 6.2 fusion.223
  752.9 5.3 fusion.224
  764.2 6.2 fusion.223
  770.4 5.4 fusion.224
  781.8 6.2 fusion.223
  788.0 5.4 fusion.224
  799.5 6.2 fusion.223
  805.6 5.4 fusion.224
  817.1 6.2 fusion.223
  823.3 5.4 fusion.224
  834.7 6.2 fusion.223
  840.9 5.4 fusion.224
  852.4 6.2 fusion.223
  858.5 5.4 fusion.224
  870.0 6.2 fusion.223
  876.2 5.4 fusion.224
  892.7 4.9 fusion.122
  914.4 58.7 %all-reduce.18 = (f32[384]{0:T(512)S(1)}, f32[384]{0:T(512)S(1)}, f32[384]{0:T(512)S(1)}, f32[1536]{0:T(1024)S(1)}, f32[384]{0:T(512)S(1)}, /*index=5*/f32[384]{...) all-reduce(f32[384]{0:T(512)S(1)} %reduce_sum.194, ...), channel_id=12, replica_groups=mesh['row'=2,'col'=16] {'col'}, use_global_device_ids=true, to_apply=%region_41.42.clone | all-reduce | flops 4608 | bytes 36864
  980.9 54.9 %reduce-scatter.25.cloned.1.call-done = f32[384,48]{0,1:T(8,128)} async-done(((f32[384,768]{0,1:T(8,128)}), f32[384,48]{0,1:T(8,128)}) %reduce-scatter.25.cloned.1.call-update) | async-done | bytes 73744 | tf_op jit(solution)/shard_map/reduce_scatter | solution.py:372
  1035.8 79.1 %reduce-scatter.27.cloned.1.call-done = f32[48,1536]{1,0:T(8,128)} async-done(((f32[768,1536]{1,0:T(8,128)}), f32[48,1536]{1,0:T(8,128)}) %reduce-scatter.27.cloned.1.call-update) | async-done | bytes 294928 | tf_op jit(solution)/shard_map/reduce_scatter | solution.py:373
  1114.9 79.2 %reduce-scatter.29.cloned.1.call-done = f32[1536,48]{0,1:T(8,128)} async-done(((f32[1536,768]{0,1:T(8,128)}), f32[1536,48]{0,1:T(8,128)}) %reduce-scatter.29.cloned.1.call-update) | async-done | bytes 294928 | tf_op jit(solution)/shard_map/reduce_scatter | solution.py:374
  1194.1 61.6 %reduce-scatter.33.cloned.1.call-done = f32[48,384]{1,0:T(8,128)} async-done(((f32[768,384]{1,0:T(8,128)}), f32[48,384]{1,0:T(8,128)}) %reduce-scatter.33.cloned.1.call-update) | async-done | bytes 73744
  1255.7 61.2 %reduce-scatter.35.cloned.1.call-done = f32[48,384]{1,0:T(8,128)} async-done(((f32[768,384]{1,0:T(8,128)}), f32[48,384]{1,0:T(8,128)}) %reduce-scatter.35.cloned.1.call-update) | async-done | bytes 73744
  (403 shorter events, 348.9 us)
Async XLA Ops:
  8.0 38.1 %copy-start.36 = (u32[32]{0:T(128)S(1)}, u32[32]{0:T(128)}, u32[]{:S(2)}) copy-start(u32[32]{0:T(128)} %constant.215) | copy-start | bytes 388
  8.0 40.0 %copy-start.37 = (bf16[24]{0:T(256)(128)(2,1)S(1)}, bf16[24]{0:T(256)(128)(2,1)}, u32[]{:S(2)}) copy-start(bf16[24]{0:T(256)(128)(2,1)} %param.38) | copy-start | bytes 148
  8.0 40.3 %copy-start.38 = (bf16[24]{0:T(256)(128)(2,1)S(1)}, bf16[24]{0:T(256)(128)(2,1)}, u32[]{:S(2)}) copy-start(bf16[24]{0:T(256)(128)(2,1)} %param.37) | copy-start | bytes 148
  8.1 40.5 %copy-start.39 = (bf16[24]{0:T(256)(128)(2,1)S(1)}, bf16[24]{0:T(256)(128)(2,1)}, u32[]{:S(2)}) copy-start(bf16[24]{0:T(256)(128)(2,1)} %param.39) | copy-start | bytes 148
  8.1 40.8 %copy-start.40 = (bf16[24]{0:T(256)(128)(2,1)S(1)}, bf16[24]{0:T(256)(128)(2,1)}, u32[]{:S(2)}) copy-start(bf16[24]{0:T(256)(128)(2,1)} %param.43) | copy-start | bytes 148
  8.1 41.0 %copy-start.41 = (bf16[24]{0:T(256)(128)(2,1)S(1)}, bf16[24]{0:T(256)(128)(2,1)}, u32[]{:S(2)}) copy-start(bf16[24]{0:T(256)(128)(2,1)} %param.42) | copy-start | bytes 148
  8.1 41.2 %copy-start.42 = (bf16[24]{0:T(256)(128)(2,1)S(1)}, bf16[24]{0:T(256)(128)(2,1)}, u32[]{:S(2)}) copy-start(bf16[24]{0:T(256)(128)(2,1)} %param.41) | copy-start | bytes 148
  8.1 41.5 %copy-start.43 = (bf16[24]{0:T(256)(128)(2,1)S(1)}, bf16[24]{0:T(256)(128)(2,1)}, u32[]{:S(2)}) copy-start(bf16[24]{0:T(256)(128)(2,1)} %param.45) | copy-start | bytes 148
  8.1 41.7 %copy-start.44 = (bf16[24]{0:T(256)(128)(2,1)S(1)}, bf16[24]{0:T(256)(128)(2,1)}, u32[]{:S(2)}) copy-start(bf16[24]{0:T(256)(128)(2,1)} %param.44) | copy-start | bytes 148
  8.1 41.9 %copy-start.45 = (bf16[96]{0:T(256)(128)(2,1)S(1)}, bf16[96]{0:T(256)(128)(2,1)}, u32[]{:S(2)}) copy-start(bf16[96]{0:T(256)(128)(2,1)} %param.40) | copy-start | bytes 580
  8.1 99.9 %copy-start.30 = (bf16[48,384]{1,0:T(8,128)(2,1)S(1)}, bf16[48,384]{1,0:T(8,128)(2,1)}, u32[]{:S(2)}) copy-start(bf16[48,384]{1,0:T(8,128)(2,1)} %param.33) | copy-start | bytes 110596
  8.1 365.8 %reduce-scatter.17.cloned.1.call-start = ((), (), s32[]{:S(2)}) async-start(), calls=%async_computation.10 | async-start | bytes 2359296 | tf_op jit(solution)/shard_map/reduce_scatter | solution.py:30
  21.3 141.3 %copy-start = (bf16[512,768]{1,0:T(8,128)(2,1)}, bf16[512,768]{1,0:T(8,128)(2,1)S(1)}, u32[]{:S(2)}) copy-start(bf16[512,768]{1,0:T(8,128)(2,1)S(1)} %all_gather.57) | copy-start | bytes 2359300
  45.2 81.7 %copy-start.15 = (bf16[768,384]{1,0:T(8,128)(2,1)}, bf16[768,384]{1,0:T(8,128)(2,1)S(1)}, u32[]{:S(2)}) copy-start(bf16[768,384]{1,0:T(8,128)(2,1)S(1)} %all_gather.60) | copy-start | bytes 1769476
  45.2 84.5 %copy-start.31 = (bf16[48,384]{1,0:T(8,128)(2,1)S(1)}, bf16[48,384]{1,0:T(8,128)(2,1)}, u32[]{:S(2)}) copy-start(bf16[48,384]{1,0:T(8,128)(2,1)} %param.31) | copy-start | bytes 110596
  45.7 81.1 %collective-permute-start.3 = (bf16[1,512,384]{1,2,0:T(8,128)(2,1)S(1)}, bf16[1,512,384]{1,2,0:T(8,128)(2,1)S(1)}, u32[]{:S(2)}, u32[]{:S(2)}) collective-permute-start(bf16[1,512,384]{1,2,0:T(8,128)(2,1)S(1)} %bitcast.205), channel_id=1, source_target_pairs={{0,1},{1,0},{2,3},{3,2},{4,5},{5,4},{6,7},{7,6},{8,9},{9,8},{10,11... | collective-permute-start | bytes 1179656 | tf_op jit(solution)/shard_map/ppermute | solution.py:22
  126.9 37.1 %copy-start.46 = (s32[2]{0:T(128)S(1)}, s32[2]{0:T(128)}, u32[]{:S(2)}) copy-start(s32[2]{0:T(128)} %param.30) | copy-start | bytes 28
  127.0 37.6 %collective-permute-start.4 = (bf16[2,512,384]{1,2,0:T(8,128)(2,1)S(1)}, bf16[2,512,384]{1,2,0:T(8,128)(2,1)}, u32[]{:S(2)}, u32[]{:S(2)}) collective-permute-start(bf16[2,512,384]{1,2,0:T(8,128)(2,1)S(1)} %maximum_select_fusion.14), channel_id=1, source_target_pairs={{0,2},{1,3},{2,0},{3,1},{4,6},{5,7},{6,4},{7,5},{8,10},{9,11},{10,... | collective-permute-start | bytes 2359304 | tf_op jit(solution)/shard_map/ppermute | solution.py:22
  129.6 91.4 %copy-start.12 = (bf16[512,384]{0,1:T(8,128)(2,1)}, bf16[512,384]{0,1:T(8,128)(2,1)S(1)}, u32[]{:S(2)}) copy-start(bf16[512,384]{0,1:T(8,128)(2,1)S(1)} %fusion.99) | copy-start | bytes 1179652
  129.6 38.5 %collective-permute-start = (bf16[1,512,384]{1,2,0:T(8,128)(2,1)S(1)}, bf16[1,512,384]{1,2,0:T(8,128)(2,1)}, u32[]{:S(2)}, u32[]{:S(2)}) collective-permute-start(bf16[1,512,384]{1,2,0:T(8,128)(2,1)S(1)} %bitcast.215), channel_id=1, source_target_pairs={{0,1},{1,0},{2,3},{3,2},{4,5},{5,4},{6,7},{7,6},{8,9},{9,8},{10,11... | collective-permute-start | bytes 1179656 | tf_op jit(solution)/shard_map/ppermute | solution.py:22
  164.0 7.0 copy-start.32
  167.4 62.1 %collective-permute-start.5 = (bf16[4,512,384]{1,2,0:T(8,128)(2,1)}, bf16[4,512,384]{1,2,0:T(8,128)(2,1)}, u32[]{:S(2)}, u32[]{:S(2)}) collective-permute-start(bf16[4,512,384]{1,2,0:T(8,128)(2,1)} %maximum_select_fusion.6), channel_id=1, source_target_pairs={{0,4},{1,5},{2,6},{3,7},{4,0},{5,1},{6,2},{7,3},{8,12},{9,13},{10,... | collective-permute-start | bytes 4718600 | tf_op jit(solution)/shard_map/ppermute | solution.py:22
  169.3 53.0 %collective-permute-start.1 = (bf16[2,512,384]{1,2,0:T(8,128)(2,1)S(1)}, bf16[2,512,384]{1,2,0:T(8,128)(2,1)}, u32[]{:S(2)}, u32[]{:S(2)}) collective-permute-start(bf16[2,512,384]{1,2,0:T(8,128)(2,1)S(1)} %maximum_select_fusion.12), channel_id=1, source_target_pairs={{0,2},{1,3},{2,0},{3,1},{4,6},{5,7},{6,4},{7,5},{8,10},{9,11},{10,... | collective-permute-start | bytes 2359304 | tf_op jit(solution)/shard_map/ppermute | solution.py:22
  225.1 79.4 %collective-permute-start.2 = (bf16[4,512,384]{1,2,0:T(8,128)(2,1)}, bf16[4,512,384]{1,2,0:T(8,128)(2,1)}, u32[]{:S(2)}, u32[]{:S(2)}) collective-permute-start(bf16[4,512,384]{1,2,0:T(8,128)(2,1)} %maximum_select_fusion.4), channel_id=1, source_target_pairs={{0,4},{1,5},{2,6},{3,7},{4,0},{5,1},{6,2},{7,3},{8,12},{9,13},{10,... | collective-permute-start | bytes 4718600 | tf_op jit(solution)/shard_map/ppermute | solution.py:22
  309.0 38.2 %copy-start.18 = (bf16[384,768]{0,1:T(8,128)(2,1)S(1)}, bf16[384,768]{0,1:T(8,128)(2,1)}, u32[]{:S(2)}) copy-start(bf16[384,768]{0,1:T(8,128)(2,1)} %all_gather.63) | copy-start | bytes 1769476
  345.1 5.0 copy-start.24
  348.9 43.9 %all-gather.3.cloned.1.call-start = ((), (), s32[]{:S(2)}) async-start(), calls=%async_computation.11 | async-start | bytes 2506752 | tf_op jit(solution)/shard_map/all_gather | solution.py:251
  349.5 86.4 %all-gather.5.cloned.1.call-start = ((), (), s32[]{:S(2)}) async-start(), calls=%async_computation.12 | async-start | bytes 2506752 | tf_op jit(solution)/shard_map/all_gather | solution.py:252
  350.1 115.3 %reduce-scatter.19.cloned.1.call-start = ((), (), s32[]{:S(2)}) async-start(), calls=%async_computation.13 | async-start | bytes 2359296 | tf_op jit(solution)/shard_map/reduce_scatter | solution.py:30
  391.1 6.7 copy-start.3
  435.9 4.9 copy-start.29
  440.7 92.2 %reduce-scatter.21.cloned.1.call-start = ((), (), s32[]{:S(2)}) async-start(), calls=%async_computation.14 | async-start | bytes 2359296 | tf_op jit(solution)/shard_map/reduce_scatter | solution.py:30
  478.7 17.3 %copy-start.33 = (f32[512]{0:T(512)}, f32[512]{0:T(512)S(1)}, u32[]{:S(2)}) copy-start(f32[512]{0:T(512)S(1)} %get-tuple-element.612) | copy-start | bytes 6148
  478.7 17.3 %copy-start.34 = (f32[512]{0:T(512)}, f32[512]{0:T(512)S(1)}, u32[]{:S(2)}) copy-start(f32[512]{0:T(512)S(1)} %get-tuple-element.613) | copy-start | bytes 6148
  490.1 5.9 copy-start.13
  490.1 7.0 copy-start.22
  499.8 478.5 %reduce-scatter.23.cloned.1.call-start = ((), (), s32[]{:S(2)}) async-start(), calls=%async_computation.15 | async-start | bytes 2359296 | tf_op jit(solution)/shard_map/reduce_scatter | solution.py:30
  499.8 1.8 collective-permute-start.6
  503.4 19.9 %collective-permute-start.7 = (bf16[2,512,384]{1,2,0:T(8,128)(2,1)}, bf16[2,512,384]{1,2,0:T(8,128)(2,1)}, u32[]{:S(2)}, u32[]{:S(2)}) collective-permute-start(bf16[2,512,384]{1,2,0:T(8,128)(2,1)} %maximum_select_fusion.16), channel_id=1, source_target_pairs={{0,2},{1,3},{2,0},{3,1},{4,6},{5,7},{6,4},{7,5},{8,10},{9,11},{10,... | collective-permute-start | bytes 2359304 | tf_op jit(solution)/shard_map/ppermute | solution.py:22
  509.5 18.5 %collective-permute-start.9 = (f32[1,6,512]{2,1,0:T(8,128)S(1)}, f32[1,6,512]{2,1,0:T(8,128)S(1)}, u32[]{:S(2)}, u32[]{:S(2)}) collective-permute-start(f32[1,6,512]{2,1,0:T(8,128)S(1)} %bitcast.226), channel_id=1, source_target_pairs={{0,1},{1,0},{2,3},{3,2},{4,5},{5,4},{6,7},{7,6},{8,9},{9,8},{10,11... | collective-permute-start | bytes 36872 | tf_op jit(solution)/shard_map/ppermute | solution.py:22
  526.5 36.6 %collective-permute-start.8 = (bf16[4,512,384]{1,2,0:T(8,128)(2,1)}, bf16[4,512,384]{1,2,0:T(8,128)(2,1)}, u32[]{:S(2)}, u32[]{:S(2)}) collective-permute-start(bf16[4,512,384]{1,2,0:T(8,128)(2,1)} %maximum_select_fusion.8), channel_id=1, source_target_pairs={{0,4},{1,5},{2,6},{3,7},{4,0},{5,1},{6,2},{7,3},{8,12},{9,13},{10,... | collective-permute-start | bytes 4718600 | tf_op jit(solution)/shard_map/ppermute | solution.py:22
  528.0 4.3 collective-permute-start.10
  532.3 34.1 %collective-permute-start.11 = (f32[4,6,512]{2,1,0:T(8,128)S(1)}, f32[4,6,512]{2,1,0:T(8,128)}, u32[]{:S(2)}, u32[]{:S(2)}) collective-permute-start(f32[4,6,512]{2,1,0:T(8,128)S(1)} %maximum_select_fusion.22), channel_id=1, source_target_pairs={{0,4},{1,5},{2,6},{3,7},{4,0},{5,1},{6,2},{7,3},{8,12},{9,13},{10,... | collective-permute-start | bytes 147464 | tf_op jit(solution)/shard_map/ppermute | solution.py:22
  541.3 11.6 copy-start.19
  541.3 21.8 %copy-start.7 = (bf16[4,512,6,64]{1,3,2,0:T(8,128)(2,1)S(1)}, bf16[4,512,6,64]{1,3,2,0:T(8,128)(2,1)}, u32[]{:S(2)}) copy-start(bf16[4,512,6,64]{1,3,2,0:T(8,128)(2,1)} %maximum_select_fusion.9) | copy-start | bytes 4718596
  541.3 25.1 %copy-start.35 = (f32[512]{0:T(512)}, f32[512]{0:T(512)S(1)}, u32[]{:S(2)}) copy-start(f32[512]{0:T(512)S(1)} %broadcast_multiply_fusion.1) | copy-start | bytes 6148
  553.8 14.3 %collective-permute-start.12 = (bf16[1,512,384]{1,2,0:T(8,128)(2,1)S(1)}, bf16[1,512,384]{1,2,0:T(8,128)(2,1)S(1)}, u32[]{:S(2)}, u32[]{:S(2)}) collective-permute-start(bf16[1,512,384]{1,2,0:T(8,128)(2,1)S(1)} %bitcast.219), channel_id=1, source_target_pairs={{0,1},{1,0},{2,3},{3,2},{4,5},{5,4},{6,7},{7,6},{8,9},{9,8},{10,11... | collective-permute-start | bytes 1179656 | tf_op jit(solution)/shard_map/ppermute | solution.py:22
  569.0 56.8 %collective-permute-start.13 = (bf16[2,512,384]{1,2,0:T(8,128)(2,1)}, bf16[2,512,384]{1,2,0:T(8,128)(2,1)}, u32[]{:S(2)}, u32[]{:S(2)}) collective-permute-start(bf16[2,512,384]{1,2,0:T(8,128)(2,1)} %maximum_select_fusion.18), channel_id=1, source_target_pairs={{0,2},{1,3},{2,0},{3,1},{4,6},{5,7},{6,4},{7,5},{8,10},{9,11},{10,... | collective-permute-start | bytes 2359304 | tf_op jit(solution)/shard_map/ppermute | solution.py:22
  625.8 100.3 %collective-permute-start.15 = (f32[1,6,512]{2,1,0:T(8,128)}, f32[1,6,512]{2,1,0:T(8,128)S(1)}, u32[]{:S(2)}, u32[]{:S(2)}) collective-permute-start(f32[1,6,512]{2,1,0:T(8,128)} %bitcast.29), channel_id=1, source_target_pairs={{0,1},{1,0},{2,3},{3,2},{4,5},{5,4},{6,7},{7,6},{8,9},{9,8},{10,11... | collective-permute-start | bytes 36872 | tf_op jit(solution)/shard_map/ppermute | solution.py:22
  629.1 107.9 %collective-permute-start.14 = (bf16[4,512,384]{1,2,0:T(8,128)(2,1)}, bf16[4,512,384]{1,2,0:T(8,128)(2,1)}, u32[]{:S(2)}, u32[]{:S(2)}) collective-permute-start(bf16[4,512,384]{1,2,0:T(8,128)(2,1)} %maximum_select_fusion.10), channel_id=1, source_target_pairs={{0,4},{1,5},{2,6},{3,7},{4,0},{5,1},{6,2},{7,3},{8,12},{9,13},{10,... | collective-permute-start | bytes 4718600 | tf_op jit(solution)/shard_map/ppermute | solution.py:22
  727.0 3.9 collective-permute-start.16
  730.9 4.3 collective-permute-start.17
  737.0 3.4 copy-start.26
  740.5 143.4 %copy-start.16 = (bf16[768,384]{1,0:T(8,128)(2,1)S(1)}, bf16[768,384]{1,0:T(8,128)(2,1)}, u32[]{:S(2)}) copy-start(bf16[768,384]{1,0:T(8,128)(2,1)} %copy-done.15) | copy-start | bytes 1769476
  882.5 3.4 copy-start.5
  882.5 3.4 copy-start.21
  887.7 93.2 %reduce-scatter.31.cloned.1.call-start = ((), (), s32[]{:S(2)}) async-start(), calls=%async_computation.19 | async-start | bytes 1253376
  888.2 4.5 copy-start.4
  889.7 146.1 %reduce-scatter.25.cloned.1.call-start = ((), (), s32[]{:S(2)}) async-start(), calls=%async_computation.16 | async-start | bytes 1253376 | tf_op jit(solution)/shard_map/reduce_scatter | solution.py:372
  892.7 222.2 %reduce-scatter.27.cloned.1.call-start = ((), (), s32[]{:S(2)}) async-start(), calls=%async_computation.17 | async-start | bytes 5013504 | tf_op jit(solution)/shard_map/reduce_scatter | solution.py:373
  897.7 296.4 %reduce-scatter.29.cloned.1.call-start = ((), (), s32[]{:S(2)}) async-start(), calls=%async_computation.18 | async-start | bytes 5013504 | tf_op jit(solution)/shard_map/reduce_scatter | solution.py:374
  903.8 351.9 %reduce-scatter.33.cloned.1.call-start = ((), (), s32[]{:S(2)}) async-start(), calls=%async_computation.20 | async-start | bytes 1253376
  906.6 71.7 %copy-start.2 = (f32[512,384]{0,1:T(8,128)S(1)}, f32[512,384]{0,1:T(8,128)}, u32[]{:S(2)}) copy-start(f32[512,384]{0,1:T(8,128)} %get-tuple-element.596) | copy-start | bytes 2359300
  906.7 410.2 %reduce-scatter.35.cloned.1.call-start = ((), (), s32[]{:S(2)}) async-start(), calls=%async_computation.21 | async-start | bytes 1253376
  (13 other events, 16.4 us)
Sparse Core Ops, SparseCore 0:
  349.0 24.8 reduce-scatter.16
  440.8 24.5 reduce-scatter.18
  499.9 26.1 reduce-scatter.20
  887.8 24.3 reduce-scatter.22
  916.2 58.2 reduce-scatter.30
  978.6 57.1 reduce-scatter.24
  1040.2 74.6 reduce-scatter.26
  1119.3 74.7 reduce-scatter.28
  1198.3 57.3 reduce-scatter.32
  1259.7 57.0 reduce-scatter.34
Sparse Core Ops, SparseCore 1:
  351.7 41.0 all-gather.2
  395.0 40.9 all-gather.4
where the time goes:
time: 1330 us; the launch traced here: 1320 us
  waiting for transfers between devices  452 us (34%)
  matrix products  387 us (29%)
  blocking collectives  304 us (23%)
  other arithmetic  111 us (8%)
  local copies, waits for them, and re-layouts  37.8 us (3%)
  between operations  19.2 us (1%)
    dot_general x32, matrix products, masked_scores(): jnp.einsum('qhd,khd->hqk', query_heads, key_heads, preferred_element_type...  132 us
    unnamed x15, waiting for transfers between devices  124 us
    unnamed x2, blocking collectives  116 us
    reduce_scatter x1, waiting for transfers between devices, per_device(): lax.psum_scatter(grad_w_outer, 'col', scatter_dimension=1, tiled=True)  79.2 us
    reduce_scatter x1, waiting for transfers between devices, per_device(): lax.psum_scatter(grad_w_inner, 'col', scatter_dimension=0, tiled=True)  79.1 us
    dot_general x8, matrix products, query_step(): jnp.einsum('hqk,khd->qhd', d_scores, key_heads, preferred_element_type=jn...  58 us
    reduce_scatter x1, waiting for transfers between devices, per_device(): lax.psum_scatter(grad_w_output, 'col', scatter_dimension=1, tiled=True)  54.9 us
    all_gather x1, blocking collectives, per_device(): lax.all_gather(w_output, 'col', axis=1, tiled=True)  50 us
  transfers between devices with their start and end apart: 30, of which 14 were waited for; matrix products, arithmetic and copies ran while one was open for 24% of the time, Pallas kernels for 0%

commit v1 on v0

v1 whole, which is shorter than its diff:
```python
import functools

import jax
import jax.numpy as jnp
from jax import lax
from jax.experimental import pallas as pl
from jax.experimental.pallas import tpu as pltpu
from jax.sharding import PartitionSpec as P

D = 768
HALF = 384
HEAD_DIM = 64
FF_HALF = 1536
PAIRS = 3
SPAN = 8
EPSILON = 1e-12
MASKED = -1e30
MESH = pl.DeviceIdType.MESH
F32 = jnp.float32
BF16 = jnp.bfloat16
REST = HALF + 2 * FF_HALF
WIDE = REST + 128
QKV = 3 * HALF


def dot(left, right, contract):
    return lax.dot_general(left, right, (contract, ((), ())), preferred_element_type=F32)


NN = ((1,), (0,))
NT = ((1,), (1,))
TN = ((0,), (0,))


class Place:
    def __init__(self, size):
        self.size = size
        self.planes = size // 4
        self.r = lax.axis_index("row")
        col = lax.axis_index("col")
        self.base = lax.div(col, size) * size
        inner = lax.rem(col, size)
        self.slot = lax.div(col, SPAN)
        self.block = lax.rem(col, SPAN)
        self.z = lax.div(inner, 4)
        self.y = lax.rem(lax.div(inner, 2), 2)
        self.j = lax.rem(inner, 2)
        self.zl = lax.rem(self.z, 2)

    def plane(self, step):
        return lax.rem(self.z + step + self.planes, self.planes)

    def device(self, r, z, y, j):
        return (r, self.base + z * 4 + y * 2 + j)

    def to_z(self, step):
        return self.device(self.r, self.plane(step), self.y, self.j)

    def to_z_near(self):
        return self.device(self.r, self.z - self.zl + (1 - self.zl), self.y, self.j)

    def to_y(self):
        return self.device(self.r, self.z, 1 - self.y, self.j)

    def to_x(self):
        return self.device(1 - self.r, self.z, self.y, self.j)

    def to_core(self):
        return self.device(self.r, self.z, self.y, 1 - self.j)

    def col_block(self, z, y, j):
        return z * 4 + y * 2 + j

    def any_block(self, r, z, y, j):
        return r * self.size + z * 4 + y * 2 + j

    def near_block(self, dz, dy, j):
        return lax.rem(self.zl + dz, 2) * 4 + lax.rem(self.y + dy, 2) * 2 + j


def meet(place):
    barrier = pltpu.get_barrier_semaphore()
    peers = [place.to_z(step) for step in range(1, place.planes)]
    peers += [place.to_y(), place.to_x(), place.to_core()]
    for peer in peers:
        pl.semaphore_signal(barrier, inc=1, device_id=peer, device_id_type=MESH)
    pl.semaphore_wait(barrier, len(peers))


def send(src, dst, sems, index, peer):
    return pltpu.make_async_remote_copy(
        src_ref=src,
        dst_ref=dst,
        send_sem=sems[0].at[index],
        recv_sem=sems[1].at[index],
        device_id=peer,
        device_id_type=MESH,
    )


class Gather:
    def __init__(self, place, own, full, sems, with_rows):
        self.place, self.own, self.full, self.sems = place, own, full, sems
        self.rows = 2 if with_rows else 1
        self.with_rows = with_rows
        n = place.planes
        self.at_y = n - 1
        self.at_x = self.at_y + n
        self.at_c = self.at_x + (2 * n if with_rows else 0)
        self.total = self.at_c + 2 * n * self.rows

    def index(self, n, k, m, j):
        p = self.place
        z, y = p.plane(-k), lax.rem(p.y + m, 2)
        if self.with_rows:
            return p.any_block(lax.rem(p.r + n, 2), z, y, j)
        return p.col_block(z, y, j)

    def move(self, number, peer, n, k, m, j, local):
        where = self.index(n, k, m, j)
        src = self.own if local else self.full.at[where]
        return send(src, self.full.at[where], self.sems, number, peer)

    def z_sends(self):
        p = self.place
        for step in range(1, p.planes):
            self.move(step - 1, p.to_z(step), 0, 0, 0, p.j, True).start()

    def z_done(self, k):
        p = self.place
        self.move(k - 1, p.to_z(k), 0, k, 0, p.j, False).wait_recv()

    def y_send(self, k):
        p = self.place
        self.move(self.at_y + k, p.to_y(), 0, k, 0, p.j, k == 0).start()

    def y_done(self, k):
        p = self.place
        self.move(self.at_y + k, p.to_y(), 0, k, 1, p.j, False).wait_recv()

    def x_send(self, k, m):
        p = self.place
        self.move(self.at_x + 2 * k + m, p.to_x(), 0, k, m, p.j, k + m == 0).start()

    def x_done(self, k, m):
        p = self.place
        self.move(self.at_x + 2 * k + m, p.to_x(), 1, k, m, p.j, False).wait_recv()

    def c_number(self, n, k, m):
        return self.at_c + (2 * k + m) * self.rows + n

    def c_send(self, n, k, m):
        p = self.place
        number = self.c_number(n, k, m)
        self.move(number, p.to_core(), n, k, m, p.j, n + k + m == 0).start()

    def c_done(self, n, k, m):
        p = self.place
        self.move(self.c_number(n, k, m), p.to_core(), n, k, m, 1 - p.j, False).wait_recv()

    def all_sent(self):
        for number in range(self.total):
            send(self.own, self.own, self.sems, number, self.place.to_core()).wait_send()


def kernel_a(
    size,
    lengths,
    hid,
    wq_in,
    bq_in,
    wr_in,
    cot,
    hid_out,
    wq_out,
    q_out,
    kv_out,
    p_out,
    m_out,
    lse_out,
    ctxt_out,
    ctx_out,
    cot_out,
    wr_all,
    hid_all,
    wq_all,
    bq_all,
    kv,
    qs,
    qm,
    acc,
    high,
    low,
    pbuf,
    ctx_tp,
    wr_send,
    wr_recv,
    wq_send,
    wq_recv,
    bq_send,
    bq_recv,
    kv_send,
    kv_recv,
    one_send,
    one_recv,
    local,
    p_sem,
):
    place = Place(size)
    rows = hid.shape[0]
    part = rows // 2
    n = place.planes
    r, y, j = place.r, place.y, place.j
    meet(place)

    single = (one_send, one_recv)
    own_rows = pl.ds(pl.multiple_of(r * part, part), part)
    other_rows = pl.ds(pl.multiple_of((1 - r) * part, part), part)
    to_hid = send(hid, hid_all.at[r], single, 0, place.to_x())
    to_hid.start()
    wq = Gather(place, wq_in, wq_all, (wq_send, wq_recv), False)
    bq = Gather(place, bq_in, bq_all, (bq_send, bq_recv), False)
    rest = Gather(place, wr_in, wr_all, (wr_send, wr_recv), True)
    for gather in (wq, bq):
        gather.z_sends()
        gather.y_send(0)
        gather.c_send(0, 0, 0)
    to_cot = send(cot.at[other_rows], cot_out.at[r], single, 1, place.to_x())
    to_cot.start()
    rest_local = pltpu.make_async_copy(
        wr_in, wr_all.at[place.any_block(r, place.z, y, j)], local.at[0]
    )
    rest_local.start()
    cot_local = pltpu.make_async_copy(cot.at[own_rows], cot_out.at[r], local.at[1])
    cot_local.start()
    hid_all[r] = hid[...]
    wq_all[place.col_block(place.z, y, j)] = wq_in[...]
    bq_all[place.col_block(place.z, y, j)] = bq_in[...]
    for k in range(1, n):
        for gather in (wq, bq):
            gather.z_done(k)
            gather.y_send(k)
            gather.c_send(0, k, 0)
    for k in range(n):
        for gather in (wq, bq):
            gather.y_done(k)
            gather.c_send(0, k, 1)
    rest.z_sends()
    rest.y_send(0)
    rest.x_send(0, 0)
    rest.c_send(0, 0, 0)
    for k in range(n):
        for m in range(2):
            for gather in (wq, bq):
                gather.c_done(0, k, m)
    send(hid, hid_all.at[1 - r], single, 0, place.to_x()).wait_recv()

    hid_local = pltpu.make_async_copy(hid_all, hid_out, local.at[2])
    hid_local.start()
    wq_local = pltpu.make_async_copy(wq_all, wq_out, local.at[3])
    wq_local.start()

    biases = jnp.sum(bq_all[...].astype(F32), axis=0)
    own = place.near_block(0, 0, j)
    half = size // 2
    for which in (1, 2, 0):
        columns = slice(which * HALF, (which + 1) * HALF)
        total = dot(hid_all[0], wq_all[:half, :, columns].reshape(HALF, HALF), NN)
        total += dot(hid_all[1], wq_all[half:, :, columns].reshape(HALF, HALF), NN)
        if which == 0:
            total += biases[0:1]
        if which == 2:
            total += biases[1:2]
        total = total.astype(BF16)
        for p in range(PAIRS):
            piece = total[:, p * 128 : (p + 1) * 128]
            if which == 0:
                lane = lax.broadcasted_iota(jnp.int32, (rows, 128), 1)
                piece = piece * jnp.asarray(0.125, BF16)
                qs[p] = piece
                qm[2 * p] = jnp.where(lane < HEAD_DIM, piece, jnp.zeros_like(piece))
                qm[2 * p + 1] = jnp.where(lane >= HEAD_DIM, piece, jnp.zeros_like(piece))
            else:
                kv[own, (which - 1) * PAIRS + p] = piece
    acc[...] = jnp.zeros_like(acc)
    high[...] = jnp.full_like(high, MASKED)
    low[...] = jnp.zeros_like(low)

    n_one = place.device(r, place.z - place.zl + lax.rem(place.zl + 1 - j, 2), lax.rem(y + j, 2), j)
    n_two = place.device(r, place.z - place.zl + lax.rem(place.zl + j, 2), lax.rem(y + 1 - j, 2), j)
    kvs = (kv_send, kv_recv)

    def kv_block(i):
        pair, core = lax.div(i, 2), lax.rem(j + lax.rem(i, 2), 2)
        b0, b1 = lax.rem(pair, 2), lax.div(pair, 2)
        return place.near_block(b0 * (1 - core) + b1 * core, b0 * core + b1 * (1 - core), core)

    def kv_move(number, what, peer):
        where = kv_block(what)
        return send(kv.at[where], kv.at[where], kvs, number, peer)

    kv_move(1, 0, place.to_core()).start()
    kv_move(2, 0, n_one).start()
    q_local = pltpu.make_async_copy(qs, q_out, local.at[4])
    q_local.start()

    def arrived(number):
        kv_move(number, number, n_one).wait_recv()

    def at_5():
        kv_move(2, 0, n_one).wait_send()
        kv_move(4, 0, n_two).start()
        arrived(2)
        kv_move(3, 2, place.to_core()).start()

    def at_11():
        kv_move(4, 0, n_two).wait_send()
        kv_move(6, 2, n_two).start()
        arrived(4)
        kv_move(5, 4, place.to_core()).start()

    def at_18():
        arrived(6)
        kv_move(7, 6, place.to_core()).start()

    def rest_y(k):
        rest.z_done(k)
        rest.y_send(k)
        rest.x_send(k, 0)
        rest.c_send(0, k, 0)

    def rest_x(k):
        rest.y_done(k)
        rest.x_send(k, 1)
        rest.c_send(0, k, 1)

    def rest_c(k, m):
        rest.x_done(k, m)
        rest.c_send(1, k, m)

    events = {
        3: [lambda: arrived(1)],
        5: [at_5],
        9: [lambda: arrived(3)],
        11: [at_11],
        15: [lambda: arrived(5)],
        18: [at_18],
        21: [lambda: arrived(7)],
    }

    def add(step, *what):
        events.setdefault(step, []).extend(what)

    spots = [6, 8, 10]
    for k in range(1, n):
        add(spots[k - 1], functools.partial(rest_y, k))
    for k in range(n):
        add(12 + k, functools.partial(rest_x, k))
    for k in range(n):
        add(16 + 2 * k, functools.partial(rest_c, k, 0))
        add(17 + 2 * k, functools.partial(rest_c, k, 1))

    length = lengths[place.slot]

    def p_copy(t, slot):
        i, p = lax.div(t, PAIRS), lax.rem(t, PAIRS)
        return pltpu.make_async_copy(
            pbuf.at[slot], p_out.at[kv_block(i), pl.ds(2 * p, 2)], p_sem.at[slot]
        )

    def kv_copy(i):
        where = kv_block(i)
        return pltpu.make_async_copy(kv.at[where], kv_out.at[where], local.at[8 + i])

    steps = SPAN * PAIRS

    def attend(t, carry):
        i, p = lax.div(t, PAIRS), lax.rem(t, PAIRS)
        for step, calls in sorted(events.items()):

            @pl.when(t == step)
            def _(calls=calls):
                for call in calls:
                    call()

        @pl.when(p == 0)
        def _():
            kv_copy(i).start()

        slot = lax.rem(t, 2)

        @pl.when(t >= 2)
        def _():
            p_copy(t - 2, slot).wait()

        where = kv_block(i)
        place_of = lax.broadcasted_iota(jnp.int32, (rows, 128), 0) + where * rows
        bias = jnp.where(place_of < length, 0.0, MASKED)
        bias = jnp.concatenate([bias] * (rows // 128), axis=1)
        key = kv[where, p]
        value_t = kv[where, PAIRS + p].T
        for h in range(2):
            g = 2 * p + h
            scores = dot(key, qm[g], NT) + bias
            top = jnp.max(scores, axis=0, keepdims=True)
            weights = jnp.exp(scores - top)
            below = jnp.sum(weights, axis=0, keepdims=True)
            rounded = weights.astype(BF16)
            pbuf[slot, h] = rounded
            term = dot(value_t[h * HEAD_DIM : (h + 1) * HEAD_DIM], rounded, NN)
            old = high[g]
            new = jnp.maximum(old, top)
            keep_old, keep_new = jnp.exp(old - new), jnp.exp(top - new)
            high[g] = new
            low[g] = low[g] * keep_old + below * keep_new
            acc[g] = acc[g] * keep_old + term * keep_new
            m_out[where, g] = top
        p_copy(t, slot).start()
        return carry

    lax.fori_loop(0, steps, attend, jnp.int32(0))

    column = lax.broadcasted_iota(jnp.int32, (1, rows), 1) + place.block * rows
    keep = jnp.where(column < length, 1.0, 0.0)
    for p in range(PAIRS):
        parts = []
        for h in range(2):
            g = 2 * p + h
            lse_out[g] = high[g] + jnp.log(low[g])
            parts.append(acc[g] / low[g])
        both = jnp.concatenate(parts, axis=0)
        ctxt_out[p] = both
        ctx_tp[:, p * 128 : (p + 1) * 128] = (both * keep).T.astype(BF16)
    for t in (steps - 2, steps - 1):
        p_copy(jnp.int32(t), t % 2).wait()
    to_ctx = send(ctx_tp.at[other_rows], ctx_out.at[r], single, 2, place.to_x())
    to_ctx.start()
    ctx_local = pltpu.make_async_copy(ctx_tp.at[own_rows], ctx_out.at[r], local.at[5])
    ctx_local.start()
    for n_at in range(2):
        for k in range(n):
            for m in range(2):
                rest.c_done(n_at, k, m)
    for gather in (wq, bq, rest):
        gather.all_sent()
    for number in (1, 3, 4, 5, 6, 7):
        if number != 4:
            kv_move(number, 0, n_one).wait_send()
    for number, ref in ((0, hid_all), (1, cot_out), (2, ctx_out)):
        if number:
            send(ref.at[1 - r], ref.at[1 - r], single, number, place.to_x()).wait_recv()
        send(ref.at[1 - r], ref.at[1 - r], single, number, place.to_x()).wait_send()
    for copy in (rest_local, cot_local, hid_local, wq_local, q_local, ctx_local):
        copy.wait()
    for i in range(SPAN):
        kv_copy(jnp.int32(i)).wait()


def forward_attention(size, lengths, hid, wq_in, bq_in, wr_in, cot):
    rows = hid.shape[0]
    part = rows // 2
    blk = wq_in.shape[0]
    n = size // 4
    any_space = pl.BlockSpec(memory_space=pl.ANY)
    vmem = pl.BlockSpec(memory_space=pltpu.VMEM)
    shape = jax.ShapeDtypeStruct
    n_col, n_all = (n - 1) + n + 2 * n, (n - 1) + n + 2 * n + 4 * n
    dma = pltpu.SemaphoreType.DMA
    return pl.pallas_call(
        functools.partial(kernel_a, size),
        out_shape=(
            shape((2, rows, HALF), BF16),
            shape((size, blk, QKV), BF16),
            shape((PAIRS, rows, 128), BF16),
            shape((SPAN, 2 * PAIRS, rows, 128), BF16),
            shape((SPAN, 2 * PAIRS, rows, rows), BF16),
            shape((SPAN, 2 * PAIRS, 1, rows), F32),
            shape((2 * PAIRS, 1, rows), F32),
            shape((PAIRS, 128, rows), F32),
            shape((2, part, HALF), BF16),
            shape((2, part, HALF), BF16),
            shape((2 * size, blk, WIDE), BF16),
        ),
        in_specs=[pl.BlockSpec(memory_space=pltpu.SMEM)] + [vmem] * 5,
        out_specs=[any_space] * 5 + [vmem] * 3 + [any_space] * 3,
        scratch_shapes=[
            pltpu.VMEM((2, rows, HALF), BF16),
            pltpu.VMEM((size, blk, QKV), BF16),
            pltpu.VMEM((size, 16, HALF), BF16),
            pltpu.VMEM((SPAN, 2 * PAIRS, rows, 128), BF16),
            pltpu.VMEM((PAIRS, rows, 128), BF16),
            pltpu.VMEM((2 * PAIRS, rows, 128), BF16),
            pltpu.VMEM((2 * PAIRS, HEAD_DIM, rows), F32),
            pltpu.VMEM((2 * PAIRS, 1, rows), F32),
            pltpu.VMEM((2 * PAIRS, 1, rows), F32),
            pltpu.VMEM((2, 2, rows, rows), BF16),
            pltpu.VMEM((rows, HALF), BF16),
            dma((n_all,)),
            dma((n_all,)),
            dma((n_col,)),
            dma((n_col,)),
            dma((n_col,)),
            dma((n_col,)),
            dma((8,)),
            dma((8,)),
            dma((3,)),
            dma((3,)),
            dma((16,)),
            dma((2,)),
        ],
        compiler_params=pltpu.CompilerParams(
            collective_id=0, has_side_effects=True, vmem_limit_bytes=60 * 2**20
        ),
        name="forward_attention",
    )(lengths, hid, wq_in, bq_in, wr_in, cot)


def kernel_c(
    size,
    dctx,
    qs,
    m_in,
    lse_in,
    ctxt,
    hid_all,
    wq_all,
    lay,
    dres_low,
    dres_own,
    kv_in,
    p_in,
    g_in,
    rest_out,
    qkv_out,
    bias_out,
    grad_out,
    lay_out,
    d_ctx,
    dtot,
    delta,
    qm,
    acc,
    kv,
    pbuf,
    big,
    cb,
    rb,
    st,
    b1,
    b2,
    b3,
    b4,
    d_all,
    gq,
    q1,
    q2,
    q3,
    near,
    dres_far,
    bias_own,
    bias_got,
    one_send,
    one_recv,
    kv_send,
    kv_recv,
    g_send,
    g_recv,
    q_send,
    q_recv,
    s_send,
    s_recv,
    load,
    p_sem,
):
    place = Place(size)
    rows = qs.shape[1]
    part = rows // 2
    n = place.planes
    r, y, j = place.r, place.y, place.j
    meet(place)
    single = (one_send, one_recv)
    gs = (g_send, g_recv)
    ks = (kv_send, kv_recv)
    at_x, at_y, at_z = 4 * n, 6 * n, 7 * n

    own_rows = pl.ds(pl.multiple_of(r * part, part), part)
    other_rows = pl.ds(pl.multiple_of((1 - r) * part, part), part)
    send(dctx.at[1 - r], d_ctx.at[own_rows], single, 0, place.to_x()).start()

    def g_block(index, core):
        n_at, m, k = lax.div(index, 2 * n), lax.rem(lax.div(index, n), 2), lax.rem(index, n)
        return place.any_block(
            lax.rem(r + 1 + n_at, 2), place.plane(k), lax.rem(y + 1 + m, 2), core
        )

    def c_move(index):
        return send(g_in.at[g_block(index, 1 - j)], b1.at[index], gs, index, place.to_core())

    def g_load(index):
        return pltpu.make_async_copy(g_in.at[g_block(index, j)], st.at[index], load.at[8 + index])

    def loop(count, body):
        def step(index, carry):
            body(index)
            return carry

        lax.fori_loop(0, count, step, jnp.int32(0))

    loop(4 * n, lambda index: c_move(index).start())
    loop(4 * n, lambda index: g_load(index).start())

    def b_block(i):
        pair, core = lax.div(i, 2), lax.rem(j + 1 + lax.rem(i, 2), 2)
        return place.near_block(1 - lax.div(pair, 2), 1 - lax.rem(pair, 2), core)

    def kv_load(i):
        return pltpu.make_async_copy(kv_in.at[b_block(i)], kv.at[i], load.at[i])

    def p_load(t, slot):
        i, p = lax.div(t, PAIRS), lax.rem(t, PAIRS)
        return pltpu.make_async_copy(
            p_in.at[b_block(i), pl.ds(2 * p, 2)], pbuf.at[slot], p_sem.at[slot]
        )

    p_load(jnp.int32(0), 0).start()
    loop(SPAN, lambda i: kv_load(i).start())

    lane = lax.broadcasted_iota(jnp.int32, (rows, 128), 1)
    for p in range(PAIRS):
        piece = qs[p]
        qm[2 * p] = jnp.where(lane < HEAD_DIM, piece, jnp.zeros_like(piece))
        qm[2 * p + 1] = jnp.where(lane >= HEAD_DIM, piece, jnp.zeros_like(piece))
    acc[...] = jnp.zeros_like(acc)
    lay_local = pltpu.make_async_copy(lay.at[r], lay_out.at[own_rows], load.at[8 + 4 * n])
    lay_local.start()
    d_ctx[own_rows, :] = dctx[r]
    send(dctx.at[1 - r], d_ctx.at[other_rows], single, 0, place.to_x()).wait_recv()
    send(lay.at[1 - r], lay_out.at[own_rows], single, 1, place.to_x()).start()
    send(dres_low.at[1 - r], dres_far, single, 2, place.to_x()).start()
    upper = lax.broadcasted_iota(jnp.int32, (128, rows), 0) < HEAD_DIM
    for p in range(PAIRS):
        turned = d_ctx[:, p * 128 : (p + 1) * 128].astype(F32).T
        product = turned * ctxt[p]
        delta[2 * p] = jnp.sum(product[:HEAD_DIM], axis=0, keepdims=True)
        delta[2 * p + 1] = jnp.sum(product[HEAD_DIM:], axis=0, keepdims=True)
        dtot[2 * p] = jnp.where(upper, turned, 0.0)
        dtot[2 * p + 1] = jnp.where(upper, 0.0, turned)

    def core_send(pair):
        return send(big.at[2 * pair], cb.at[pair], ks, pair, place.to_core())

    def core_add(pair):
        core_send(pair).wait_recv()
        for piece in range(2 * PAIRS):
            total = big[2 * pair + 1, piece].astype(F32) + cb[pair, piece].astype(F32)
            big[2 * pair + 1, piece] = total.astype(BF16)

    keys, values = pl.ds(0, PAIRS), pl.ds(PAIRS, PAIRS)

    def hop(number):
        pair, part_of, along_z = (
            (0, keys, False),
            (0, values, True),
            (1, keys, True),
            (1, values, True),
            (2, values, False),
            (2, keys, False),
        )[number]
        peer = place.to_z_near() if along_z else place.to_y()
        return send(big.at[2 * pair + 1, part_of], rb.at[number], ks, 4 + number, peer)

    def hop_add(number, pair, start):
        hop(number).wait_recv()
        for piece in range(PAIRS):
            total = big[2 * pair + 1, start + piece].astype(F32) + rb[number, piece].astype(F32)
            big[2 * pair + 1, start + piece] = total.astype(BF16)

    def fold(target, source, at):
        total = target[at].astype(F32) + source.astype(F32)
        target[at] = total.astype(BF16)

    def g_core_add(index):
        c_move(index).wait_recv()
        g_load(index).wait()
        fold(st, b1[index], index)

    def g_x_send(index):
        return send(st.at[index], b2.at[index], gs, at_x + index, place.to_x())

    def g_x_add(index):
        g_x_send(index).wait_recv()
        fold(st, b2[index], 2 * n + index)

    def g_y_send(k):
        return send(st.at[2 * n + k], b3.at[k], gs, at_y + k, place.to_y())

    def g_y_add(k):
        g_y_send(k).wait_recv()
        fold(st, b3[k], 3 * n + k)

    def g_z_send(k):
        return send(st.at[3 * n + k], b4.at[k - 1], gs, at_z + k - 1, place.to_z(k))

    events = {}

    def add(step, what, *inputs):
        events.setdefault(step, []).append(functools.partial(what, *inputs))

    def start(what, number):
        what(number).start()

    for at in range(n):
        add(at, lambda at: loop(2, lambda i: g_core_add(2 * at + i)), at)
        add(at + 1, lambda at: loop(2, lambda i: g_x_send(2 * at + i).start()), at)
    for at in range(n):
        add(n + 1 + at, lambda at: loop(2, lambda i: g_core_add(2 * n + 2 * at + i)), at)
    for pair in range(4):
        add(6 * pair + 3, start, core_send, pair)
        if pair < 3:
            add(6 * pair + 6, core_add, pair)
    add(7, start, hop, 0)
    add(7, start, hop, 1)
    add(13, start, hop, 3)
    add(17, hop_add, 0, 1, 0)
    add(18, start, hop, 2)
    add(19, start, hop, 5)
    add(20, hop_add, 1, 2, PAIRS)
    add(21, start, hop, 4)

    steps = SPAN * PAIRS

    def back(t, carry):
        i, p = lax.div(t, PAIRS), lax.rem(t, PAIRS)
        for step, calls in sorted(events.items()):

            @pl.when(t == step)
            def _(calls=calls):
                for call in calls:
                    call()

        slot = lax.rem(t, 2)

        @pl.when(t + 1 < steps)
        def _():
            p_load(t + 1, 1 - slot).start()

        @pl.when(p == 0)
        def _():
            kv_load(i).wait()

        p_load(t, slot).wait()
        where = b_block(i)
        key = kv[i, p]
        value = kv[i, PAIRS + p]
        key_t = key.T
        d_key = d_value = None
        for h in range(2):
            g = 2 * p + h
            factor = jnp.exp(m_in[where, g] - lse_in[g])
            d_rows = (dtot[g] * factor).astype(BF16)
            weights = pbuf[slot, h]
            d_probs = dot(value, d_rows, NN)
            d_scores = (weights.astype(F32) * (d_probs - delta[g] * factor)).astype(BF16)
            value_term = dot(weights, d_rows, NT)
            key_term = dot(d_scores, qm[g], NN)
            acc[g] += dot(key_t[h * HEAD_DIM : (h + 1) * HEAD_DIM], d_scores, NN)
            d_key = key_term if d_key is None else d_key + key_term
            d_value = value_term if d_value is None else d_value + value_term
        big[i, p] = d_key.astype(BF16)
        big[i, PAIRS + p] = d_value.astype(BF16)
        return carry

    lax.fori_loop(0, steps, back, jnp.int32(0))

    for p in range(PAIRS):
        both = jnp.concatenate([acc[2 * p], acc[2 * p + 1]], axis=0)
        d_all[:, p * 128 : (p + 1) * 128] = (both.T * 0.125).astype(BF16)
    core_send(3).wait_recv()
    for number in (2, 3, 4, 5):
        hop(number).wait_recv()
    for piece in range(PAIRS):
        at = HALF + piece * 128
        total = big[7, piece].astype(F32) + cb[3, piece].astype(F32)
        total += rb[2, piece].astype(F32) + rb[5, piece].astype(F32)
        d_all[:, at : at + 128] = total.astype(BF16)
        at = 2 * HALF + piece * 128
        total = big[7, PAIRS + piece].astype(F32) + cb[3, PAIRS + piece].astype(F32)
        total += rb[3, piece].astype(F32) + rb[4, piece].astype(F32)
        d_all[:, at : at + 128] = total.astype(BF16)

    half = size // 2
    blk = wq_all.shape[1]

    def input_term(which):
        weight = wq_all[pl.ds(which * half, half)].reshape(HALF, QKV)
        return dot(d_all[...], weight, NT)

    near[0] = input_term(1 - r).astype(BF16)
    for which in range(2):
        term = dot(hid_all[which], d_all[...], TN).astype(BF16)
        gq[which * half : (which + 1) * half] = term.reshape(half, blk, QKV)
    to_near = send(near.at[0], near.at[1], single, 3, place.to_x())
    to_near.start()
    qz = (q_send, q_recv)

    def q_block(index, core):
        m, k = lax.div(index, n), lax.rem(index, n)
        return place.col_block(place.plane(k), lax.rem(y + 1 + m, 2), core)

    def q_core(index):
        return send(gq.at[q_block(index, 1 - j)], q1.at[index], qz, index, place.to_core())

    def q_side(k):
        return send(gq.at[q_block(k, j)], q2.at[k], qz, 2 * n + k, place.to_y())

    def q_plane(k):
        return send(gq.at[q_block(n + k, j)], q3.at[k - 1], qz, 3 * n + k - 1, place.to_z(k))

    loop(2 * n, lambda index: q_core(index).start())
    bias_own[0, 0:1] = jnp.sum(d_all[:, :HALF].astype(F32), axis=0, keepdims=True)
    bias_own[0, 1:2] = jnp.sum(d_all[:, 2 * HALF :].astype(F32), axis=0, keepdims=True)
    bias_own[0, 2:8] = jnp.zeros((6, HALF), F32)
    sz = (s_send, s_recv)

    def small(number):
        level = min(number, 2)
        peer = (place.to_core(), place.to_y(), place.to_z(max(number - 1, 1)))[level]
        return send(bias_own.at[level], bias_got.at[number], sz, number, peer)

    grad_out[...] = input_term(r)
    small(0).start()

    def q_core_add(index):
        q_core(index).wait_recv()
        fold(gq, q1[index], q_block(index, j))

    loop(n, q_core_add)
    small(0).wait_recv()
    bias_own[1] = bias_own[0] + bias_got[0]
    loop(n, lambda k: q_side(k).start())
    loop(n, lambda k: q_core_add(n + k))
    small(1).start()
    grad_out[own_rows, :] = grad_out[own_rows, :] + dres_own[...]
    send(dres_low.at[1 - r], dres_far, single, 2, place.to_x()).wait_recv()
    grad_out[other_rows, :] = grad_out[other_rows, :] + dres_far[...].astype(F32)
    small(1).wait_recv()
    bias_own[2] = bias_own[1] + bias_got[1]

    def q_side_add(k):
        q_side(k).wait_recv()
        fold(gq, q2[k], q_block(n + k, j))

    loop(n, q_side_add)
    loop(n - 1, lambda k: q_plane(k + 1).start())
    for step in range(1, n):
        small(1 + step).start()

    loop(n, g_x_add)
    loop(n, lambda k: g_y_send(k).start())
    loop(n, lambda k: g_x_add(n + k))
    loop(n, g_y_add)
    for k in range(1, n):
        g_z_send(k).start()
    to_near.wait_recv()
    grad_out[...] = grad_out[...] + near[1].astype(F32)
    total = bias_own[2]
    for step in range(1, n):
        small(1 + step).wait_recv()
        total = total + bias_got[1 + step]
    bias_out[...] = total
    total = gq[q_block(n, j)].astype(F32)
    for k in range(1, n):
        q_plane(k).wait_recv()
        total = total + q3[k - 1].astype(F32)
    qkv_out[...] = total
    total = st[3 * n].astype(F32)
    for k in range(1, n):
        g_z_send(k).wait_recv()
        total = total + b4[k - 1].astype(F32)
    rest_out[...] = total

    loop(4 * n, lambda index: c_move(index).wait_send())
    loop(2 * n, lambda index: g_x_send(index).wait_send())
    loop(n, lambda k: g_y_send(k).wait_send())
    for k in range(1, n):
        g_z_send(k).wait_send()
        q_plane(k).wait_send()
        small(1 + k).wait_send()
    small(0).wait_send()
    small(1).wait_send()
    loop(2 * n, lambda index: q_core(index).wait_send())
    loop(n, lambda k: q_side(k).wait_send())
    for pair in range(4):
        core_send(pair).wait_send()
    for number in range(6):
        hop(number).wait_send()
    to_near.wait_send()
    send(dctx.at[1 - r], d_ctx.at[own_rows], single, 0, place.to_x()).wait_send()
    to_lay = send(lay.at[1 - r], lay_out.at[other_rows], single, 1, place.to_x())
    to_lay.wait_recv()
    to_lay.wait_send()
    send(dres_low.at[1 - r], dres_far, single, 2, place.to_x()).wait_send()
    lay_local.wait()


def backward_attention(
    size, dctx, qs, m_in, lse_in, ctxt, hid_all, wq_all, lay, dres_low, dres_own, kv_in, p_in, g_in
):
    rows = qs.shape[1]
    part = rows // 2
    blk = wq_all.shape[1]
    n = size // 4
    any_space = pl.BlockSpec(memory_space=pl.ANY)
    vmem = pl.BlockSpec(memory_space=pltpu.VMEM)
    shape = jax.ShapeDtypeStruct
    dma = pltpu.SemaphoreType.DMA
    scratch = pltpu.VMEM
    g_count, q_count = 4 * n + 2 * n + n + n - 1, 2 * n + n + n - 1
    return pl.pallas_call(
        functools.partial(kernel_c, size),
        out_shape=(
            shape((blk, WIDE), F32),
            shape((blk, QKV), F32),
            shape((8, HALF), F32),
            shape((rows, HALF), F32),
            shape((rows, HALF), BF16),
        ),
        in_specs=[vmem] * 10 + [any_space] * 3,
        out_specs=[vmem] * 4 + [any_space],
        scratch_shapes=[
            scratch((rows, HALF), BF16),
            scratch((2 * PAIRS, 128, rows), F32),
            scratch((2 * PAIRS, 1, rows), F32),
            scratch((2 * PAIRS, rows, 128), BF16),
            scratch((2 * PAIRS, HEAD_DIM, rows), F32),
            scratch((SPAN, 2 * PAIRS, rows, 128), BF16),
            scratch((2, 2, rows, rows), BF16),
            scratch((SPAN, 2 * PAIRS, rows, 128), BF16),
            scratch((4, 2 * PAIRS, rows, 128), BF16),
            scratch((6, PAIRS, rows, 128), BF16),
            scratch((4 * n, blk, WIDE), BF16),
            scratch((4 * n, blk, WIDE), BF16),
            scratch((2 * n, blk, WIDE), BF16),
            scratch((n, blk, WIDE), BF16),
            scratch((n - 1, blk, WIDE), BF16),
            scratch((rows, QKV), BF16),
            scratch((size, blk, QKV), BF16),
            scratch((2 * n, blk, QKV), BF16),
            scratch((n, blk, QKV), BF16),
            scratch((n - 1, blk, QKV), BF16),
            scratch((2, rows, HALF), BF16),
            scratch((part, HALF), BF16),
            scratch((3, 8, HALF), F32),
            scratch((n + 1, 8, HALF), F32),
            dma((4,)),
            dma((4,)),
            dma((10,)),
            dma((10,)),
            dma((g_count,)),
            dma((g_count,)),
            dma((q_count,)),
            dma((q_count,)),
            dma((n + 1,)),
            dma((n + 1,)),
            dma((9 + 4 * n,)),
            dma((2,)),
        ],
        compiler_params=pltpu.CompilerParams(
            collective_id=1, has_side_effects=True, vmem_limit_bytes=63 * 2**20
        ),
        name="backward_attention",
    )(dctx, qs, m_in, lse_in, ctxt, hid_all, wq_all, lay, dres_low, dres_own, kv_in, p_in, g_in)


def gelu(argument):
    return 0.5 * argument * (1.0 + lax.erf(argument * 0.7071067811865476))


def gelu_slope(argument):
    bell = jnp.exp(argument * argument * -0.5) * 0.3989422804014327
    return 0.5 * (1.0 + lax.erf(argument * 0.7071067811865476)) + argument * bell


def norm_forward(resid, gain, shift):
    center = resid - jnp.mean(resid, axis=1, keepdims=True)
    scale = lax.rsqrt(jnp.mean(center * center, axis=1, keepdims=True) + EPSILON)
    normal = center * scale
    return normal * gain + shift, normal, scale


def norm_backward(incoming, normal, scale, gain):
    scaled = incoming * gain
    first = jnp.mean(scaled, axis=1, keepdims=True)
    second = jnp.mean(scaled * normal, axis=1, keepdims=True)
    result = scale * (scaled - first - normal * second)
    return result, jnp.sum(incoming * normal, axis=0), jnp.sum(incoming, axis=0)


def middle(size, keep, ctx, hidden, cotangent, wr_all):
    tall = wr_all.reshape(2, D, WIDE)
    w_out = [tall[h, :, :HALF] for h in range(2)]
    w_in = [tall[h, :, HALF : HALF + FF_HALF] for h in range(2)]
    w_outer = [tall[h, :, HALF + FF_HALF : REST] for h in range(2)]
    per = D // (2 * size)
    vectors = tall[:, :, REST : REST + 5].reshape(2 * size, 10 * per).astype(F32)
    b_output, b_outer, gain_one, shift_one, gain_two, shift_two = [
        vectors[:, at * per : (at + 1) * per].reshape(1, D) for at in range(6)
    ]
    b_inner = vectors[:, 6 * per :].reshape(2, 2 * D)

    attn = dot(ctx[0], w_out[0], NT) + dot(ctx[1], w_out[1], NT) + b_output
    normed, normal_one, scale_one = norm_forward(hidden.astype(F32) + attn, gain_one, shift_one)
    normed_low = normed.astype(BF16)
    inner = [dot(normed_low, w_in[h], NN) + b_inner[h] for h in range(2)]
    act = [gelu(inner[h]).astype(BF16) for h in range(2)]
    outer = dot(act[0], w_outer[0], NT) + dot(act[1], w_outer[1], NT) + b_outer
    result, normal_two, scale_two = norm_forward(normed + outer, gain_two, shift_two)
    seed = cotangent.astype(F32) * keep
    d_res_two, g_gain_two, g_shift_two = norm_backward(seed, normal_two, scale_two, gain_two)
    d_outer = d_res_two.astype(BF16)
    d_inner = [
        (dot(d_outer, w_outer[h], NN) * gelu_slope(inner[h])).astype(BF16) for h in range(2)
    ]
    d_normed = d_res_two + dot(d_inner[0], w_in[0], NT) + dot(d_inner[1], w_in[1], NT)
    d_res_one, g_gain_one, g_shift_one = norm_backward(d_normed, normal_one, scale_one, gain_one)
    d_attn = d_res_one.astype(BF16)
    d_context = [(dot(d_attn, w_out[h], NN) * keep).astype(BF16) for h in range(2)]

    sums = [
        jnp.sum(d_attn.astype(F32), axis=0),
        jnp.sum(d_outer.astype(F32), axis=0),
        g_gain_one,
        g_shift_one,
        g_gain_two,
        g_shift_two,
    ]
    g_b_inner = jnp.stack([jnp.sum(d_inner[h].astype(F32), axis=0) for h in range(2)])
    small = jnp.concatenate(
        [v.reshape(2 * size, per) for v in sums] + [g_b_inner.reshape(2 * size, 4 * per)], axis=1
    )
    small = jnp.pad(small.reshape(2, D, 5), ((0, 0), (0, 0), (0, 123))).astype(BF16)
    parts = []
    for h in range(2):
        parts += [
            jnp.concatenate(
                [
                    dot(d_attn, ctx[h], TN).astype(BF16),
                    dot(normed_low, d_inner[h], TN).astype(BF16),
                    dot(d_outer, act[h], TN).astype(BF16),
                    small[h],
                ],
                axis=1,
            )
        ]
    g_parts = jnp.stack(parts).reshape(wr_all.shape)
    return result.astype(BF16), d_res_one, d_attn, jnp.stack(d_context), g_parts


def halves(array):
    return jnp.stack([array[:, :HALF], array[:, HALF:]])


def per_device(
    group,
    hidden_in,
    cotangent,
    lengths,
    w_query,
    w_key,
    w_value,
    w_output,
    w_inner,
    w_outer,
    b_query,
    b_value,
    b_output,
    b_inner,
    b_outer,
    gain_one,
    shift_one,
    gain_two,
    shift_two,
):
    cols = lax.axis_size("col")
    size = group
    ways = cols // size
    col = lax.axis_index("col")
    row = lax.axis_index("row")
    inside = col % size
    rows = hidden_in.shape[0]
    part = rows // 2

    def regroup(block):
        if ways == 1:
            return block
        whole = lax.all_gather(block, "col", axis=0, tiled=True)
        count = block.shape[0] * ways
        return lax.dynamic_slice_in_dim(whole, inside * count, count, axis=0)

    wq_block = regroup(jnp.concatenate([w_query, w_key, w_value], axis=1))
    bq, bv = regroup(b_query), regroup(b_value)
    vectors = [
        regroup(v) for v in (b_output, b_outer, gain_one, shift_one, gain_two, shift_two, b_inner)
    ]
    blk = wq_block.shape[0]
    per = blk // 2
    column = jnp.concatenate(vectors).reshape(blk, 5)
    wr_block = jnp.concatenate(
        [
            regroup(w_output.T),
            regroup(w_inner),
            regroup(w_outer.T),
            jnp.pad(column, ((0, 0), (0, 123))),
        ],
        axis=1,
    )
    placed = jnp.stack([bq, bv]).reshape(2, 1, per)
    slots = lax.broadcasted_iota(jnp.int32, (1, size, 1), 1)
    placed = jnp.where(slots == inside, placed, jnp.zeros((), BF16)).reshape(2, HALF)
    placed = jnp.pad(placed, ((0, 14), (0, 0)))

    (hid_all, wq_all, qs, kv, probs, m_all, lse, ctxt, ctx_dp, cot_dp, wr_all) = forward_attention(
        size, lengths, hidden_in, wq_block, placed, wr_block, cotangent
    )

    spot = (col % SPAN) * rows + row * part + lax.broadcasted_iota(jnp.int32, (part, 1), 0)
    keep = (spot < lengths[col // SPAN]).astype(F32)
    hid_dp = lax.dynamic_slice_in_dim(hid_all, row * part, part, axis=1)
    hid_dp = jnp.concatenate([hid_dp[0], hid_dp[1]], axis=1)
    cot_own = jnp.concatenate([cot_dp[0], cot_dp[1]], axis=1)
    result, d_res_one, d_attn, d_context, g_parts = middle(
        size, keep, ctx_dp, hid_dp, cot_own, wr_all
    )
    d_res_own = lax.dynamic_slice_in_dim(d_res_one, row * HALF, HALF, axis=1)
    g_rest, g_qkv, g_bias, grad_in, layer_out = backward_attention(
        size,
        d_context,
        qs,
        m_all,
        lse,
        ctxt,
        hid_all,
        wq_all,
        halves(result),
        halves(d_attn),
        d_res_own,
        kv,
        probs,
        g_parts,
    )

    def spread(block):
        if ways == 1:
            return block
        count = block.shape[0]
        whole = jnp.zeros((count * size,) + block.shape[1:], block.dtype)
        whole = lax.dynamic_update_slice_in_dim(whole, block, inside * count, axis=0)
        return lax.psum_scatter(whole, "col", scatter_dimension=0, tiled=True)

    flat = g_rest[:, REST : REST + 5].reshape(10 * per)
    pieces = [spread(flat[at * per : (at + 1) * per]) for at in range(6)]
    g_b_output, g_b_outer, g_gain_one, g_shift_one, g_gain_two, g_shift_two = pieces
    g_b_inner = spread(flat[6 * per :])
    g_b_query = spread(lax.dynamic_slice_in_dim(g_bias[0], inside * per, per))
    g_b_value = spread(lax.dynamic_slice_in_dim(g_bias[1], inside * per, per))
    return (
        layer_out,
        grad_in,
        spread(g_qkv[:, :HALF]),
        spread(g_qkv[:, HALF : 2 * HALF]),
        spread(g_qkv[:, 2 * HALF :]),
        spread(g_rest[:, :HALF]).T,
        spread(g_rest[:, HALF : HALF + FF_HALF]),
        spread(g_rest[:, HALF + FF_HALF : REST]).T,
        g_b_query,
        g_b_value,
        g_b_output,
        g_b_inner,
        g_b_outer,
        g_gain_one,
        g_shift_one,
        g_gain_two,
        g_shift_two,
    )


def solution(mesh):
    cols = mesh.shape["col"]
    group = max(s for s in range(SPAN, cols + 1, 4) if cols % s == 0 and D // s % 16 == 0)
    token, weight, turned = P("col", "row"), P("col", "row"), P("row", "col")
    vector = P(("row", "col"))
    return jax.shard_map(
        functools.partial(per_device, group),
        mesh=mesh,
        in_specs=(token, token, P()) + (weight,) * 3 + (turned, weight, turned) + (vector,) * 9,
        out_specs=(token, token) + (weight,) * 3 + (turned, weight, turned) + (vector,) * 9,
        check_vma=False,
    )
```

time: 1330 us -> 336 us (0.25)
  waiting for transfers between devices: 452 us -> 0 us
  matrix products: 387 us -> 32.6 us
  blocking collectives: 304 us -> 0 us
  Pallas kernels: 0 us -> 255 us
  other arithmetic: 111 us -> 16 us
  between operations: 19.2 us -> 1.15 us
    dot_general x90 -> x18, matrix products: 387 us -> 32.6 us  [dot(): lax.dot_general(left, right, (contract, ((), ())), preferred_element_type...]
    reduce_scatter x7 -> x0, waiting for transfers between devices: 260 us -> none  [the longest x1 79.2 us: per_device(): lax.psum_scatter(grad_w_outer, 'col', scatter_dimension=1, tiled=True)]
    pallas_call x0 -> x2, Pallas kernels: none -> 255 us  [the longest x1 134 us: backward_attention(): pl.pallas_call(functools.partial(kernel_c, size), out_shape=(shape((blk,...]
    all_gather x8 -> x0, blocking collectives: 168 us -> none  [the longest x1 50 us: per_device(): lax.all_gather(w_output, 'col', axis=1, tiled=True)]
    unnamed x15 -> x0, waiting for transfers between devices: 124 us -> none
    unnamed x2 -> x0, blocking collectives: 116 us -> none
    select_n x26 -> x1, other arithmetic: 44 us -> 0.01 us  [per_device(): jnp.where(slots == inside, placed, jnp.zeros((), BF16)).reshape(2, HALF)]
    all_gather x2 -> x0, waiting for transfers between devices: 39.9 us -> none  [the longest x1 38.2 us: per_device(): lax.all_gather(w_outer, 'col', axis=1, tiled=True)]
  transfers between devices with their start and end apart: 30 -> 0, of which waited for: 14 -> 0; matrix products, arithmetic and copies ran while one was open for 24% -> 0% of each run, Pallas kernels for 0% -> 0%
where the time goes in v1:
time: 336 us; the launch traced here: 331 us
  Pallas kernels  255 us (76%)
  matrix products  32.6 us (10%)
  local copies, waits for them, and re-layouts  25.8 us (8%)
  other arithmetic  16 us (5%)
    pallas_call x1, Pallas kernels, backward_attention(): pl.pallas_call(functools.partial(kernel_c, size), out_shape=(shape((blk,...  134 us
    pallas_call x1, Pallas kernels, forward_attention(): pl.pallas_call(functools.partial(kernel_a, size), out_shape=(shape((2, ro...  121 us
    dot_general x18, matrix products, dot(): lax.dot_general(left, right, (contract, ((), ())), preferred_element_type...  32.6 us

profile of v1, /device:TPU:0, one launch (start us, length us, event | category | flops | bytes accessed | tf_op | source)
XLA Modules:
  0.0 330.5 jit_solution(5486685534730198710)
XLA Ops:
  0.7 1.2 dynamic_slice.20
  1.9 0.6 compare_convert_fusion
  2.6 0.7 pad_maximum_fusion.7
  3.3 4.8 %concatenate.26 = bf16[240]{0:T(256)(128)(2,1)S(1)} concatenate(bf16[24]{0:T(256)(128)(2,1)} %param.29, bf16[24]{0:T(256)(128)(2,1)} %param.31, bf16[24]{0:T(256)(128)(2,1)} %param.32, bf16[24]{0:T(256)(128)(2,1)} %param.33, bf16[24]{0:T(256)(128)(2,1)} %param.34, bf16[24]{0:T(256)(128)(2,1)} %param.35, bf16[96]{0:T(256)(128)(2,1)} %param.30), dimensions={0} | concatenate | bytes 960 | tf_op jit(solution)/shard_map/concatenate | solution.py:1107
  8.1 0.1 broadcast_in_dim.35
  8.4 0.6 pad.13.bq_in
  9.0 0.1 reshape.159
  9.1 1.5 pad_maximum_fusion.5.wq_in
  10.6 1.7 fusion.23.wr_in
  12.3 121.2 %forward_attention.1 = (bf16[2,512,384]{2,1,0:T(8,128)(2,1)}, bf16[16,48,1152]{2,1,0:T(8,128)(2,1)}, bf16[3,512,128]{2,1,0:T(8,128)(2,1)}, bf16[8,6,512,128]{3,2...) custom-call(s32[2]{0:T(128)} %lengths.1, ...), custom_call_target="tpu_custom_call" | custom-call | tf_op jit(solution)/shard_map/forward_attention/pallas_call | solution.py:469
  133.5 1.3 dynamic-slice_bitcast_fusion.1
  134.9 1.0 slice_convert_fusion
  135.9 0.3 reshape.171
  137.1 1.4 fusion.22
  138.6 1.7 fusion.45
  140.3 0.2 multiply_reduce_fusion.5
  140.5 0.2 fusion.20
  140.7 4.3 %multiply_convert_fusion = (bf16[256,1536]{1,0:T(8,128)(2,1)S(1)}, f32[256,1536]{1,0:T(8,128)}) fusion(f32[1536]{0:T(1024)S(1)} %add.164, bf16[256,768]{1,0:T(8,128)(2,1)S(1)} %fusion.20, bf16[2,768,3584]{2,1,0:T(8,128)(2,1)} %bitcast.127), kind=kOutput, calls=%fused_computation.21 | convolution fusion | flops 606339072 | bytes 5117952 | tf_op jit(solution)/shard_map/dot_general | solution.py:27
  145.0 2.0 multiply_convert_fusion.1
  147.0 0.9 copy-done.1
  147.9 0.8 fusion.3
  148.7 1.0 fusion.46
  149.7 0.2 multiply_reduce_fusion.4
  149.9 0.6 multiply_reduce_fusion
  150.8 0.8 pad_maximum_fusion.3.lay
  151.6 0.3 fusion.37
  151.9 0.4 copy-done.9
  152.3 3.7 %fusion.47 = (bf16[1536]{0:T(1024)(128)(2,1)S(1)}, bf16[256,1536]{1,0:T(8,128)(2,1)}) fusion(f32[256,1536]{1,0:T(8,128)S(1)} %copy-done.9, bf16[256,768]{1,0:T(8,128)(2,1)S(1)} %get-tuple-element.58, bf16[2,768,3584]{2,1,0:T(8,128)(2,1)} %bitcast.128), kind=kOutput, calls=%fused_computation.121 | convolution fusion | flops 608303616 | bytes 5114880 | tf_op jit(solution)/shard_map/dot_general | solution.py:27
  156.0 2.7 fusion.48
  158.7 3.7 %fusion.11 = f32[256,768]{1,0:T(8,128)} fusion(bf16[256,1536]{1,0:T(8,128)(2,1)S(1)} %get-tuple-element.106, bf16[2,768,3584]{2,1,0:T(8,128)(2,1)} %bitcast.130, f32[256]{0:T(256)S(1)} %broadcast_multiply_fusion.2, f32[256,768]{1,0:T(8,128)S(1)} %get-tuple-element.101, f32[256]{0:T(256)S(1)} %broadcast_multiply_fusion.4, ...), kind=kOutput, calls=%fused_computation.33 | convolution fusion | flops 606535680 | bytes 5120000 | tf_op jit(solution)/shard_map/dot_general | solution.py:27
  162.6 3.1 multiply_reduce_fusion.1
  165.7 0.3 fusion.39
  166.3 0.1 concatenate.30
  166.4 1.4 fusion.15
  167.9 1.4 fusion.16
  169.3 0.8 pad_maximum_fusion.2.dctx
  170.1 0.3 reshape.168
  170.5 0.8 constant_dynamic-slice_fusion.2.dres_own
  171.4 0.8 pad_maximum_fusion.4.dres_low
  172.2 0.4 convolution_convert_fusion.5
  172.5 0.4 convolution_convert_fusion.4
  172.9 0.3 copy.37
  173.3 2.2 convolution_convert_fusion.1
  175.5 0.8 convolution_convert_fusion.3
  176.3 0.3 copy-done.4
  176.6 0.8 convolution_convert_fusion
  177.5 0.5 maximum_bitcast_fusion.1
  177.9 0.6 copy-done.2
  178.6 0.8 convolution_convert_fusion.2
  179.4 0.5 maximum_bitcast_fusion
  179.9 5.1 %pad_maximum_fusion = bf16[2,768,3584]{2,1,0:T(8,128)(2,1)} fusion(bf16[1,768,3584]{2,1,0:T(8,128)(2,1)S(1)} %maximum_bitcast_fusion.1, bf16[1,768,3584]{2,1,0:T(8,128)(2,1)S(1)} %maximum_bitcast_fusion), kind=kLoop, calls=%fused_computation | loop fusion | flops 5505024 | bytes 22020096 | tf_op jit(solution)/shard_map/stack | solution.py:1055
  185.0 133.8 %backward_attention.1 = (f32[48,3584]{1,0:T(8,128)}, f32[48,1152]{1,0:T(8,128)}, f32[8,384]{1,0:T(8,128)}, f32[512,384]{1,0:T(8,128)}, bf16[512,384]{1,0:T(8,128)(2,1)}) custom-call(bf16[2,256,384]{2,1,0:T(8,128)(2,1)} %pad_maximum_fusion.2.dctx, bf16[3,512,128]{2,1,0:T(8,128)(2,1)} %get-tuple-element.37.qs, f32[8,6,1,512]{3,2,1,0:T(1,128)} %get-tuple-element.38.m_in, ...), custom_call_target="tpu_custom_call" | custom-call | tf_op jit(solution)/shard_map/backward_attention/pallas_call | solution.py:919
  318.8 0.8 fusion.43
  319.6 0.6 fusion.35
  320.2 0.6 fusion.34
  320.7 0.7 slice.171
  321.5 0.1 reshape.170
  321.6 0.6 slice.173
  322.2 0.6 fusion.44
  322.8 1.5 slice_bitcast_fusion.35
  324.3 1.9 slice_bitcast_fusion.28
  326.2 1.6 fusion.40
  327.9 1.8 copy.42
  329.6 0.9 copy.43
  (54 shorter events, 1.9 us)
Async XLA Ops:
  133.5 3.6 %copy-start = (bf16[2,256,384]{2,1,0:T(8,128)(2,1)S(1)}, bf16[2,256,384]{2,1,0:T(8,128)(2,1)}, u32[]{:S(2)}) copy-start(bf16[2,256,384]{2,1,0:T(8,128)(2,1)} %get-tuple-element.34) | copy-start | bytes 1179652
  138.6 6.4 %copy-start.8 = (bf16[32,48,3584]{2,1,0:T(8,128)(2,1)S(1)}, bf16[32,48,3584]{2,1,0:T(8,128)(2,1)}, u32[]{:S(2)}) copy-start(bf16[32,48,3584]{2,1,0:T(8,128)(2,1)} %get-tuple-element.35) | copy-start | bytes 33030148
  145.0 3.7 %copy-start.3 = (bf16[256,1536]{1,0:T(8,128)(2,1)}, bf16[256,1536]{1,0:T(8,128)(2,1)S(1)}, u32[]{:S(2)}) copy-start(bf16[256,1536]{1,0:T(8,128)(2,1)S(1)} %get-tuple-element.98) | copy-start | bytes 2359300
  147.0 0.9 copy-start.1
  150.7 1.6 copy-start.9
  152.3 3.7 %copy-start.10 = (f32[256,1536]{1,0:T(8,128)S(1)}, f32[256,1536]{1,0:T(8,128)}, u32[]{:S(2)}) copy-start(f32[256,1536]{1,0:T(8,128)} %get-tuple-element.97) | copy-start | bytes 4718596
  158.7 3.7 %copy-start.5 = (bf16[256,1536]{1,0:T(8,128)(2,1)}, bf16[256,1536]{1,0:T(8,128)(2,1)S(1)}, u32[]{:S(2)}) copy-start(bf16[256,1536]{1,0:T(8,128)(2,1)S(1)} %get-tuple-element.106) | copy-start | bytes 2359300
  173.2 2.3 copy-start.6
  175.5 1.1 copy-start.4
  177.5 1.1 copy-start.2
  318.8 10.9 %copy-start.7 = (f32[512,384]{1,0:T(8,128)S(1)}, f32[512,384]{1,0:T(8,128)}, u32[]{:S(2)}) copy-start(f32[512,384]{1,0:T(8,128)} %get-tuple-element.127) | copy-start | bytes 2359300

commit v2 on v1

v2 whole, which is shorter than its diff:
```python
import functools

import jax
import jax.numpy as jnp
from jax import lax
from jax.experimental import pallas as pl
from jax.experimental.pallas import tpu as pltpu
from jax.sharding import PartitionSpec as P

D = 768
HALF = 384
HEAD_DIM = 64
FF_HALF = 1536
PAIRS = 3
SPAN = 8
EPSILON = 1e-12
MASKED = -1e30
MESH = pl.DeviceIdType.MESH
F32 = jnp.float32
BF16 = jnp.bfloat16
FIRST = HALF + FF_HALF
REST = HALF + 2 * FF_HALF
QKV = 3 * HALF


def dot(left, right, contract):
    return lax.dot_general(left, right, (contract, ((), ())), preferred_element_type=F32)


NN = ((1,), (0,))
NT = ((1,), (1,))
TN = ((0,), (0,))


class Place:
    def __init__(self, size):
        self.size = size
        self.planes = size // 4
        self.r = lax.axis_index("row")
        col = lax.axis_index("col")
        self.base = lax.div(col, size) * size
        inner = lax.rem(col, size)
        self.slot = lax.div(col, SPAN)
        self.block = lax.rem(col, SPAN)
        self.z = lax.div(inner, 4)
        self.y = lax.rem(lax.div(inner, 2), 2)
        self.j = lax.rem(inner, 2)
        self.zl = lax.rem(self.z, 2)

    def plane(self, step):
        return lax.rem(self.z + step + self.planes, self.planes)

    def device(self, r, z, y, j):
        return (r, self.base + z * 4 + y * 2 + j)

    def to_z(self, step):
        return self.device(self.r, self.plane(step), self.y, self.j)

    def to_z_near(self):
        return self.device(self.r, self.z - self.zl + (1 - self.zl), self.y, self.j)

    def to_y(self):
        return self.device(self.r, self.z, 1 - self.y, self.j)

    def to_x(self):
        return self.device(1 - self.r, self.z, self.y, self.j)

    def to_core(self):
        return self.device(self.r, self.z, self.y, 1 - self.j)

    def col_block(self, z, y, j):
        return z * 4 + y * 2 + j

    def any_block(self, r, z, y, j):
        return r * self.size + z * 4 + y * 2 + j

    def near_block(self, dz, dy, j):
        return lax.rem(self.zl + dz, 2) * 4 + lax.rem(self.y + dy, 2) * 2 + j


def meet(place):
    barrier = pltpu.get_barrier_semaphore()
    peers = [place.to_z(step) for step in range(1, place.planes)]
    peers += [place.to_y(), place.to_x(), place.to_core()]
    for peer in peers:
        pl.semaphore_signal(barrier, inc=1, device_id=peer, device_id_type=MESH)
    pl.semaphore_wait(barrier, len(peers))


def send(src, dst, sems, index, peer):
    return pltpu.make_async_remote_copy(
        src_ref=src,
        dst_ref=dst,
        send_sem=sems[0].at[index],
        recv_sem=sems[1].at[index],
        device_id=peer,
        device_id_type=MESH,
    )


class Gather:
    def __init__(self, place, own, full, sems, with_rows):
        self.place, self.own, self.full, self.sems = place, own, full, sems
        self.rows = 2 if with_rows else 1
        self.with_rows = with_rows
        n = place.planes
        self.at_y = n - 1
        self.at_x = self.at_y + n
        self.at_c = self.at_x + (2 * n if with_rows else 0)
        self.total = self.at_c + 2 * n * self.rows

    def index(self, n, k, m, j):
        p = self.place
        z, y = p.plane(-k), lax.rem(p.y + m, 2)
        if self.with_rows:
            return p.any_block(lax.rem(p.r + n, 2), z, y, j)
        return p.col_block(z, y, j)

    def move(self, number, peer, n, k, m, j, local):
        where = self.index(n, k, m, j)
        src = self.own if local else self.full.at[where]
        return send(src, self.full.at[where], self.sems, number, peer)

    def z_sends(self):
        p = self.place
        for step in range(1, p.planes):
            self.move(step - 1, p.to_z(step), 0, 0, 0, p.j, True).start()

    def z_done(self, k):
        p = self.place
        self.move(k - 1, p.to_z(k), 0, k, 0, p.j, False).wait_recv()

    def y_send(self, k):
        p = self.place
        self.move(self.at_y + k, p.to_y(), 0, k, 0, p.j, k == 0).start()

    def y_done(self, k):
        p = self.place
        self.move(self.at_y + k, p.to_y(), 0, k, 1, p.j, False).wait_recv()

    def x_send(self, k, m):
        p = self.place
        self.move(self.at_x + 2 * k + m, p.to_x(), 0, k, m, p.j, k + m == 0).start()

    def x_done(self, k, m):
        p = self.place
        self.move(self.at_x + 2 * k + m, p.to_x(), 1, k, m, p.j, False).wait_recv()

    def c_number(self, n, k, m):
        return self.at_c + (2 * k + m) * self.rows + n

    def c_send(self, n, k, m):
        p = self.place
        number = self.c_number(n, k, m)
        self.move(number, p.to_core(), n, k, m, p.j, n + k + m == 0).start()

    def c_done(self, n, k, m):
        p = self.place
        self.move(self.c_number(n, k, m), p.to_core(), n, k, m, 1 - p.j, False).wait_recv()

    def all_sent(self):
        for number in range(self.total):
            send(self.own, self.own, self.sems, number, self.place.to_core()).wait_send()


def spread_rows(tiles, picks, per, width):
    blocks = tiles.shape[0]
    flat = tiles.reshape(blocks * 16, 128)
    total = len(picks) * blocks
    line = lax.broadcasted_iota(jnp.int32, (total, blocks * 16), 0)
    at = lax.broadcasted_iota(jnp.int32, (total, blocks * 16), 1)
    wanted = jnp.zeros((total, blocks * 16), F32)
    for spot, pick in enumerate(picks):
        hit = at == (line - spot * blocks) * 16 + pick
        inside = (line >= spot * blocks) & (line < (spot + 1) * blocks)
        wanted = jnp.where(hit & inside, 1.0, wanted)
    taken = dot(wanted.astype(BF16), flat, NN).astype(BF16)
    lane = lax.broadcasted_iota(jnp.int32, (128, width), 1).astype(F32)
    group = jnp.floor((lane + 0.5) * (1.0 / per))
    place = lax.broadcasted_iota(jnp.int32, (128, width), 0).astype(F32)
    copies = jnp.where(lane - group * per == place, 1.0, 0.0).astype(BF16)
    wide = dot(taken, copies, NN)
    first = lax.broadcasted_iota(jnp.int32, (blocks, width), 0) * per
    column = lax.broadcasted_iota(jnp.int32, (blocks, width), 1)
    mask = (column >= first) & (column < first + per)
    rows = []
    for spot in range(len(picks)):
        part = jnp.where(mask, wide[spot * blocks : (spot + 1) * blocks], 0.0)
        rows.append(jnp.sum(part, axis=0, keepdims=True))
    return rows


def gelu_both(argument):
    spread = 1.0 + lax.erf(argument * 0.7071067811865476)
    bell = jnp.exp(argument * argument * -0.5) * 0.3989422804014327
    return 0.5 * argument * spread, 0.5 * spread + argument * bell


def norm_forward(resid, gain, shift):
    center = resid - jnp.mean(resid, axis=1, keepdims=True)
    scale = lax.rsqrt(jnp.mean(center * center, axis=1, keepdims=True) + EPSILON)
    normal = center * scale
    return normal * gain + shift, normal, scale


def norm_backward(incoming, normal, scale, gain):
    scaled = incoming * gain
    first = jnp.mean(scaled, axis=1, keepdims=True)
    second = jnp.mean(scaled * normal, axis=1, keepdims=True)
    result = scale * (scaled - first - normal * second)
    sums = jnp.sum(incoming * normal, axis=0, keepdims=True)
    return result, sums, jnp.sum(incoming, axis=0, keepdims=True)


def kernel_a(
    size,
    lengths,
    hid,
    w_query,
    w_key,
    w_value,
    w_output,
    w_inner,
    w_outer,
    vec_in,
    cot,
    hid_out,
    wq_out,
    q_out,
    kv_out,
    p_out,
    m_out,
    lse_out,
    ctxt_out,
    g_out,
    final_out,
    low_out,
    own_out,
    d_out,
    small_out,
    hid_all,
    wq_own,
    wq_all,
    vec_all,
    one_own,
    one_all,
    two_all,
    kv,
    qs,
    qm,
    acc,
    high,
    low,
    pbuf,
    ctx_tp,
    ctx_in,
    cot_in,
    lay_out,
    lay_far,
    normed_ref,
    normal_ref,
    low_ref,
    slope_ref,
    act_ref,
    d_ref,
    one_send,
    one_recv,
    two_send,
    two_recv,
    wq_send,
    wq_recv,
    vec_send,
    vec_recv,
    kv_send,
    kv_recv,
    lone_send,
    lone_recv,
    local,
    p_sem,
):
    place = Place(size)
    rows = hid.shape[0]
    part = rows // 2
    n = place.planes
    r, y, j = place.r, place.y, place.j
    blk = w_query.shape[0]
    for at, source in enumerate((w_query, w_key, w_value)):
        wq_own[:, at * HALF : (at + 1) * HALF] = source[...]
    one_own[:, :HALF] = w_output[...]
    one_own[:, HALF:] = w_inner[...]
    with jax.named_scope("meet"):
        meet(place)

    single = (lone_send, lone_recv)
    own_rows = pl.ds(pl.multiple_of(r * part, part), part)
    other_rows = pl.ds(pl.multiple_of((1 - r) * part, part), part)
    to_hid = send(hid, hid_all.at[r], single, 0, place.to_x())
    to_hid.start()
    vec = Gather(place, vec_in, vec_all, (vec_send, vec_recv), True)
    wq = Gather(place, wq_own, wq_all, (wq_send, wq_recv), False)
    one = Gather(place, one_own, one_all, (one_send, one_recv), True)
    two = Gather(place, w_outer, two_all, (two_send, two_recv), True)
    for gather in (vec, wq):
        gather.z_sends()
        gather.y_send(0)
        gather.c_send(0, 0, 0)
    vec.x_send(0, 0)
    one.x_send(0, 0)
    one.y_send(0)
    two.x_send(0, 0)
    to_cot = send(cot.at[other_rows], cot_in.at[r], single, 1, place.to_x())
    to_cot.start()
    one.c_send(0, 0, 0)
    two.c_send(0, 0, 0)
    hid_all[r] = hid[...]
    mine = place.any_block(r, place.z, y, j)
    wq_all[place.col_block(place.z, y, j)] = wq_own[...]
    vec_all[mine] = vec_in[...]
    one_all[mine] = one_own[...]
    two_all[mine] = w_outer[...]
    cot_in[r] = cot[own_rows, :]
    for k in range(1, n):
        with jax.named_scope(f"qkv_plane_{k}"):
            for gather in (vec, wq):
                gather.z_done(k)
                gather.y_send(k)
                gather.c_send(0, k, 0)
            vec.x_send(k, 0)
    one.z_sends()
    two.y_send(0)
    for k in range(n):
        with jax.named_scope(f"qkv_side_{k}"):
            for gather in (vec, wq):
                gather.y_done(k)
                gather.c_send(0, k, 1)
            vec.x_send(k, 1)
    with jax.named_scope("qkv_core"):
        for k in range(n):
            for m in range(2):
                for gather in (vec, wq):
                    gather.c_done(0, k, m)
    with jax.named_scope("hidden"):
        send(hid, hid_all.at[1 - r], single, 0, place.to_x()).wait_recv()

    def rest_y(gather, k):
        gather.z_done(k)
        gather.y_send(k)
        gather.x_send(k, 0)
        gather.c_send(0, k, 0)

    def rest_x(gather, k):
        gather.y_done(k)
        gather.x_send(k, 1)
        gather.c_send(0, k, 1)

    def rest_c(gather, k, m):
        gather.x_done(k, m)
        gather.c_send(1, k, m)

    def rest_all(gather):
        for n_at in range(2):
            for k in range(n):
                for m in range(2):
                    if gather is not vec or n_at:
                        gather.c_done(n_at, k, m)

    hid_local = pltpu.make_async_copy(hid_all, hid_out, local.at[2])
    hid_local.start()
    wq_local = pltpu.make_async_copy(wq_all, wq_out, local.at[3])
    wq_local.start()

    own_tiles = vec_all[pl.ds(r * size, size)]
    b_query, b_value = spread_rows(own_tiles, (0, 1), HALF // size, HALF)
    own = place.near_block(0, 0, j)
    half = size // 2
    for which in (1, 2, 0):
        columns = slice(which * HALF, (which + 1) * HALF)
        total = dot(hid_all[0], wq_all[:half, :, columns].reshape(HALF, HALF), NN)
        total += dot(hid_all[1], wq_all[half:, :, columns].reshape(HALF, HALF), NN)
        if which == 0:
            total += b_query
        if which == 2:
            total += b_value
        total = total.astype(BF16)
        for p in range(PAIRS):
            piece = total[:, p * 128 : (p + 1) * 128]
            if which == 0:
                lane = lax.broadcasted_iota(jnp.int32, (rows, 128), 1)
                piece = piece * jnp.asarray(0.125, BF16)
                qs[p] = piece
                qm[2 * p] = jnp.where(lane < HEAD_DIM, piece, jnp.zeros_like(piece))
                qm[2 * p + 1] = jnp.where(lane >= HEAD_DIM, piece, jnp.zeros_like(piece))
            else:
                kv[own, (which - 1) * PAIRS + p] = piece
        if which == 1:
            with jax.named_scope("after_key"):
                rest_x(one, 0)
        if which == 2:
            with jax.named_scope("after_value"):
                rest_y(one, 1)
    acc[...] = jnp.zeros_like(acc)
    high[...] = jnp.full_like(high, MASKED)
    low[...] = jnp.zeros_like(low)

    n_one = place.device(r, place.z - place.zl + lax.rem(place.zl + 1 - j, 2), lax.rem(y + j, 2), j)
    n_two = place.device(r, place.z - place.zl + lax.rem(place.zl + j, 2), lax.rem(y + 1 - j, 2), j)
    kvs = (kv_send, kv_recv)

    def kv_block(i):
        pair, core = lax.div(i, 2), lax.rem(j + lax.rem(i, 2), 2)
        b0, b1 = lax.rem(pair, 2), lax.div(pair, 2)
        return place.near_block(b0 * (1 - core) + b1 * core, b0 * core + b1 * (1 - core), core)

    def kv_move(number, what, peer):
        where = kv_block(what)
        return send(kv.at[where], kv.at[where], kvs, number, peer)

    kv_move(1, 0, place.to_core()).start()
    kv_move(2, 0, n_one).start()
    q_local = pltpu.make_async_copy(qs, q_out, local.at[4])
    q_local.start()

    def arrived(number):
        kv_move(number, number, n_one).wait_recv()

    def second():
        kv_move(4, 0, n_two).start()

    def first_here():
        arrived(2)
        kv_move(3, 2, place.to_core()).start()

    def third():
        kv_move(6, 2, n_two).start()

    def second_here():
        arrived(4)
        kv_move(5, 4, place.to_core()).start()

    def third_here():
        arrived(6)
        kv_move(7, 6, place.to_core()).start()

    def vec_rows():
        for k in range(n):
            for m in range(2):
                rest_c(vec, k, m)

    def two_start():
        two.z_sends()

    events = {}

    def add(step, what, *inputs):
        events.setdefault(step, []).append(functools.partial(what, *inputs))

    add(1, vec_rows)
    add(2, rest_x, one, 1)
    add(2, two_start)
    add(3, arrived, 1)
    add(4, rest_y, one, 2)
    add(5, rest_y, one, 3)
    add(5, second)
    add(6, rest_x, two, 0)
    add(6, first_here)
    add(7, rest_x, one, 2)
    add(8, rest_x, one, 3)
    add(8, rest_c, one, 0, 0)
    add(8, third)
    add(9, rest_c, one, 1, 0)
    add(9, arrived, 3)
    add(10, rest_y, two, 1)
    add(12, second_here)
    add(13, rest_c, one, 0, 1)
    add(13, rest_c, one, 1, 1)
    add(13, rest_y, two, 2)
    add(14, rest_x, two, 1)
    add(15, arrived, 5)
    add(15, rest_y, two, 3)
    add(16, rest_c, one, 2, 0)
    add(17, rest_c, one, 3, 0)
    add(17, rest_x, two, 2)
    add(18, third_here)
    add(19, rest_c, one, 2, 1)
    add(20, rest_x, two, 3)
    add(21, arrived, 7)
    add(21, rest_c, one, 3, 1)
    add(22, rest_c, two, 0, 0)
    add(23, rest_c, two, 0, 1)

    length = lengths[place.slot]

    def p_copy(t, slot):
        i, p = lax.div(t, PAIRS), lax.rem(t, PAIRS)
        return pltpu.make_async_copy(
            pbuf.at[slot], p_out.at[kv_block(i), pl.ds(2 * p, 2)], p_sem.at[slot]
        )

    def kv_copy(i):
        where = kv_block(i)
        return pltpu.make_async_copy(kv.at[where], kv_out.at[where], local.at[8 + i])

    steps = SPAN * PAIRS

    def attend(t, carry):
        i, p = lax.div(t, PAIRS), lax.rem(t, PAIRS)
        for step, calls in sorted(events.items()):

            @pl.when(t == step)
            def _(calls=calls):
                for call in calls:
                    with jax.named_scope(f"at_{step}"):
                        call()

        @pl.when(p == 0)
        def _():
            kv_copy(i).start()

        slot = lax.rem(t, 2)

        @pl.when(t >= 2)
        def _():
            p_copy(t - 2, slot).wait()

        where = kv_block(i)
        place_of = lax.broadcasted_iota(jnp.int32, (rows, 128), 0) + where * rows
        bias = jnp.where(place_of < length, 0.0, MASKED)
        bias = jnp.concatenate([bias] * (rows // 128), axis=1)
        key = kv[where, p]
        value_t = kv[where, PAIRS + p].T
        for h in range(2):
            g = 2 * p + h
            scores = dot(key, qm[g], NT) + bias
            top = jnp.max(scores, axis=0, keepdims=True)
            weights = jnp.exp(scores - top)
            below = jnp.sum(weights, axis=0, keepdims=True)
            rounded = weights.astype(BF16)
            pbuf[slot, h] = rounded
            term = dot(value_t[h * HEAD_DIM : (h + 1) * HEAD_DIM], rounded, NN)
            old = high[g]
            new = jnp.maximum(old, top)
            keep_old, keep_new = jnp.exp(old - new), jnp.exp(top - new)
            high[g] = new
            low[g] = low[g] * keep_old + below * keep_new
            acc[g] = acc[g] * keep_old + term * keep_new
            m_out[where, g] = top
        p_copy(t, slot).start()
        return carry

    lax.fori_loop(0, steps, attend, jnp.int32(0))

    column = lax.broadcasted_iota(jnp.int32, (1, rows), 1) + place.block * rows
    keep = jnp.where(column < length, 1.0, 0.0)
    for p in range(PAIRS):
        parts = []
        for h in range(2):
            g = 2 * p + h
            lse_out[g] = high[g] + jnp.log(low[g])
            parts.append(acc[g] / low[g])
        both = jnp.concatenate(parts, axis=0)
        ctxt_out[p] = both
        ctx_tp[:, p * 128 : (p + 1) * 128] = (both * keep).T.astype(BF16)
    for t in (steps - 2, steps - 1):
        p_copy(jnp.int32(t), t % 2).wait()
    to_ctx = send(ctx_tp.at[other_rows], ctx_in.at[r], single, 2, place.to_x())
    to_ctx.start()
    ctx_in[r] = ctx_tp[own_rows, :]
    with jax.named_scope("one_all"):
        rest_all(vec)
        rest_all(one)
    six = spread_rows(vec_all[...], (2, 3, 4, 5, 6, 7), HALF // size, D)
    b_output, b_outer, gain_one, shift_one, gain_two, shift_two = six
    (b_inner,) = spread_rows(vec_all[...], (8,), FF_HALF // size, 2 * FF_HALF)
    hidden = jnp.concatenate([hid_all[0, own_rows, :], hid_all[1, own_rows, :]], axis=1)
    with jax.named_scope("context"):
        send(ctx_tp.at[other_rows], ctx_in.at[1 - r], single, 2, place.to_x()).wait_recv()

    def weight(ref, h, columns):
        block = ref[h * size : (h + 1) * size, :, columns]
        return block.reshape(D, block.shape[2])

    out_cols, in_cols, all_cols = slice(0, HALF), slice(HALF, FIRST), slice(0, FF_HALF)
    with jax.named_scope("middle_one"):
        attn = dot(ctx_in[0], weight(one_all, 0, out_cols), NT)
        attn += dot(ctx_in[1], weight(one_all, 1, out_cols), NT) + b_output
        normed, normal, scale_one = norm_forward(hidden.astype(F32) + attn, gain_one, shift_one)
        normed_ref[...] = normed
        normal_ref[...] = normal
        low_ref[...] = normed.astype(BF16)
    with jax.named_scope("two_late"):
        rest_c(two, 1, 0)
        rest_c(two, 1, 1)
    for h in range(2):
        with jax.named_scope(f"inner_{h}"):
            span = slice(h * FF_HALF, (h + 1) * FF_HALF)
            inner = dot(low_ref[...], weight(one_all, h, in_cols), NN) + b_inner[:, span]
            value, slope = gelu_both(inner)
            act_ref[:, span] = value.astype(BF16)
            slope_ref[:, span] = slope
    with jax.named_scope("two_all"):
        for k in range(2, n):
            for m in range(2):
                rest_c(two, k, m)
        rest_all(two)
    with jax.named_scope("outer"):
        outer = dot(act_ref[:, :FF_HALF], weight(two_all, 0, all_cols), NT)
        outer += dot(act_ref[:, FF_HALF:], weight(two_all, 1, all_cols), NT) + b_outer
        result, normal_two, scale_two = norm_forward(normed_ref[...] + outer, gain_two, shift_two)
        lay_out[0] = result[:, :HALF].astype(BF16)
        lay_out[1] = result[:, HALF:].astype(BF16)
    to_lay = send(lay_out.at[1 - r], lay_far.at[r], single, 3, place.to_x())
    to_lay.start()
    spot = lax.broadcasted_iota(jnp.int32, (part, 1), 0) + place.block * rows + r * part
    keep = jnp.where(spot < length, 1.0, 0.0)
    with jax.named_scope("cotangent"):
        send(cot.at[other_rows], cot_in.at[1 - r], single, 1, place.to_x()).wait_recv()
    with jax.named_scope("norm_two"):
        seed = jnp.concatenate([cot_in[0], cot_in[1]], axis=1).astype(F32) * keep
        d_two, g_gain_two, g_shift_two = norm_backward(seed, normal_two, scale_two, gain_two)
        d_outer = d_two.astype(BF16)
        small_out[4:5] = g_gain_two
        small_out[5:6] = g_shift_two
        small_out[1:2] = jnp.sum(d_outer.astype(F32), axis=0, keepdims=True)
    d_normed = d_two
    d_outer_t = d_outer.T
    for h in range(2):
        with jax.named_scope(f"d_inner_{h}"):
            span = slice(h * FF_HALF, (h + 1) * FF_HALF)
            d_inner = dot(d_outer, weight(two_all, h, all_cols), NN) * slope_ref[:, span]
            d_inner = d_inner.astype(BF16)
            d_ref[:, span] = d_inner
            sums = jnp.sum(d_inner.astype(F32), axis=0, keepdims=True)
            small_out[6 + 2 * h : 7 + 2 * h] = sums[:, :D]
            small_out[7 + 2 * h : 8 + 2 * h] = sums[:, D:]
            d_normed += dot(d_inner, weight(one_all, h, in_cols), NT)
    with jax.named_scope("all_sent"):
        for gather in (vec, wq, one, two):
            gather.all_sent()
    own_col = pl.ds(pl.multiple_of(r * HALF, HALF), HALF)

    def give(number, ref, h, columns, target):
        return pltpu.make_async_copy(
            ref.at[pl.ds(h * size, size), :, columns],
            g_out.at[pl.ds(h * size, size), :, target],
            local.at[16 + number],
        )

    gives = []
    for h in range(2):
        with jax.named_scope(f"g_outer_{h}"):
            span = slice(h * FF_HALF, (h + 1) * FF_HALF)
            term = dot(d_outer_t, act_ref[:, span], NN).astype(BF16)
            two_all[h * size : (h + 1) * size] = term.reshape(size, blk, FF_HALF)
            copy = give(h, two_all, h, pl.ds(0, FF_HALF), pl.ds(FIRST, FF_HALF))
            copy.start()
            gives.append(copy)
    with jax.named_scope("norm_one"):
        d_one, g_gain_one, g_shift_one = norm_backward(d_normed, normal_ref[...], scale_one, gain_one)
        d_attn = d_one.astype(BF16)
        small_out[2:3] = g_gain_one
        small_out[3:4] = g_shift_one
        small_out[0:1] = jnp.sum(d_attn.astype(F32), axis=0, keepdims=True)
        small_out[10:16] = jnp.zeros((6, D), F32)
        for h in range(2):
            low_out[h] = d_attn[:, h * HALF : (h + 1) * HALF]
        normed_ref[...] = d_one
        own_out[...] = normed_ref[:, own_col]
    with jax.named_scope("d_context"):
        for h in range(2):
            d_context = dot(d_attn, weight(one_all, h, out_cols), NN) * keep
            d_out[h] = d_context.astype(BF16)
    low_t = low_ref[...].T
    d_attn_t = d_attn.T
    for h in range(2):
        with jax.named_scope(f"g_inner_{h}"):
            span = slice(h * FF_HALF, (h + 1) * FF_HALF)
            term = dot(low_t, d_ref[:, span], NN).astype(BF16)
            one_all[h * size : (h + 1) * size, :, HALF:] = term.reshape(size, blk, FF_HALF)
            term = dot(d_attn_t, ctx_in[h], NN).astype(BF16)
            one_all[h * size : (h + 1) * size, :, :HALF] = term.reshape(size, blk, HALF)
            copy = give(2 + h, one_all, h, pl.ds(0, FIRST), pl.ds(0, FIRST))
            copy.start()
            gives.append(copy)
    for number in range(1, 8):
        kv_move(number, 0, n_one).wait_send()
    to_lay.wait_send()
    send(lay_far.at[r], lay_far.at[1 - r], single, 3, place.to_x()).wait_recv()
    final_out[own_rows, :] = lay_out[r]
    final_out[other_rows, :] = lay_far[1 - r]
    for number in range(3):
        block = hid if number == 0 else ctx_in.at[0]
        send(block, block, single, number, place.to_x()).wait_send()
    for copy in [hid_local, wq_local, q_local] + gives:
        copy.wait()
    for i in range(SPAN):
        kv_copy(jnp.int32(i)).wait()


def forward_attention(size, lengths, hid, qkv_weights, rest_weights, vec, cot):
    rows = hid.shape[0]
    part = rows // 2
    blk = qkv_weights[0].shape[0]
    n = size // 4
    any_space = pl.BlockSpec(memory_space=pl.ANY)
    vmem = pl.BlockSpec(memory_space=pltpu.VMEM)
    shape = jax.ShapeDtypeStruct
    n_col, n_all = (n - 1) + n + 2 * n, (n - 1) + n + 2 * n + 4 * n
    dma = pltpu.SemaphoreType.DMA
    scratch = pltpu.VMEM
    return pl.pallas_call(
        functools.partial(kernel_a, size),
        out_shape=(
            shape((2, rows, HALF), BF16),
            shape((size, blk, QKV), BF16),
            shape((PAIRS, rows, 128), BF16),
            shape((SPAN, 2 * PAIRS, rows, 128), BF16),
            shape((SPAN, 2 * PAIRS, rows, rows), BF16),
            shape((SPAN, 2 * PAIRS, 1, rows), F32),
            shape((2 * PAIRS, 1, rows), F32),
            shape((PAIRS, 128, rows), F32),
            shape((2 * size, blk, REST), BF16),
            shape((rows, HALF), BF16),
            shape((2, part, HALF), BF16),
            shape((part, HALF), F32),
            shape((2, part, HALF), BF16),
            shape((16, D), F32),
        ),
        in_specs=[pl.BlockSpec(memory_space=pltpu.SMEM)] + [vmem] * 9,
        out_specs=[any_space] * 5 + [vmem] * 3 + [any_space] + [vmem] * 5,
        scratch_shapes=[
            scratch((2, rows, HALF), BF16),
            scratch((blk, QKV), BF16),
            scratch((size, blk, QKV), BF16),
            scratch((2 * size, 16, 128), BF16),
            scratch((blk, FIRST), BF16),
            scratch((2 * size, blk, FIRST), BF16),
            scratch((2 * size, blk, FF_HALF), BF16),
            scratch((SPAN, 2 * PAIRS, rows, 128), BF16),
            scratch((PAIRS, rows, 128), BF16),
            scratch((2 * PAIRS, rows, 128), BF16),
            scratch((2 * PAIRS, HEAD_DIM, rows), F32),
            scratch((2 * PAIRS, 1, rows), F32),
            scratch((2 * PAIRS, 1, rows), F32),
            scratch((2, 2, rows, rows), BF16),
            scratch((rows, HALF), BF16),
            scratch((2, part, HALF), BF16),
            scratch((2, part, HALF), BF16),
            scratch((2, part, HALF), BF16),
            scratch((2, part, HALF), BF16),
            scratch((part, D), F32),
            scratch((part, D), F32),
            scratch((part, D), BF16),
            scratch((part, 2 * FF_HALF), F32),
            scratch((part, 2 * FF_HALF), BF16),
            scratch((part, 2 * FF_HALF), BF16),
            dma((n_all,)),
            dma((n_all,)),
            dma((n_all,)),
            dma((n_all,)),
            dma((n_col,)),
            dma((n_col,)),
            dma((n_all,)),
            dma((n_all,)),
            dma((8,)),
            dma((8,)),
            dma((4,)),
            dma((4,)),
            dma((20,)),
            dma((2,)),
        ],
        compiler_params=pltpu.CompilerParams(
            collective_id=0, has_side_effects=True, vmem_limit_bytes=62 * 2**20
        ),
        name="forward_attention",
    )(lengths, hid, *qkv_weights, *rest_weights, vec, cot)


def kernel_c(
    size,
    dctx,
    qs,
    m_in,
    lse_in,
    ctxt,
    hid_all,
    wq_all,
    dres_low,
    dres_own,
    small_in,
    kv_in,
    p_in,
    g_in,
    query_out,
    key_out,
    value_out,
    wo_out,
    wi_out,
    wu_out,
    small_out,
    bias_out,
    grad_out,
    d_ctx,
    dtot,
    delta,
    qm,
    acc,
    kv,
    pbuf,
    big,
    cb,
    rb,
    st,
    b1,
    b2,
    b3,
    b4,
    d_all,
    gq,
    q1,
    q2,
    q3,
    near,
    bias_own,
    bias_got,
    vec_sum,
    vec_got,
    one_send,
    one_recv,
    kv_send,
    kv_recv,
    g_send,
    g_recv,
    q_send,
    q_recv,
    s_send,
    s_recv,
    v_send,
    v_recv,
    load,
    p_sem,
):
    place = Place(size)
    rows = qs.shape[1]
    part = rows // 2
    n = place.planes
    r, y, j = place.r, place.y, place.j
    with jax.named_scope("meet"):
        meet(place)
    single = (one_send, one_recv)
    gs = (g_send, g_recv)
    ks = (kv_send, kv_recv)
    at_x, at_y, at_z = 4 * n, 6 * n, 7 * n

    own_rows = pl.ds(pl.multiple_of(r * part, part), part)
    other_rows = pl.ds(pl.multiple_of((1 - r) * part, part), part)
    send(dctx.at[1 - r], d_ctx.at[own_rows], single, 0, place.to_x()).start()
    send(small_in, vec_got.at[0], (v_send, v_recv), 0, place.to_x()).start()

    def g_block(index, core):
        n_at, m = lax.div(index, 2 * n), lax.rem(index, 2)
        k = lax.rem(lax.div(lax.rem(index, 2 * n), 2) + 1, n)
        return place.any_block(
            lax.rem(r + 1 + n_at, 2), place.plane(k), lax.rem(y + 1 + m, 2), core
        )

    def c_move(index):
        return send(g_in.at[g_block(index, 1 - j)], b1.at[index], gs, index, place.to_core())

    def g_load(index):
        return pltpu.make_async_copy(g_in.at[g_block(index, j)], st.at[index], load.at[8 + index])

    def loop(count, body):
        def step(index, carry):
            body(index)
            return carry

        lax.fori_loop(0, count, step, jnp.int32(0))

    loop(4 * n, lambda index: c_move(index).start())
    loop(4 * n, lambda index: g_load(index).start())

    def b_block(i):
        pair, core = lax.div(i, 2), lax.rem(j + 1 + lax.rem(i, 2), 2)
        return place.near_block(1 - lax.div(pair, 2), 1 - lax.rem(pair, 2), core)

    def kv_load(i):
        return pltpu.make_async_copy(kv_in.at[b_block(i)], kv.at[i], load.at[i])

    def p_load(t, slot):
        i, p = lax.div(t, PAIRS), lax.rem(t, PAIRS)
        return pltpu.make_async_copy(
            p_in.at[b_block(i), pl.ds(2 * p, 2)], pbuf.at[slot], p_sem.at[slot]
        )

    p_load(jnp.int32(0), 0).start()
    loop(SPAN, lambda i: kv_load(i).start())

    lane = lax.broadcasted_iota(jnp.int32, (rows, 128), 1)
    for p in range(PAIRS):
        piece = qs[p]
        qm[2 * p] = jnp.where(lane < HEAD_DIM, piece, jnp.zeros_like(piece))
        qm[2 * p + 1] = jnp.where(lane >= HEAD_DIM, piece, jnp.zeros_like(piece))
    acc[...] = jnp.zeros_like(acc)
    d_ctx[own_rows, :] = dctx[r]
    def core_send(pair):
        return send(big.at[2 * pair], cb.at[pair], ks, pair, place.to_core())

    def core_add(pair):
        core_send(pair).wait_recv()
        for piece in range(2 * PAIRS):
            total = big[2 * pair + 1, piece].astype(F32) + cb[pair, piece].astype(F32)
            big[2 * pair + 1, piece] = total.astype(BF16)

    keys, values = pl.ds(0, PAIRS), pl.ds(PAIRS, PAIRS)

    def hop(number):
        pair, part_of, along_z = (
            (0, keys, False),
            (0, values, True),
            (1, keys, True),
            (1, values, True),
            (2, values, False),
            (2, keys, False),
        )[number]
        peer = place.to_z_near() if along_z else place.to_y()
        return send(big.at[2 * pair + 1, part_of], rb.at[number], ks, 4 + number, peer)

    def hop_add(number, pair, start):
        hop(number).wait_recv()
        for piece in range(PAIRS):
            total = big[2 * pair + 1, start + piece].astype(F32) + rb[number, piece].astype(F32)
            big[2 * pair + 1, start + piece] = total.astype(BF16)

    def fold(target, source, at):
        total = target[at].astype(F32) + source.astype(F32)
        target[at] = total.astype(BF16)

    def g_core_add(index):
        c_move(index).wait_recv()
        g_load(index).wait()
        fold(st, b1[index], index)

    def g_x_send(index):
        return send(st.at[index], b2.at[index], gs, at_x + index, place.to_x())

    def g_x_add(index):
        g_x_send(index).wait_recv()
        fold(st, b2[index], 2 * n + index)

    def kept(m, k):
        return 2 * n + 2 * ((k + n - 1) % n) + m

    def g_y_send(k):
        return send(st.at[kept(0, k)], b3.at[k], gs, at_y + k, place.to_y())

    def g_y_add(k):
        g_y_send(k).wait_recv()
        fold(st, b3[k], kept(1, k))

    def g_z_send(k):
        return send(st.at[kept(1, k)], b4.at[k - 1], gs, at_z + k - 1, place.to_z(k))

    with jax.named_scope("first_adds"):
        for at in range(2):
            g_core_add(at)
            g_x_send(at).start()
    with jax.named_scope("context_row"):
        send(dctx.at[1 - r], d_ctx.at[other_rows], single, 0, place.to_x()).wait_recv()
    upper = lax.broadcasted_iota(jnp.int32, (128, rows), 0) < HEAD_DIM
    for p in range(PAIRS):
        turned = d_ctx[:, p * 128 : (p + 1) * 128].astype(F32).T
        product = turned * ctxt[p]
        delta[2 * p] = jnp.sum(product[:HEAD_DIM], axis=0, keepdims=True)
        delta[2 * p + 1] = jnp.sum(product[HEAD_DIM:], axis=0, keepdims=True)
        dtot[2 * p] = jnp.where(upper, turned, 0.0)
        dtot[2 * p + 1] = jnp.where(upper, 0.0, turned)

    vz = (v_send, v_recv)

    def vector(number):
        level = min(number, 3)
        step = max(number - 2, 1)
        peer = (place.to_x(), place.to_core(), place.to_y(), place.to_z(step))[level]
        source = small_in if level == 0 else vec_sum.at[level - 1]
        return send(source, vec_got.at[number], vz, number, peer)

    def vector_add(level):
        vector(level).wait_recv()
        before = small_in[...] if level == 0 else vec_sum[level - 1]
        vec_sum[level] = before + vec_got[level]

    events = {}

    def add(step, what, *inputs):
        events.setdefault(step, []).append(functools.partial(what, *inputs))

    def start(what, number):
        what(number).start()

    for at in range(2 * n):
        if at > 1:
            add(at - 2, g_core_add, at)
            add(at - 1, start, g_x_send, at)
        add(6 + at, g_core_add, 2 * n + at)
    arrive = [8, 13, 18, 23]
    for at, step in enumerate(arrive):
        add(step, g_x_add, at)
    for pair in range(4):
        add(6 * pair + 3, start, core_send, pair)
        if pair < 3:
            add(6 * pair + 6, core_add, pair)
    for level in range(3):
        add(2 * level, vector_add, level)
        add(2 * level + 1, start, vector, level + 1)
    for step in range(2, n):
        add(5, start, vector, 2 + step)
    add(7, start, hop, 0)
    add(7, start, hop, 1)
    add(13, start, hop, 3)
    add(17, hop_add, 0, 1, 0)
    add(18, start, hop, 2)
    add(19, start, hop, 5)
    add(20, hop_add, 1, 2, PAIRS)
    add(21, start, hop, 4)
    add(9, start, g_y_send, 1)
    add(18, g_y_add, 1)
    add(19, start, g_z_send, 1)
    add(22, start, g_y_send, 2)

    steps = SPAN * PAIRS

    def back(t, carry):
        i, p = lax.div(t, PAIRS), lax.rem(t, PAIRS)
        for step, calls in sorted(events.items()):

            @pl.when(t == step)
            def _(calls=calls):
                with jax.named_scope(f"step_{step}"):
                    for call in calls:
                        call()

        slot = lax.rem(t, 2)

        @pl.when(t + 1 < steps)
        def _():
            p_load(t + 1, 1 - slot).start()

        @pl.when(p == 0)
        def _():
            kv_load(i).wait()

        p_load(t, slot).wait()
        where = b_block(i)
        key = kv[i, p]
        value = kv[i, PAIRS + p]
        key_t = key.T
        d_key = d_value = None
        for h in range(2):
            g = 2 * p + h
            factor = jnp.exp(m_in[where, g] - lse_in[g])
            d_rows = (dtot[g] * factor).astype(BF16)
            weights = pbuf[slot, h]
            d_probs = dot(value, d_rows, NN)
            d_scores = (weights.astype(F32) * (d_probs - delta[g] * factor)).astype(BF16)
            value_term = dot(weights, d_rows, NT)
            key_term = dot(d_scores, qm[g], NN)
            acc[g] += dot(key_t[h * HEAD_DIM : (h + 1) * HEAD_DIM], d_scores, NN)
            d_key = key_term if d_key is None else d_key + key_term
            d_value = value_term if d_value is None else d_value + value_term
        big[i, p] = d_key.astype(BF16)
        big[i, PAIRS + p] = d_value.astype(BF16)
        return carry

    lax.fori_loop(0, steps, back, jnp.int32(0))

    for p in range(PAIRS):
        both = jnp.concatenate([acc[2 * p], acc[2 * p + 1]], axis=0)
        d_all[:, p * 128 : (p + 1) * 128] = (both.T * 0.125).astype(BF16)
    with jax.named_scope("g_x_4"):
        g_x_add(4)
        g_x_add(5)
    g_y_send(3).start()
    with jax.named_scope("last_hops"):
        core_send(3).wait_recv()
        for number in (2, 3, 5, 4):
            hop(number).wait_recv()
    for piece in range(PAIRS):
        at = HALF + piece * 128
        total = big[7, piece].astype(F32) + cb[3, piece].astype(F32)
        total += rb[2, piece].astype(F32) + rb[5, piece].astype(F32)
        d_all[:, at : at + 128] = total.astype(BF16)
        at = 2 * HALF + piece * 128
        total = big[7, PAIRS + piece].astype(F32) + cb[3, PAIRS + piece].astype(F32)
        total += rb[3, piece].astype(F32) + rb[4, piece].astype(F32)
        d_all[:, at : at + 128] = total.astype(BF16)

    half = size // 2
    blk = wq_all.shape[1]

    def input_term(which):
        weight = wq_all[pl.ds(which * half, half)].reshape(HALF, QKV)
        return dot(d_all[...], weight, NT)

    with jax.named_scope("input_term"):
        grad_out[...] = input_term(1 - r)
        grad_out[own_rows, :] = grad_out[own_rows, :] + dres_low[1 - r].astype(F32)
        near[0] = grad_out[...].astype(BF16)
    with jax.named_scope("g_x_6"):
        g_x_add(6)
    with jax.named_scope("g_y_2"):
        g_y_add(2)
    to_near = send(near.at[0], near.at[1], single, 3, place.to_x())
    to_near.start()
    g_z_send(2).start()
    with jax.named_scope("qkv_grad"):
        for which in range(2):
            term = dot(hid_all[which], d_all[...], TN).astype(BF16)
            gq[which * half : (which + 1) * half] = term.reshape(half, blk, QKV)
    g_y_send(0).start()
    qz = (q_send, q_recv)

    def q_block(index, core):
        m, k = lax.div(index, n), lax.rem(index, n)
        return place.col_block(place.plane(k), lax.rem(y + 1 + m, 2), core)

    def q_core(index):
        return send(gq.at[q_block(index, 1 - j)], q1.at[index], qz, index, place.to_core())

    def q_side(k):
        return send(gq.at[q_block(k, j)], q2.at[k], qz, 2 * n + k, place.to_y())

    def q_plane(k):
        return send(gq.at[q_block(n + k, j)], q3.at[k - 1], qz, 3 * n + k - 1, place.to_z(k))

    bias_own[0, 0:1] = jnp.sum(d_all[:, :HALF].astype(F32), axis=0, keepdims=True)
    bias_own[0, 1:2] = jnp.sum(d_all[:, 2 * HALF :].astype(F32), axis=0, keepdims=True)
    bias_own[0, 2:8] = jnp.zeros((6, HALF), F32)
    sz = (s_send, s_recv)

    def small(number):
        level = min(number, 2)
        peer = (place.to_core(), place.to_y(), place.to_z(max(number - 1, 1)))[level]
        return send(bias_own.at[level], bias_got.at[number], sz, number, peer)

    loop(2 * n, lambda index: q_core(index).start())
    with jax.named_scope("input_own"):
        grad_out[...] = input_term(r)
        grad_out[own_rows, :] = grad_out[own_rows, :] + dres_own[...]
    small(0).start()

    def q_core_add(index):
        q_core(index).wait_recv()
        fold(gq, q1[index], q_block(index, j))

    with jax.named_scope("q_core_a"):
        loop(n, q_core_add)
        small(0).wait_recv()
    bias_own[1] = bias_own[0] + bias_got[0]
    loop(n, lambda k: q_side(k).start())
    with jax.named_scope("q_core_b"):
        loop(n, lambda k: q_core_add(n + k))
    small(1).start()
    with jax.named_scope("g_x_7"):
        g_x_add(7)
    with jax.named_scope("g_y_3"):
        g_y_add(3)
        g_z_send(3).start()
    with jax.named_scope("g_y_0"):
        g_y_add(0)
    with jax.named_scope("q_side"):
        for k in range(n):
            q_side(k).wait_recv()
            fold(gq, q2[k], q_block(n + k, j))
            if k:
                q_plane(k).start()
        small(1).wait_recv()
    bias_own[2] = bias_own[1] + bias_got[1]
    with jax.named_scope("near_wait"):
        to_near.wait_recv()
    grad_out[...] = grad_out[...] + near[1].astype(F32)
    for step in range(1, n):
        small(1 + step).start()
    total = vec_sum[2]
    for step in range(1, n):
        vector(2 + step).wait_recv()
        total = total + vec_got[2 + step]
    small_out[...] = total
    total = st[kept(1, 0)].astype(F32)
    with jax.named_scope("g_plane"):
        for k in range(1, n):
            g_z_send(k).wait_recv()
            total = total + b4[k - 1].astype(F32)
        wo_out[...] = total[:, :HALF]
        wi_out[...] = total[:, HALF:FIRST]
        wu_out[...] = total[:, FIRST:]
    total = gq[q_block(n, j)].astype(F32)
    with jax.named_scope("q_plane"):
        for k in range(1, n):
            q_plane(k).wait_recv()
            total = total + q3[k - 1].astype(F32)
        query_out[...] = total[:, :HALF]
        key_out[...] = total[:, HALF : 2 * HALF]
        value_out[...] = total[:, 2 * HALF :]
        total = bias_own[2]
        for step in range(1, n):
            small(1 + step).wait_recv()
            total = total + bias_got[1 + step]
        bias_out[...] = total

    loop(4 * n, lambda index: c_move(index).wait_send())
    loop(2 * n, lambda index: g_x_send(index).wait_send())
    for k in range(n):
        g_y_send(k).wait_send()
    for k in range(1, n):
        g_z_send(k).wait_send()
        q_plane(k).wait_send()
        small(1 + k).wait_send()
    small(0).wait_send()
    for number in range(n + 2):
        vector(number).wait_send()
    small(1).wait_send()
    loop(2 * n, lambda index: q_core(index).wait_send())
    loop(n, lambda k: q_side(k).wait_send())
    for pair in range(4):
        core_send(pair).wait_send()
    for number in range(6):
        hop(number).wait_send()
    to_near.wait_send()
    send(dctx.at[1 - r], d_ctx.at[own_rows], single, 0, place.to_x()).wait_send()


def backward_attention(
    size, dctx, qs, m_in, lse_in, ctxt, hid_all, wq_all, dres_low, dres_own, small_in, kv_in, p_in, g_in
):
    rows = qs.shape[1]
    part = rows // 2
    blk = wq_all.shape[1]
    n = size // 4
    any_space = pl.BlockSpec(memory_space=pl.ANY)
    vmem = pl.BlockSpec(memory_space=pltpu.VMEM)
    shape = jax.ShapeDtypeStruct
    dma = pltpu.SemaphoreType.DMA
    scratch = pltpu.VMEM
    g_count, q_count = 4 * n + 2 * n + n + n - 1, 2 * n + n + n - 1
    return pl.pallas_call(
        functools.partial(kernel_c, size),
        out_shape=(
            shape((blk, HALF), F32),
            shape((blk, HALF), F32),
            shape((blk, HALF), F32),
            shape((blk, HALF), F32),
            shape((blk, FF_HALF), F32),
            shape((blk, FF_HALF), F32),
            shape((16, D), F32),
            shape((8, HALF), F32),
            shape((rows, HALF), F32),
        ),
        in_specs=[vmem] * 10 + [any_space] * 3,
        out_specs=[vmem] * 9,
        scratch_shapes=[
            scratch((rows, HALF), BF16),
            scratch((2 * PAIRS, 128, rows), F32),
            scratch((2 * PAIRS, 1, rows), F32),
            scratch((2 * PAIRS, rows, 128), BF16),
            scratch((2 * PAIRS, HEAD_DIM, rows), F32),
            scratch((SPAN, 2 * PAIRS, rows, 128), BF16),
            scratch((2, 2, rows, rows), BF16),
            scratch((SPAN, 2 * PAIRS, rows, 128), BF16),
            scratch((4, 2 * PAIRS, rows, 128), BF16),
            scratch((6, PAIRS, rows, 128), BF16),
            scratch((4 * n, blk, REST), BF16),
            scratch((4 * n, blk, REST), BF16),
            scratch((2 * n, blk, REST), BF16),
            scratch((n, blk, REST), BF16),
            scratch((n - 1, blk, REST), BF16),
            scratch((rows, QKV), BF16),
            scratch((size, blk, QKV), BF16),
            scratch((2 * n, blk, QKV), BF16),
            scratch((n, blk, QKV), BF16),
            scratch((n - 1, blk, QKV), BF16),
            scratch((2, rows, HALF), BF16),
            scratch((3, 8, HALF), F32),
            scratch((n + 1, 8, HALF), F32),
            scratch((3, 16, D), F32),
            scratch((n + 2, 16, D), F32),
            dma((4,)),
            dma((4,)),
            dma((10,)),
            dma((10,)),
            dma((g_count,)),
            dma((g_count,)),
            dma((q_count,)),
            dma((q_count,)),
            dma((n + 1,)),
            dma((n + 1,)),
            dma((n + 2,)),
            dma((n + 2,)),
            dma((9 + 4 * n,)),
            dma((2,)),
        ],
        compiler_params=pltpu.CompilerParams(
            collective_id=1, has_side_effects=True, vmem_limit_bytes=63 * 2**20
        ),
        name="backward_attention",
    )(dctx, qs, m_in, lse_in, ctxt, hid_all, wq_all, dres_low, dres_own, small_in, kv_in, p_in, g_in)


def kernel_d(size, per, big, small, bias, *refs):
    sources, targets, tile = refs[: big + 2], refs[big + 2 : -1], refs[-1]
    for source, target in zip(sources, targets):
        target[...] = source[...]
    row = lax.axis_index("row")
    inside = lax.rem(lax.axis_index("col"), size)
    start = row * HALF + inside * per
    lines = small[...]
    tile[0:6] = pltpu.roll(lines, D - start, 1)[0:6, :128]
    spot = inside * 4 * per
    hidden = pltpu.roll(lines, D - lax.rem(spot, D), 1)[:, :128]
    wanted = 6 + 2 * row + lax.div(spot, D)
    line = lax.broadcasted_iota(jnp.int32, hidden.shape, 0)
    tile[6:7] = jnp.sum(jnp.where(line == wanted, hidden, 0.0), axis=0, keepdims=True)
    tile[7:9] = pltpu.roll(bias[...], HALF - inside * per, 1)[0:2, :128]
    tile[9:16] = jnp.zeros((7, 128), F32)


def finish(size, small, bias, arrays):
    vmem = pl.BlockSpec(memory_space=pltpu.VMEM)
    shapes = [jax.ShapeDtypeStruct(a.shape, a.dtype) for a in arrays]
    return pl.pallas_call(
        functools.partial(kernel_d, size, HALF // size, len(arrays) - 2),
        out_shape=shapes + [jax.ShapeDtypeStruct((16, 128), F32)],
        in_specs=[vmem] * (len(arrays) + 2),
        out_specs=[vmem] * (len(arrays) + 1),
        compiler_params=pltpu.CompilerParams(vmem_limit_bytes=32 * 2**20),
        name="finish",
    )(small, bias, *arrays)


def per_device(group, hidden_in, cotangent, lengths, *params):
    w_query, w_key, w_value, w_output, w_inner, w_outer = params[:6]
    b_query, b_value, b_output, b_inner, b_outer = params[6:11]
    gain_one, shift_one, gain_two, shift_two = params[11:]
    cols = lax.axis_size("col")
    size = group
    ways = cols // size
    inside = lax.axis_index("col") % size
    row = lax.axis_index("row")

    def regroup(block):
        if ways == 1:
            return block
        whole = lax.all_gather(block, "col", axis=0, tiled=True)
        count = block.shape[0] * ways
        return lax.dynamic_slice_in_dim(whole, inside * count, count, axis=0)

    vec = jnp.zeros((16, 128), BF16)
    vectors = (b_query, b_value, b_output, b_outer, gain_one, shift_one, gain_two, shift_two)
    for at, vector in enumerate(vectors + (b_inner,)):
        line = regroup(vector)
        vec += jnp.pad(line[None, :], ((at, 15 - at), (0, 128 - line.shape[0])))
    qkv_weights = [regroup(w) for w in (w_query, w_key, w_value)]
    rest_weights = [regroup(w) for w in (w_output.T, w_inner, w_outer.T)]
    (hid_all, wq_all, qs, kv, probs, m_all, lse, ctxt, g_parts, layer_out, low, own, d_context, small) = (
        forward_attention(size, lengths, hidden_in, qkv_weights, rest_weights, vec, cotangent)
    )
    (g_query, g_key, g_value, g_output, g_inner, g_outer, g_small, g_bias, grad_in) = (
        backward_attention(
            size,
            d_context,
            qs,
            m_all,
            lse,
            ctxt,
            hid_all,
            wq_all,
            low,
            own,
            small,
            kv,
            probs,
            g_parts,
        )
    )

    def spread(block):
        if ways == 1:
            return block
        count = block.shape[0]
        whole = jnp.zeros((count * size,) + block.shape[1:], block.dtype)
        whole = lax.dynamic_update_slice_in_dim(whole, block, inside * count, axis=0)
        return lax.psum_scatter(whole, "col", scatter_dimension=0, tiled=True)

    arrays = [g_query, g_key, g_value, g_output, g_inner, g_outer, grad_in, layer_out]
    *arrays, tile = finish(size, g_small, g_bias, arrays)
    g_query, g_key, g_value, g_output, g_inner, g_outer, grad_in, layer_out = arrays
    per = HALF // size
    pieces = [spread(tile[at, : 4 * per if at == 6 else per]) for at in range(9)]
    g_b_output, g_b_outer, g_gain_one, g_shift_one, g_gain_two, g_shift_two = pieces[:6]
    g_b_inner, g_b_query, g_b_value = pieces[6:]
    return (
        layer_out,
        grad_in,
        spread(g_query),
        spread(g_key),
        spread(g_value),
        spread(g_output).T,
        spread(g_inner),
        spread(g_outer).T,
        g_b_query,
        g_b_value,
        g_b_output,
        g_b_inner,
        g_b_outer,
        g_gain_one,
        g_shift_one,
        g_gain_two,
        g_shift_two,
    )


def solution(mesh):
    cols = mesh.shape["col"]
    group = max(s for s in range(SPAN, cols + 1, 4) if cols % s == 0 and D // s % 16 == 0)
    token, weight, turned = P("col", "row"), P("col", "row"), P("row", "col")
    vector = P(("row", "col"))
    return jax.shard_map(
        functools.partial(per_device, group),
        mesh=mesh,
        in_specs=(token, token, P()) + (weight,) * 3 + (turned, weight, turned) + (vector,) * 9,
        out_specs=(token, token) + (weight,) * 3 + (turned, weight, turned) + (vector,) * 9,
        check_vma=False,
    )
```

time: 336 us -> 236 us (0.70); the launches traced: 331 us -> 235 us
  matrix products: 32.6 us -> 0 us
  Pallas kernels: 255 us -> 224 us
  local copies, waits for them, and re-layouts: 25.8 us -> 9.15 us
  other arithmetic: 16 us -> 1.4 us
    dot_general x18 -> x0, matrix products: 32.6 us -> none  [dot(): lax.dot_general(left, right, (contract, ((), ())), preferred_element_type...]
    pallas_call x1, Pallas kernels: 134 us -> 111 us  [backward_attention(): pl.pallas_call(functools.partial(kernel_c, size), out_shape=(shape((blk,...]
    pallas_call x1, Pallas kernels: 121 us -> 112 us  [forward_attention(): pl.pallas_call(functools.partial(kernel_a, size), out_shape=(shape((2, ro...]
    another operation x8 -> x0, other arithmetic: 9.12 us -> none  [the longest x3 6.04 us: middle(): g_parts = jnp.stack(parts).reshape(wr_all.shape)]
    concatenate x2 -> x0, local copies, waits for them, and re-layouts: 4.86 us -> none  [the longest x1 4.76 us: per_device(): column = jnp.concatenate(vectors).reshape(blk, 5)]
    slice x7 -> x0, local copies, waits for them, and re-layouts: 4.53 us -> none  [the longest x1 1.64 us: per_device(): g_qkv[:, 2 * HALF:]]
    transpose x2 -> x0, local copies, waits for them, and re-layouts: 3.42 us -> none  [the longest x1 1.9 us: per_device(): spread(g_rest[:, HALF + FF_HALF:REST])]
    unnamed x24 -> x20, local copies, waits for them, and re-layouts: 4.91 us -> 8.09 us
where the time goes in v2:
time: 236 us; the launch traced here: 235 us
  Pallas kernels  224 us (95%)
  local copies, waits for them, and re-layouts  9.15 us (4%)
    pallas_call x1, Pallas kernels, forward_attention(): pl.pallas_call(functools.partial(kernel_a, size), out_shape=(shape((2, ro...  112 us
    pallas_call x1, Pallas kernels, backward_attention(): pl.pallas_call(functools.partial(kernel_c, size), out_shape=(shape((blk,...  111 us
    unnamed x20, local copies, waits for them, and re-layouts  8.09 us

profile of v2, /device:TPU:0, one launch (start us, length us, event | category | flops | bytes accessed | tf_op | source)
XLA Modules:
  0.0 235.0 jit_solution(13594586626895604892)
XLA Ops:
  0.7 1.4 pad_add_fusion.vec_in
  2.1 111.9 %forward_attention.1 = (bf16[2,512,384]{2,1,0:T(8,128)(2,1)}, bf16[16,48,1152]{2,1,0:T(8,128)(2,1)}, bf16[3,512,128]{2,1,0:T(8,128)(2,1)}, bf16[8,6,512,128]{3,2...) custom-call(s32[2]{0:T(128)} %lengths.1, ...), custom_call_target="tpu_custom_call" | custom-call | tf_op jit(solution)/shard_map/forward_attention/pallas_call | solution.py:710
  114.0 0.0 copy-start.1
  114.0 110.5 %backward_attention.1 = (f32[48,384]{1,0:T(8,128)}, f32[48,384]{1,0:T(8,128)}, f32[48,384]{1,0:T(8,128)}, f32[48,384]{1,0:T(8,128)}, f32[48,1536]{1,0:T(8,128)},...) custom-call(bf16[2,256,384]{2,1,0:T(8,128)(2,1)} %get-tuple-element.49.dctx, ...), custom_call_target="tpu_custom_call" | custom-call | tf_op jit(solution)/shard_map/backward_attention/pallas_call | solution.py:1245
  224.5 0.0 copy-done.1
  224.5 0.0 copy-start
  224.5 1.1 copy-done
  225.6 0.0 copy-start.2
  225.6 1.0 copy-done.2
  226.6 0.0 copy-start.3
  226.6 1.0 copy-done.3
  227.6 0.0 copy-start.4
  227.6 0.9 copy-done.4
  228.4 0.0 copy-start.5
  228.5 0.9 copy-done.5
  229.3 0.0 copy-start.6
  229.3 0.9 copy-done.6
  230.2 0.0 copy-start.7
  230.2 0.9 copy-done.7
  231.1 0.0 copy-start.8
  231.1 0.8 copy-done.8
  231.9 0.0 copy-start.9
  231.9 0.7 copy-done.9
  232.6 1.3 finish.1
  233.9 0.5 slice_bitcast_fusion.5
  234.4 0.5 slice_bitcast_fusion
Async XLA Ops:
  114.0 110.5 %copy-start.1 = (bf16[512,384]{1,0:T(8,128)(2,1)S(1)}, bf16[512,384]{1,0:T(8,128)(2,1)}, u32[]{:S(2)}) copy-start(bf16[512,384]{1,0:T(8,128)(2,1)} %get-tuple-element.71.refs_7_) | copy-start | bytes 1179652
  224.5 1.1 copy-start
  225.6 1.0 copy-start.2
  226.6 1.0 copy-start.3
  227.6 0.9 copy-start.4
  228.4 0.9 copy-start.5
  229.3 0.9 copy-start.6
  230.2 0.9 copy-start.7
  231.1 0.8 copy-start.8
  231.9 0.7 copy-start.9

commit v3 on v2

--- a/solution.py
+++ b/solution.py
@@ -815,6 +815,8 @@
     b3,
     b4,
     d_all,
+    hid_t,
+    far,
     gq,
     q1,
     q2,
@@ -844,126 +846,153 @@
     part = rows // 2
     n = place.planes
     r, y, j = place.r, place.y, place.j
-    with jax.named_scope("meet"):
-        meet(place)
-    single = (one_send, one_recv)
-    gs = (g_send, g_recv)
-    ks = (kv_send, kv_recv)
-    at_x, at_y, at_z = 4 * n, 6 * n, 7 * n
-
+    half = size // 2
+    blk = wq_all.shape[1]
     own_rows = pl.ds(pl.multiple_of(r * part, part), part)
     other_rows = pl.ds(pl.multiple_of((1 - r) * part, part), part)
-    send(dctx.at[1 - r], d_ctx.at[own_rows], single, 0, place.to_x()).start()
-    send(small_in, vec_got.at[0], (v_send, v_recv), 0, place.to_x()).start()
-
-    def g_block(index, core):
-        n_at, m = lax.div(index, 2 * n), lax.rem(index, 2)
-        k = lax.rem(lax.div(lax.rem(index, 2 * n), 2) + 1, n)
+
+    def b_block(i):
+        pair, core = lax.div(i, 2), lax.rem(j + 1 + lax.rem(i, 2), 2)
+        return place.near_block(1 - lax.div(pair, 2), 1 - lax.rem(pair, 2), core)
+
+    def kv_load(i):
+        return pltpu.make_async_copy(kv_in.at[b_block(i)], kv.at[i], load.at[i])
+
+    def p_load(t, slot):
+        p, i = lax.div(t, SPAN), lax.rem(t, SPAN)
+        return pltpu.make_async_copy(
+            p_in.at[b_block(i), pl.ds(2 * p, 2)], pbuf.at[slot], p_sem.at[slot]
+        )
+
+    def index(other, k, m):
+        return 2 * n * other + 2 * ((k + n - 1) % n) + m
+
+    def g_block(at, core):
+        n_at, m = at // (2 * n), at % 2
+        k = ((at % (2 * n)) // 2 + 1) % n
         return place.any_block(
             lax.rem(r + 1 + n_at, 2), place.plane(k), lax.rem(y + 1 + m, 2), core
         )
 
-    def c_move(index):
-        return send(g_in.at[g_block(index, 1 - j)], b1.at[index], gs, index, place.to_core())
-
-    def g_load(index):
-        return pltpu.make_async_copy(g_in.at[g_block(index, j)], st.at[index], load.at[8 + index])
+    def g_load(at):
+        return pltpu.make_async_copy(g_in.at[g_block(at, j)], st.at[at], load.at[8 + at])
 
     def loop(count, body):
-        def step(index, carry):
-            body(index)
+        def step(at, carry):
+            body(at)
             return carry
 
         lax.fori_loop(0, count, step, jnp.int32(0))
 
-    loop(4 * n, lambda index: c_move(index).start())
-    loop(4 * n, lambda index: g_load(index).start())
-
-    def b_block(i):
-        pair, core = lax.div(i, 2), lax.rem(j + 1 + lax.rem(i, 2), 2)
-        return place.near_block(1 - lax.div(pair, 2), 1 - lax.rem(pair, 2), core)
-
-    def kv_load(i):
-        return pltpu.make_async_copy(kv_in.at[b_block(i)], kv.at[i], load.at[i])
-
-    def p_load(t, slot):
-        i, p = lax.div(t, PAIRS), lax.rem(t, PAIRS)
-        return pltpu.make_async_copy(
-            p_in.at[b_block(i), pl.ds(2 * p, 2)], pbuf.at[slot], p_sem.at[slot]
-        )
-
+    needed = [(0, 1, 0), (0, 2, 0), (1, 2, 0), (0, 1, 1), (0, 3, 0), (0, 3, 1), (0, 2, 1), (1, 2, 1)]
+    needed += [(1, 1, 0), (1, 1, 1), (0, 0, 0), (0, 0, 1), (1, 3, 0), (1, 3, 1), (1, 0, 0), (1, 0, 1)]
+    needed = [index(*at) for at in needed]
     p_load(jnp.int32(0), 0).start()
+    for at in needed[:4]:
+        g_load(at).start()
     loop(SPAN, lambda i: kv_load(i).start())
-
+    for at in needed[4:]:
+        g_load(at).start()
     lane = lax.broadcasted_iota(jnp.int32, (rows, 128), 1)
     for p in range(PAIRS):
         piece = qs[p]
         qm[2 * p] = jnp.where(lane < HEAD_DIM, piece, jnp.zeros_like(piece))
         qm[2 * p + 1] = jnp.where(lane >= HEAD_DIM, piece, jnp.zeros_like(piece))
     acc[...] = jnp.zeros_like(acc)
+    for which in range(2):
+        hid_t[which] = hid_all[which].T
     d_ctx[own_rows, :] = dctx[r]
-    def core_send(pair):
-        return send(big.at[2 * pair], cb.at[pair], ks, pair, place.to_core())
-
-    def core_add(pair):
-        core_send(pair).wait_recv()
-        for piece in range(2 * PAIRS):
-            total = big[2 * pair + 1, piece].astype(F32) + cb[pair, piece].astype(F32)
-            big[2 * pair + 1, piece] = total.astype(BF16)
-
-    keys, values = pl.ds(0, PAIRS), pl.ds(PAIRS, PAIRS)
-
-    def hop(number):
-        pair, part_of, along_z = (
-            (0, keys, False),
-            (0, values, True),
-            (1, keys, True),
-            (1, values, True),
-            (2, values, False),
-            (2, keys, False),
-        )[number]
-        peer = place.to_z_near() if along_z else place.to_y()
-        return send(big.at[2 * pair + 1, part_of], rb.at[number], ks, 4 + number, peer)
-
-    def hop_add(number, pair, start):
-        hop(number).wait_recv()
-        for piece in range(PAIRS):
-            total = big[2 * pair + 1, start + piece].astype(F32) + rb[number, piece].astype(F32)
-            big[2 * pair + 1, start + piece] = total.astype(BF16)
+    far[...] = jnp.zeros_like(far)
+    far[own_rows, :] = dres_low[1 - r].astype(F32)
+    grad_out[...] = jnp.zeros_like(grad_out)
+    grad_out[own_rows, :] = dres_own[...]
+    with jax.named_scope("meet"):
+        meet(place)
+    single = (one_send, one_recv)
+    gs = (g_send, g_recv)
+    ks = (kv_send, kv_recv)
+    at_x, at_y, at_z = 4 * n, 6 * n, 8 * n
+
+    send(dctx.at[1 - r], d_ctx.at[own_rows], single, 0, place.to_x()).start()
+    send(small_in, vec_got.at[0], (v_send, v_recv), 0, place.to_x()).start()
+
+    def c_move(at):
+        return send(g_in.at[g_block(at, 1 - j)], b1.at[at], gs, at, place.to_core())
+
+    for at in needed:
+        c_move(at).start()
 
     def fold(target, source, at):
         total = target[at].astype(F32) + source.astype(F32)
         target[at] = total.astype(BF16)
 
-    def g_core_add(index):
-        c_move(index).wait_recv()
-        g_load(index).wait()
-        fold(st, b1[index], index)
-
-    def g_x_send(index):
-        return send(st.at[index], b2.at[index], gs, at_x + index, place.to_x())
-
-    def g_x_add(index):
-        g_x_send(index).wait_recv()
-        fold(st, b2[index], 2 * n + index)
-
-    def kept(m, k):
-        return 2 * n + 2 * ((k + n - 1) % n) + m
-
-    def g_y_send(k):
-        return send(st.at[kept(0, k)], b3.at[k], gs, at_y + k, place.to_y())
-
-    def g_y_add(k):
-        g_y_send(k).wait_recv()
-        fold(st, b3[k], kept(1, k))
-
-    def g_z_send(k):
-        return send(st.at[kept(1, k)], b4.at[k - 1], gs, at_z + k - 1, place.to_z(k))
+    def pieces(p):
+        return pl.ds(2 * p, 2)
+
+    def core_send(p, pair):
+        return send(
+            big.at[2 * pair, pieces(p)], cb.at[pair, pieces(p)], ks, 4 * p + pair, place.to_core()
+        )
+
+    def core_add(p, pair):
+        core_send(p, pair).wait_recv()
+        for piece in (2 * p, 2 * p + 1):
+            fold(big, cb[pair, piece], (2 * pair + 1, piece))
+
+    def hop(p, pair):
+        peer = place.to_y() if pair == 2 else place.to_z_near()
+        number = 4 * PAIRS + 3 * p + pair
+        return send(big.at[2 * pair + 1, pieces(p)], rb.at[pair, pieces(p)], ks, number, peer)
+
+    def hop_add(p):
+        hop(p, 0).wait_recv()
+        for piece in (2 * p, 2 * p + 1):
+            fold(big, rb[0, piece], (5, piece))
+
+    def g_core_add(other, k, m):
+        at = index(other, k, m)
+        c_move(at).wait_recv()
+        g_load(at).wait()
+        fold(st, b1[at], at)
+
+    def gx(k, m):
+        at = index(0, k, m)
+        return send(st.at[at], b2.at[at], gs, at_x + at, place.to_x())
+
+    def gx_add(k, m):
+        gx(k, m).wait_recv()
+        fold(st, b2[index(0, k, m)], index(1, k, m))
+
+    def gy(k, other):
+        slot = 2 * k + other
+        return send(st.at[index(other, k, 0)], b3.at[slot], gs, at_y + slot, place.to_y())
+
+    def gy_add(k, other):
+        gy(k, other).wait_recv()
+        fold(st, b3[2 * k + other], index(other, k, 1))
+
+    def gz(k):
+        return send(st.at[index(1, k, 1)], b4.at[k - 1], gs, at_z + k - 1, place.to_z(k))
+
+    vz = (v_send, v_recv)
+
+    def vector(number):
+        level = min(number, 3)
+        step = max(number - 2, 1)
+        peer = (place.to_x(), place.to_core(), place.to_y(), place.to_z(step))[level]
+        source = small_in if level == 0 else vec_sum.at[level - 1]
+        return send(source, vec_got.at[number], vz, number, peer)
+
+    def vector_add(level):
+        vector(level).wait_recv()
+        before = small_in[...] if level == 0 else vec_sum[level - 1]
+        vec_sum[level] = before + vec_got[level]
 
     with jax.named_scope("first_adds"):
-        for at in range(2):
-            g_core_add(at)
-            g_x_send(at).start()
+        g_core_add(0, 1, 0)
+        gx(1, 0).start()
+        g_core_add(0, 2, 0)
+        gy(2, 0).start()
     with jax.named_scope("context_row"):
         send(dctx.at[1 - r], d_ctx.at[other_rows], single, 0, place.to_x()).wait_recv()
     upper = lax.broadcasted_iota(jnp.int32, (128, rows), 0) < HEAD_DIM
@@ -974,70 +1003,149 @@
         delta[2 * p + 1] = jnp.sum(product[HEAD_DIM:], axis=0, keepdims=True)
         dtot[2 * p] = jnp.where(upper, turned, 0.0)
         dtot[2 * p + 1] = jnp.where(upper, 0.0, turned)
-
-    vz = (v_send, v_recv)
-
-    def vector(number):
-        level = min(number, 3)
-        step = max(number - 2, 1)
-        peer = (place.to_x(), place.to_core(), place.to_y(), place.to_z(step))[level]
-        source = small_in if level == 0 else vec_sum.at[level - 1]
-        return send(source, vec_got.at[number], vz, number, peer)
-
-    def vector_add(level):
-        vector(level).wait_recv()
-        before = small_in[...] if level == 0 else vec_sum[level - 1]
-        vec_sum[level] = before + vec_got[level]
+    with jax.named_scope("vector_row"):
+        vector_add(0)
+        vector(1).start()
+
+    qz = (q_send, q_recv)
+
+    def q_core(p):
+        return send(gq.at[p, 1 - j], q1.at[p], qz, (n + 1) * p, place.to_core())
+
+    def q_side(p):
+        return send(gq.at[p, j, 1 - y], q2.at[p], qz, (n + 1) * p + 1, place.to_y())
+
+    def q_plane(p, k):
+        return send(
+            gq.at[p, j, y, place.plane(k)], q3.at[p, k - 1], qz, (n + 1) * p + 1 + k, place.to_z(k)
+        )
+
+    def q_core_add(p):
+        q_core(p).wait_recv()
+        for side in range(2):
+            fold(gq, q1[p, side], (p, j, side))
+
+    def q_side_add(p):
+        q_side(p).wait_recv()
+        fold(gq, q2[p], (p, j, y))
+
+    def q_planes(p):
+        for k in range(1, n):
+            q_plane(p, k).start()
+
+    def settle(p):
+        core_send(p, 3).wait_recv()
+        hop(p, 1).wait_recv()
+        hop(p, 2).wait_recv()
+        both = jnp.concatenate([acc[2 * p], acc[2 * p + 1]], axis=0)
+        d_query = (both.T * 0.125).astype(BF16)
+        d_all[p, :, 0:128] = d_query
+        lanes = slice(p * 128, (p + 1) * 128)
+        bias_own[0, 0:1, lanes] = jnp.sum(d_query.astype(F32), axis=0, keepdims=True)
+        for at in range(2):
+            piece = 2 * p + at
+            total = big[7, piece].astype(F32) + cb[3, piece].astype(F32)
+            total += rb[1, piece].astype(F32) + rb[2, piece].astype(F32)
+            low = total.astype(BF16)
+            d_all[p, :, (at + 1) * 128 : (at + 2) * 128] = low
+        bias_own[0, 1:2, lanes] = jnp.sum(low.astype(F32), axis=0, keepdims=True)
+
+    def input_term(p, which):
+        parts = []
+        for at in range(3):
+            columns = slice(at * HALF + p * 128, at * HALF + (p + 1) * 128)
+            parts.append(wq_all[pl.ds(which * half, half), :, columns].reshape(HALF, 128))
+        return dot(d_all[p], jnp.concatenate(parts, axis=1), NT)
+
+    def far_term(p):
+        far[...] = far[...] + input_term(p, 1 - r)
+
+    def own_term(p):
+        grad_out[...] = grad_out[...] + input_term(p, r)
+
+    def grads(p):
+        for which in range(2):
+            term = dot(hid_t[which], d_all[p], NN).astype(BF16)
+            for b in range(half):
+                c = which * half + b
+                gq[p, c % 2, (c // 2) % 2, c // 4] = term[b * blk : (b + 1) * blk]
 
     events = {}
 
     def add(step, what, *inputs):
         events.setdefault(step, []).append(functools.partial(what, *inputs))
 
-    def start(what, number):
-        what(number).start()
-
-    for at in range(2 * n):
-        if at > 1:
-            add(at - 2, g_core_add, at)
-            add(at - 1, start, g_x_send, at)
-        add(6 + at, g_core_add, 2 * n + at)
-    arrive = [8, 13, 18, 23]
-    for at, step in enumerate(arrive):
-        add(step, g_x_add, at)
-    for pair in range(4):
-        add(6 * pair + 3, start, core_send, pair)
-        if pair < 3:
-            add(6 * pair + 6, core_add, pair)
-    for level in range(3):
-        add(2 * level, vector_add, level)
-        add(2 * level + 1, start, vector, level + 1)
-    for step in range(2, n):
-        add(5, start, vector, 2 + step)
-    add(7, start, hop, 0)
-    add(7, start, hop, 1)
-    add(13, start, hop, 3)
-    add(17, hop_add, 0, 1, 0)
-    add(18, start, hop, 2)
-    add(19, start, hop, 5)
-    add(20, hop_add, 1, 2, PAIRS)
-    add(21, start, hop, 4)
-    add(9, start, g_y_send, 1)
-    add(18, g_y_add, 1)
-    add(19, start, g_z_send, 1)
-    add(22, start, g_y_send, 2)
+    def start(step, what, *inputs):
+        add(step, lambda: what(*inputs).start())
+
+    bias_own[0, 2:8] = jnp.zeros((6, HALF), F32)
+    add(0, g_core_add, 0, 1, 1)
+    add(0, g_core_add, 1, 2, 0)
+    start(1, gx, 1, 1)
+    start(1, gy, 2, 1)
+    add(1, g_core_add, 0, 3, 0)
+    add(2, g_core_add, 0, 3, 1)
+    late = [(1, 1, 0), (1, 1, 1), (0, 2, 1), (1, 2, 1), (0, 0, 0), (0, 0, 1), (1, 3, 0), (1, 3, 1)]
+    for at, what in enumerate(late + [(1, 0, 0), (1, 0, 1)]):
+        add(3 + at, g_core_add, *what)
+    start(2, gx, 3, 0)
+    add(5, vector_add, 1)
+    start(5, vector, 2)
+    add(7, gy_add, 2, 0)
+    add(7, gx_add, 1, 0)
+    add(7, gx_add, 1, 1)
+    start(8, gy, 1, 1)
+    add(8, gy_add, 2, 1)
+    start(9, gx, 2, 1)
+    start(9, gx, 3, 1)
+    start(9, gx, 0, 0)
+    start(10, gx, 0, 1)
+    add(10, vector_add, 2)
+    for step in range(1, n):
+        start(10, vector, 2 + step)
+    add(15, gy_add, 1, 1)
+    start(15, gz, 1)
+    add(17, gx_add, 2, 1)
+    add(18, gx_add, 3, 0)
+    add(18, gx_add, 3, 1)
+    start(18, gy, 3, 1)
+    start(22, gz, 2)
+    for p in range(PAIRS):
+        base = SPAN * p
+        late = 7 if p == PAIRS - 1 else 8
+        start(base + 2, core_send, p, 0)
+        add(base + 3, core_add, p, 0)
+        start(base + 3, hop, p, 0)
+        start(base + 4, core_send, p, 1)
+        add(base + 5, core_add, p, 1)
+        start(base + 5, hop, p, 1)
+        start(base + 6, core_send, p, 2)
+        add(base + 7, core_add, p, 2)
+        add(base + late, hop_add, p)
+        start(base + late, hop, p, 2)
+        start(base + 8, core_send, p, 3)
+        if p < PAIRS - 1:
+            add(base + 14, settle, p)
+            add(base + 14, grads, p)
+            start(base + 14, q_core, p)
+            add(base + 15, far_term, p)
+            add(base + 15, own_term, p)
+            add(base + 15, q_core_add, p)
+    add(23, gy_add, 3, 1)
+    start(23, gz, 3)
 
     steps = SPAN * PAIRS
 
     def back(t, carry):
-        i, p = lax.div(t, PAIRS), lax.rem(t, PAIRS)
+        p, i = lax.div(t, SPAN), lax.rem(t, SPAN)
         for step, calls in sorted(events.items()):
-
-            @pl.when(t == step)
-            def _(calls=calls):
-                with jax.named_scope(f"step_{step}"):
-                    for call in calls:
-                        call()
+            if step < steps:
+
+                @pl.when(t == step)
+                def _(calls=calls):
+                    with jax.named_scope(f"step_{step}"):
+                        for call in calls:
+                            call()
 
         slot = lax.rem(t, 2)
 
@@ -1067,74 +1175,27 @@
             acc[g] += dot(key_t[h * HEAD_DIM : (h + 1) * HEAD_DIM], d_scores, NN)
             d_key = key_term if d_key is None else d_key + key_term
             d_value = value_term if d_value is None else d_value + value_term
-        big[i, p] = d_key.astype(BF16)
-        big[i, PAIRS + p] = d_value.astype(BF16)
+        big[i, 2 * p] = d_key.astype(BF16)
+        big[i, 2 * p + 1] = d_value.astype(BF16)
         return carry
 
     lax.fori_loop(0, steps, back, jnp.int32(0))
 
-    for p in range(PAIRS):
-        both = jnp.concatenate([acc[2 * p], acc[2 * p + 1]], axis=0)
-        d_all[:, p * 128 : (p + 1) * 128] = (both.T * 0.125).astype(BF16)
-    with jax.named_scope("g_x_4"):
-        g_x_add(4)
-        g_x_add(5)
-    g_y_send(3).start()
-    with jax.named_scope("last_hops"):
-        core_send(3).wait_recv()
-        for number in (2, 3, 5, 4):
-            hop(number).wait_recv()
-    for piece in range(PAIRS):
-        at = HALF + piece * 128
-        total = big[7, piece].astype(F32) + cb[3, piece].astype(F32)
-        total += rb[2, piece].astype(F32) + rb[5, piece].astype(F32)
-        d_all[:, at : at + 128] = total.astype(BF16)
-        at = 2 * HALF + piece * 128
-        total = big[7, PAIRS + piece].astype(F32) + cb[3, PAIRS + piece].astype(F32)
-        total += rb[3, piece].astype(F32) + rb[4, piece].astype(F32)
-        d_all[:, at : at + 128] = total.astype(BF16)
-
-    half = size // 2
-    blk = wq_all.shape[1]
-
-    def input_term(which):
-        weight = wq_all[pl.ds(which * half, half)].reshape(HALF, QKV)
-        return dot(d_all[...], weight, NT)
-
-    with jax.named_scope("input_term"):
-        grad_out[...] = input_term(1 - r)
-        grad_out[own_rows, :] = grad_out[own_rows, :] + dres_low[1 - r].astype(F32)
-        near[0] = grad_out[...].astype(BF16)
-    with jax.named_scope("g_x_6"):
-        g_x_add(6)
-    with jax.named_scope("g_y_2"):
-        g_y_add(2)
+    last = PAIRS - 1
+    for call in events[steps]:
+        call()
+    q_side(0).start()
+    q_side(1).start()
+    with jax.named_scope("settle"):
+        settle(last)
+    with jax.named_scope("far"):
+        far_term(last)
+        near[0] = far[...].astype(BF16)
     to_near = send(near.at[0], near.at[1], single, 3, place.to_x())
+    with jax.named_scope("grads"):
+        grads(last)
     to_near.start()
-    g_z_send(2).start()
-    with jax.named_scope("qkv_grad"):
-        for which in range(2):
-            term = dot(hid_all[which], d_all[...], TN).astype(BF16)
-            gq[which * half : (which + 1) * half] = term.reshape(half, blk, QKV)
-    g_y_send(0).start()
-    qz = (q_send, q_recv)
-
-    def q_block(index, core):
-        m, k = lax.div(index, n), lax.rem(index, n)
-        return place.col_block(place.plane(k), lax.rem(y + 1 + m, 2), core)
-
-    def q_core(index):
-        return send(gq.at[q_block(index, 1 - j)], q1.at[index], qz, index, place.to_core())
-
-    def q_side(k):
-        return send(gq.at[q_block(k, j)], q2.at[k], qz, 2 * n + k, place.to_y())
-
-    def q_plane(k):
-        return send(gq.at[q_block(n + k, j)], q3.at[k - 1], qz, 3 * n + k - 1, place.to_z(k))
-
-    bias_own[0, 0:1] = jnp.sum(d_all[:, :HALF].astype(F32), axis=0, keepdims=True)
-    bias_own[0, 1:2] = jnp.sum(d_all[:, 2 * HALF :].astype(F32), axis=0, keepdims=True)
-    bias_own[0, 2:8] = jnp.zeros((6, HALF), F32)
+    q_core(last).start()
     sz = (s_send, s_recv)
 
     def small(number):
@@ -1142,89 +1203,100 @@
         peer = (place.to_core(), place.to_y(), place.to_z(max(number - 1, 1)))[level]
         return send(bias_own.at[level], bias_got.at[number], sz, number, peer)
 
-    loop(2 * n, lambda index: q_core(index).start())
-    with jax.named_scope("input_own"):
-        grad_out[...] = input_term(r)
-        grad_out[own_rows, :] = grad_out[own_rows, :] + dres_own[...]
     small(0).start()
-
-    def q_core_add(index):
-        q_core(index).wait_recv()
-        fold(gq, q1[index], q_block(index, j))
-
-    with jax.named_scope("q_core_a"):
-        loop(n, q_core_add)
+    with jax.named_scope("own"):
+        own_term(last)
+    with jax.named_scope("q_core"):
+        q_core_add(last)
         small(0).wait_recv()
-    bias_own[1] = bias_own[0] + bias_got[0]
-    loop(n, lambda k: q_side(k).start())
-    with jax.named_scope("q_core_b"):
-        loop(n, lambda k: q_core_add(n + k))
+        bias_own[1] = bias_own[0] + bias_got[0]
+    q_side(last).start()
     small(1).start()
-    with jax.named_scope("g_x_7"):
-        g_x_add(7)
-    with jax.named_scope("g_y_3"):
-        g_y_add(3)
-        g_z_send(3).start()
-    with jax.named_scope("g_y_0"):
-        g_y_add(0)
-    with jax.named_scope("q_side"):
-        for k in range(n):
-            q_side(k).wait_recv()
-            fold(gq, q2[k], q_block(n + k, j))
-            if k:
-                q_plane(k).start()
+    with jax.named_scope("g_x_0"):
+        gx_add(0, 0)
+        gx_add(0, 1)
+    gy(0, 1).start()
+    with jax.named_scope("q_side_0"):
+        q_side_add(0)
+        q_planes(0)
+    with jax.named_scope("q_side_1"):
+        q_side_add(1)
+        q_planes(1)
+    with jax.named_scope("q_side_2"):
+        q_side_add(last)
+        q_planes(last)
         small(1).wait_recv()
-    bias_own[2] = bias_own[1] + bias_got[1]
+        bias_own[2] = bias_own[1] + bias_got[1]
+    for step in range(1, n):
+        small(1 + step).start()
+    with jax.named_scope("vectors"):
+        total = vec_sum[2]
+        for step in range(1, n):
+            vector(2 + step).wait_recv()
+            total = total + vec_got[2 + step]
+        small_out[...] = total
+
+    def q_out(p):
+        total = gq[p, j, y, place.z].astype(F32)
+        for k in range(1, n):
+            q_plane(p, k).wait_recv()
+            total = total + q3[p, k - 1].astype(F32)
+        lanes = slice(p * 128, (p + 1) * 128)
+        query_out[:, lanes] = total[:, :128]
+        key_out[:, lanes] = total[:, 128:256]
+        value_out[:, lanes] = total[:, 256:]
+
+    with jax.named_scope("q_out_0"):
+        q_out(0)
     with jax.named_scope("near_wait"):
         to_near.wait_recv()
-    grad_out[...] = grad_out[...] + near[1].astype(F32)
-    for step in range(1, n):
-        small(1 + step).start()
-    total = vec_sum[2]
-    for step in range(1, n):
-        vector(2 + step).wait_recv()
-        total = total + vec_got[2 + step]
-    small_out[...] = total
-    total = st[kept(1, 0)].astype(F32)
-    with jax.named_scope("g_plane"):
+        grad_out[...] = grad_out[...] + near[1].astype(F32)
+    with jax.named_scope("g_z"):
+        total = None
         for k in range(1, n):
-            g_z_send(k).wait_recv()
-            total = total + b4[k - 1].astype(F32)
+            gz(k).wait_recv()
+            got = b4[k - 1].astype(F32)
+            total = got if total is None else total + got
+    with jax.named_scope("g_y_0"):
+        gy_add(0, 1)
+        total = total + st[index(1, 0, 1)].astype(F32)
         wo_out[...] = total[:, :HALF]
         wi_out[...] = total[:, HALF:FIRST]
         wu_out[...] = total[:, FIRST:]
-    total = gq[q_block(n, j)].astype(F32)
-    with jax.named_scope("q_plane"):
-        for k in range(1, n):
-            q_plane(k).wait_recv()
-            total = total + q3[k - 1].astype(F32)
-        query_out[...] = total[:, :HALF]
-        key_out[...] = total[:, HALF : 2 * HALF]
-        value_out[...] = total[:, 2 * HALF :]
+    with jax.named_scope("q_out"):
+        q_out(1)
+        q_out(last)
         total = bias_own[2]
         for step in range(1, n):
             small(1 + step).wait_recv()
             total = total + bias_got[1 + step]
         bias_out[...] = total
 
-    loop(4 * n, lambda index: c_move(index).wait_send())
-    loop(2 * n, lambda index: g_x_send(index).wait_send())
+    for at in range(4 * n):
+        c_move(at).wait_send()
     for k in range(n):
-        g_y_send(k).wait_send()
+        first = (2,) if k == 2 else ()
+        for m in range(2):
+            if not first or m == 1:
+                gx(k, m).wait_send()
+            if first or m == 1:
+                gy(k, m).wait_send()
     for k in range(1, n):
-        g_z_send(k).wait_send()
-        q_plane(k).wait_send()
+        gz(k).wait_send()
         small(1 + k).wait_send()
+        for p in range(PAIRS):
+            q_plane(p, k).wait_send()
     small(0).wait_send()
+    small(1).wait_send()
     for number in range(n + 2):
         vector(number).wait_send()
-    small(1).wait_send()
-    loop(2 * n, lambda index: q_core(index).wait_send())
-    loop(n, lambda k: q_side(k).wait_send())
-    for pair in range(4):
-        core_send(pair).wait_send()
-    for number in range(6):
-        hop(number).wait_send()
+    for p in range(PAIRS):
+        q_core(p).wait_send()
+        q_side(p).wait_send()
+        for pair in range(4):
+            core_send(p, pair).wait_send()
+        for pair in range(3):
+            hop(p, pair).wait_send()
     to_near.wait_send()
     send(dctx.at[1 - r], d_ctx.at[own_rows], single, 0, place.to_x()).wait_send()
 
@@ -1241,7 +1313,7 @@
     shape = jax.ShapeDtypeStruct
     dma = pltpu.SemaphoreType.DMA
     scratch = pltpu.VMEM
-    g_count, q_count = 4 * n + 2 * n + n + n - 1, 2 * n + n + n - 1
+    g_count, q_count = 4 * n + 2 * n + 2 * n + n - 1, PAIRS * (n + 1)
     return pl.pallas_call(
         functools.partial(kernel_c, size),
         out_shape=(
@@ -1267,17 +1339,19 @@
             scratch((2, 2, rows, rows), BF16),
             scratch((SPAN, 2 * PAIRS, rows, 128), BF16),
             scratch((4, 2 * PAIRS, rows, 128), BF16),
-            scratch((6, PAIRS, rows, 128), BF16),
+            scratch((3, 2 * PAIRS, rows, 128), BF16),
             scratch((4 * n, blk, REST), BF16),
             scratch((4 * n, blk, REST), BF16),
             scratch((2 * n, blk, REST), BF16),
-            scratch((n, blk, REST), BF16),
+            scratch((2 * n, blk, REST), BF16),
             scratch((n - 1, blk, REST), BF16),
-            scratch((rows, QKV), BF16),
-            scratch((size, blk, QKV), BF16),
-            scratch((2 * n, blk, QKV), BF16),
-            scratch((n, blk, QKV), BF16),
-            scratch((n - 1, blk, QKV), BF16),
+            scratch((PAIRS, rows, HALF), BF16),
+            scratch((2, HALF, rows), BF16),
+            scratch((rows, HALF), F32),
+            scratch((PAIRS, 2, 2, n, blk, HALF), BF16),
+            scratch((PAIRS, 2, n, blk, HALF), BF16),
+            scratch((PAIRS, n, blk, HALF), BF16),
+            scratch((PAIRS, n - 1, blk, HALF), BF16),
             scratch((2, rows, HALF), BF16),
             scratch((3, 8, HALF), F32),
             scratch((n + 1, 8, HALF), F32),
@@ -1285,8 +1359,8 @@
             scratch((n + 2, 16, D), F32),
             dma((4,)),
             dma((4,)),
-            dma((10,)),
-            dma((10,)),
+            dma((7 * PAIRS,)),
+            dma((7 * PAIRS,)),
             dma((g_count,)),
             dma((g_count,)),
             dma((q_count,)),
@@ -1305,10 +1379,17 @@
     )(dctx, qs, m_in, lse_in, ctxt, hid_all, wq_all, dres_low, dres_own, small_in, kv_in, p_in, g_in)
 
 
-def kernel_d(size, per, big, small, bias, *refs):
-    sources, targets, tile = refs[: big + 2], refs[big + 2 : -1], refs[-1]
-    for source, target in zip(sources, targets):
-        target[...] = source[...]
+def kernel_d(size, per, count, *refs):
+    sources, targets = refs[:count], refs[count : 2 * count - 1]
+    held, tile, come, go = refs[2 * count - 1 : 3 * count - 1], refs[-3], refs[-2], refs[-1]
+    small, bias = held[0], held[1]
+    loads = [pltpu.make_async_copy(s, h, come.at[at]) for at, (s, h) in enumerate(zip(sources, held))]
+    done = list(held[2:]) + [tile]
+    stores = [pltpu.make_async_copy(h, t, go.at[at]) for at, (h, t) in enumerate(zip(done, targets))]
+    for copy in loads:
+        copy.start()
+    loads[0].wait()
+    loads[1].wait()
     row = lax.axis_index("row")
     inside = lax.rem(lax.axis_index("col"), size)
     start = row * HALF + inside * per
@@ -1321,19 +1402,30 @@
     tile[6:7] = jnp.sum(jnp.where(line == wanted, hidden, 0.0), axis=0, keepdims=True)
     tile[7:9] = pltpu.roll(bias[...], HALF - inside * per, 1)[0:2, :128]
     tile[9:16] = jnp.zeros((7, 128), F32)
+    stores[-1].start()
+    for load, store in zip(loads[2:], stores):
+        load.wait()
+        store.start()
+    for store in stores:
+        store.wait()
 
 
 def finish(size, small, bias, arrays):
-    vmem = pl.BlockSpec(memory_space=pltpu.VMEM)
+    space = pl.BlockSpec(memory_space=pl.ANY)
     shapes = [jax.ShapeDtypeStruct(a.shape, a.dtype) for a in arrays]
+    arrays = [small, bias] + arrays
+    count = len(arrays)
     return pl.pallas_call(
-        functools.partial(kernel_d, size, HALF // size, len(arrays) - 2),
+        functools.partial(kernel_d, size, HALF // size, count),
         out_shape=shapes + [jax.ShapeDtypeStruct((16, 128), F32)],
-        in_specs=[vmem] * (len(arrays) + 2),
-        out_specs=[vmem] * (len(arrays) + 1),
-        compiler_params=pltpu.CompilerParams(vmem_limit_bytes=32 * 2**20),
+        in_specs=[space] * count,
+        out_specs=[space] * (count - 1),
+        scratch_shapes=[pltpu.VMEM(a.shape, a.dtype) for a in arrays]
+        + [pltpu.VMEM((16, 128), F32)]
+        + [pltpu.SemaphoreType.DMA((count,))] * 2,
+        compiler_params=pltpu.CompilerParams(vmem_limit_bytes=63 * 2**20),
         name="finish",
-    )(small, bias, *arrays)
+    )(*arrays)
 
 
 def per_device(group, hidden_in, cotangent, lengths, *params):

time: 236 us -> 222 us (0.941)
  Pallas kernels: 224 us -> 217 us
  local copies, waits for them, and re-layouts: 9.15 us -> 2.66 us
    pallas_call x1, Pallas kernels: 111 us -> 102 us  [backward_attention(): pl.pallas_call(functools.partial(kernel_c, size), out_shape=(shape((blk,...]
    unnamed x20 -> x0, local copies, waits for them, and re-layouts: 8.09 us -> none
where the time goes in v3:
time: 222 us
  Pallas kernels  217 us (98%)
  local copies, waits for them, and re-layouts  2.66 us (1%)
    pallas_call x1, Pallas kernels, forward_attention(): pl.pallas_call(functools.partial(kernel_a, size), out_shape=(shape((2, ro...  112 us
    pallas_call x1, Pallas kernels, backward_attention(): pl.pallas_call(functools.partial(kernel_c, size), out_shape=(shape((blk,...  102 us

profile of v3, /device:TPU:0, one launch (start us, length us, event | category | flops | bytes accessed | tf_op | source)
XLA Modules:
  0.0 221.7 jit_solution(1934404475468471012)
XLA Ops:
  0.7 1.4 pad_add_fusion.vec_in
  2.1 111.8 %forward_attention.1 = (bf16[2,512,384]{2,1,0:T(8,128)(2,1)}, bf16[16,48,1152]{2,1,0:T(8,128)(2,1)}, bf16[3,512,128]{2,1,0:T(8,128)(2,1)}, bf16[8,6,512,128]{3,2...) custom-call(s32[2]{0:T(128)} %lengths.1, ...), custom_call_target="tpu_custom_call" | custom-call | tf_op jit(solution)/shard_map/forward_attention/pallas_call | solution.py:710
  113.8 102.4 %backward_attention.1 = (f32[48,384]{1,0:T(8,128)}, f32[48,384]{1,0:T(8,128)}, f32[48,384]{1,0:T(8,128)}, f32[48,384]{1,0:T(8,128)}, f32[48,1536]{1,0:T(8,128)},...) custom-call(bf16[2,256,384]{2,1,0:T(8,128)(2,1)} %get-tuple-element.49.dctx, ...), custom_call_target="tpu_custom_call" | custom-call | tf_op jit(solution)/shard_map/backward_attention/pallas_call | solution.py:1317
  216.2 2.7 %finish.1 = (f32[48,384]{1,0:T(8,128)}, f32[48,384]{1,0:T(8,128)}, f32[48,384]{1,0:T(8,128)}, f32[48,384]{1,0:T(8,128)}, f32[48,1536]{1,0:T(8,128)}, /*index=5*/...) custom-call(f32[16,768]{1,0:T(8,128)} %get-tuple-element.62.refs_0_, ...), custom_call_target="tpu_custom_call" | custom-call | tf_op jit(solution)/shard_map/finish/pallas_call | solution.py:1418
  218.9 1.2 slice_bitcast_fusion.5
  220.1 1.5 slice_bitcast_fusion

commit v4 on v3

--- a/solution.py
+++ b/solution.py
@@ -369,6 +369,30 @@
     wq_local = pltpu.make_async_copy(wq_all, wq_out, local.at[3])
     wq_local.start()
 
+    kvs = (kv_send, kv_recv)
+
+    def kv_block(i):
+        pair, core = lax.div(i, 2), lax.rem(j + lax.rem(i, 2), 2)
+        return place.near_block(lax.div(pair, 2), lax.rem(pair, 2), core)
+
+    def kv_move(number, p):
+        what = (0, 0, 0, 2, 0, 4, 2, 6)[number]
+        if number % 2:
+            peer = place.to_core()
+        else:
+            peer = place.to_y() if number == 2 else place.to_z_near()
+        where = kv_block(jnp.int32(what))
+        block = kv.at[where, pl.ds(2 * p, 2)]
+        return send(block, block, kvs, SPAN * p + number, peer)
+
+    def kv_start(number, p):
+        kv_move(number, p).start()
+
+    def kv_here(number, p):
+        where = kv_block(jnp.int32(number))
+        block = kv.at[where, pl.ds(2 * p, 2)]
+        send(block, block, kvs, SPAN * p + number, place.to_core()).wait_recv()
+
     own_tiles = vec_all[pl.ds(r * size, size)]
     b_query, b_value = spread_rows(own_tiles, (0, 1), HALF // size, HALF)
     own = place.near_block(0, 0, j)
@@ -391,55 +415,21 @@
                 qm[2 * p] = jnp.where(lane < HEAD_DIM, piece, jnp.zeros_like(piece))
                 qm[2 * p + 1] = jnp.where(lane >= HEAD_DIM, piece, jnp.zeros_like(piece))
             else:
-                kv[own, (which - 1) * PAIRS + p] = piece
+                kv[own, 2 * p + which - 1] = piece
         if which == 1:
             with jax.named_scope("after_key"):
                 rest_x(one, 0)
         if which == 2:
             with jax.named_scope("after_value"):
+                for number in (2, 4, 1):
+                    kv_start(number, 0)
                 rest_y(one, 1)
     acc[...] = jnp.zeros_like(acc)
     high[...] = jnp.full_like(high, MASKED)
     low[...] = jnp.zeros_like(low)
 
-    n_one = place.device(r, place.z - place.zl + lax.rem(place.zl + 1 - j, 2), lax.rem(y + j, 2), j)
-    n_two = place.device(r, place.z - place.zl + lax.rem(place.zl + j, 2), lax.rem(y + 1 - j, 2), j)
-    kvs = (kv_send, kv_recv)
-
-    def kv_block(i):
-        pair, core = lax.div(i, 2), lax.rem(j + lax.rem(i, 2), 2)
-        b0, b1 = lax.rem(pair, 2), lax.div(pair, 2)
-        return place.near_block(b0 * (1 - core) + b1 * core, b0 * core + b1 * (1 - core), core)
-
-    def kv_move(number, what, peer):
-        where = kv_block(what)
-        return send(kv.at[where], kv.at[where], kvs, number, peer)
-
-    kv_move(1, 0, place.to_core()).start()
-    kv_move(2, 0, n_one).start()
     q_local = pltpu.make_async_copy(qs, q_out, local.at[4])
     q_local.start()
-
-    def arrived(number):
-        kv_move(number, number, n_one).wait_recv()
-
-    def second():
-        kv_move(4, 0, n_two).start()
-
-    def first_here():
-        arrived(2)
-        kv_move(3, 2, place.to_core()).start()
-
-    def third():
-        kv_move(6, 2, n_two).start()
-
-    def second_here():
-        arrived(4)
-        kv_move(5, 4, place.to_core()).start()
-
-    def third_here():
-        arrived(6)
-        kv_move(7, 6, place.to_core()).start()
 
     def vec_rows():
         for k in range(n):
@@ -454,56 +444,112 @@
     def add(step, what, *inputs):
         events.setdefault(step, []).append(functools.partial(what, *inputs))
 
+    add(1, kv_here, 1, 0)
     add(1, vec_rows)
     add(2, rest_x, one, 1)
-    add(2, two_start)
-    add(3, arrived, 1)
-    add(4, rest_y, one, 2)
-    add(5, rest_y, one, 3)
-    add(5, second)
+    add(2, kv_here, 2, 0)
+    add(2, kv_start, 3, 0)
+    add(2, kv_start, 6, 0)
+    add(3, kv_here, 3, 0)
+    add(3, rest_y, one, 2)
+    add(4, kv_here, 4, 0)
+    add(4, kv_start, 5, 0)
+    add(4, rest_y, one, 3)
+    add(5, kv_here, 5, 0)
+    add(5, two_start)
+    add(5, kv_start, 2, 1)
+    add(5, kv_start, 4, 1)
+    add(5, kv_start, 1, 1)
+    add(6, kv_here, 6, 0)
+    add(6, kv_start, 7, 0)
     add(6, rest_x, two, 0)
-    add(6, first_here)
+    add(7, kv_here, 7, 0)
     add(7, rest_x, one, 2)
     add(8, rest_x, one, 3)
     add(8, rest_c, one, 0, 0)
-    add(8, third)
+    add(9, kv_here, 1, 1)
     add(9, rest_c, one, 1, 0)
-    add(9, arrived, 3)
-    add(10, rest_y, two, 1)
-    add(12, second_here)
+    add(10, kv_here, 2, 1)
+    add(10, kv_start, 3, 1)
+    add(10, kv_start, 6, 1)
+    add(11, kv_here, 3, 1)
+    add(11, rest_y, two, 1)
+    add(11, kv_start, 2, 2)
+    add(11, kv_start, 4, 2)
+    add(11, kv_start, 1, 2)
+    add(12, kv_here, 4, 1)
+    add(12, kv_start, 5, 1)
+    add(13, kv_here, 5, 1)
     add(13, rest_c, one, 0, 1)
     add(13, rest_c, one, 1, 1)
     add(13, rest_y, two, 2)
+    add(14, kv_here, 6, 1)
+    add(14, kv_start, 7, 1)
     add(14, rest_x, two, 1)
-    add(15, arrived, 5)
+    add(15, kv_here, 7, 1)
     add(15, rest_y, two, 3)
     add(16, rest_c, one, 2, 0)
+    add(17, kv_here, 1, 2)
     add(17, rest_c, one, 3, 0)
     add(17, rest_x, two, 2)
-    add(18, third_here)
+    add(18, kv_here, 2, 2)
+    add(18, kv_start, 3, 2)
+    add(18, kv_start, 6, 2)
+    add(19, kv_here, 3, 2)
     add(19, rest_c, one, 2, 1)
+    add(20, kv_here, 4, 2)
+    add(20, kv_start, 5, 2)
     add(20, rest_x, two, 3)
-    add(21, arrived, 7)
+    add(21, kv_here, 5, 2)
     add(21, rest_c, one, 3, 1)
+    add(22, kv_here, 6, 2)
+    add(22, kv_start, 7, 2)
     add(22, rest_c, two, 0, 0)
+    add(23, kv_here, 7, 2)
     add(23, rest_c, two, 0, 1)
 
     length = lengths[place.slot]
 
     def p_copy(t, slot):
-        i, p = lax.div(t, PAIRS), lax.rem(t, PAIRS)
+        p, i = lax.div(t, SPAN), lax.rem(t, SPAN)
         return pltpu.make_async_copy(
             pbuf.at[slot], p_out.at[kv_block(i), pl.ds(2 * p, 2)], p_sem.at[slot]
         )
 
-    def kv_copy(i):
-        where = kv_block(i)
-        return pltpu.make_async_copy(kv.at[where], kv_out.at[where], local.at[8 + i])
+    def kv_copy(t):
+        p, i = lax.div(t, SPAN), lax.rem(t, SPAN)
+        where, both = kv_block(i), pl.ds(2 * p, 2)
+        return pltpu.make_async_copy(
+            kv.at[where, both], kv_out.at[where, both], local.at[8 + t]
+        )
 
     steps = SPAN * PAIRS
+    column = lax.broadcasted_iota(jnp.int32, (1, rows), 1) + place.block * rows
+    keep_row = jnp.where(column < length, 1.0, 0.0)
+
+    def to_ctx(p):
+        lanes = pl.ds(p * 128, 128)
+        return send(
+            ctx_tp.at[other_rows, lanes], ctx_in.at[r, :, lanes], single, (2, 5, 6)[p], place.to_x()
+        )
+
+    def context(p):
+        parts = []
+        for h in range(2):
+            g = 2 * p + h
+            lse_out[g] = high[g] + jnp.log(low[g])
+            parts.append(acc[g] / low[g])
+        both = jnp.concatenate(parts, axis=0)
+        ctxt_out[p] = both
+        ctx_tp[:, p * 128 : (p + 1) * 128] = (both * keep_row).T.astype(BF16)
+        to_ctx(p).start()
+        ctx_in[r, :, p * 128 : (p + 1) * 128] = ctx_tp[own_rows, p * 128 : (p + 1) * 128]
+
+    for p in range(PAIRS - 1):
+        add(SPAN * (p + 1), context, p)
 
     def attend(t, carry):
-        i, p = lax.div(t, PAIRS), lax.rem(t, PAIRS)
+        p, i = lax.div(t, SPAN), lax.rem(t, SPAN)
         for step, calls in sorted(events.items()):
 
             @pl.when(t == step)
@@ -512,9 +558,7 @@
                     with jax.named_scope(f"at_{step}"):
                         call()
 
-        @pl.when(p == 0)
-        def _():
-            kv_copy(i).start()
+        kv_copy(t).start()
 
         slot = lax.rem(t, 2)
 
@@ -526,8 +570,8 @@
         place_of = lax.broadcasted_iota(jnp.int32, (rows, 128), 0) + where * rows
         bias = jnp.where(place_of < length, 0.0, MASKED)
         bias = jnp.concatenate([bias] * (rows // 128), axis=1)
-        key = kv[where, p]
-        value_t = kv[where, PAIRS + p].T
+        key = kv[where, 2 * p]
+        value_t = kv[where, 2 * p + 1].T
         for h in range(2):
             g = 2 * p + h
             scores = dot(key, qm[g], NT) + bias
@@ -549,22 +593,9 @@
 
     lax.fori_loop(0, steps, attend, jnp.int32(0))
 
-    column = lax.broadcasted_iota(jnp.int32, (1, rows), 1) + place.block * rows
-    keep = jnp.where(column < length, 1.0, 0.0)
-    for p in range(PAIRS):
-        parts = []
-        for h in range(2):
-            g = 2 * p + h
-            lse_out[g] = high[g] + jnp.log(low[g])
-            parts.append(acc[g] / low[g])
-        both = jnp.concatenate(parts, axis=0)
-        ctxt_out[p] = both
-        ctx_tp[:, p * 128 : (p + 1) * 128] = (both * keep).T.astype(BF16)
+    context(PAIRS - 1)
     for t in (steps - 2, steps - 1):
         p_copy(jnp.int32(t), t % 2).wait()
-    to_ctx = send(ctx_tp.at[other_rows], ctx_in.at[r], single, 2, place.to_x())
-    to_ctx.start()
-    ctx_in[r] = ctx_tp[own_rows, :]
     with jax.named_scope("one_all"):
         rest_all(vec)
         rest_all(one)
@@ -573,7 +604,11 @@
     (b_inner,) = spread_rows(vec_all[...], (8,), FF_HALF // size, 2 * FF_HALF)
     hidden = jnp.concatenate([hid_all[0, own_rows, :], hid_all[1, own_rows, :]], axis=1)
     with jax.named_scope("context"):
-        send(ctx_tp.at[other_rows], ctx_in.at[1 - r], single, 2, place.to_x()).wait_recv()
+        for p in range(PAIRS):
+            lanes = pl.ds(p * 128, 128)
+            send(
+                ctx_tp.at[other_rows, lanes], ctx_in.at[1 - r, :, lanes], single, (2, 5, 6)[p], place.to_x()
+            ).wait_recv()
 
     def weight(ref, h, columns):
         block = ref[h * size : (h + 1) * size, :, columns]
@@ -642,7 +677,7 @@
         return pltpu.make_async_copy(
             ref.at[pl.ds(h * size, size), :, columns],
             g_out.at[pl.ds(h * size, size), :, target],
-            local.at[16 + number],
+            local.at[8 + SPAN * PAIRS + number],
         )
 
     gives = []
@@ -666,9 +701,14 @@
         normed_ref[...] = d_one
         own_out[...] = normed_ref[:, own_col]
     with jax.named_scope("d_context"):
+        to_lay.wait_send()
+        final_out[own_rows, :] = lay_out[r]
         for h in range(2):
             d_context = dot(d_attn, weight(one_all, h, out_cols), NN) * keep
-            d_out[h] = d_context.astype(BF16)
+            lay_out[h] = d_context.astype(BF16)
+        to_d = send(lay_out.at[1 - r], d_out.at[own_rows], single, 4, place.to_x())
+        to_d.start()
+        d_out[own_rows, :] = lay_out[r]
     low_t = low_ref[...].T
     d_attn_t = d_attn.T
     for h in range(2):
@@ -681,19 +721,21 @@
             copy = give(2 + h, one_all, h, pl.ds(0, FIRST), pl.ds(0, FIRST))
             copy.start()
             gives.append(copy)
-    for number in range(1, 8):
-        kv_move(number, 0, n_one).wait_send()
-    to_lay.wait_send()
+    for number in range(1, SPAN):
+        for p in range(PAIRS):
+            kv_move(number, p).wait_send()
     send(lay_far.at[r], lay_far.at[1 - r], single, 3, place.to_x()).wait_recv()
-    final_out[own_rows, :] = lay_out[r]
     final_out[other_rows, :] = lay_far[1 - r]
-    for number in range(3):
-        block = hid if number == 0 else ctx_in.at[0]
-        send(block, block, single, number, place.to_x()).wait_send()
+    send(hid, hid, single, 0, place.to_x()).wait_send()
+    send(ctx_in.at[0], ctx_in.at[0], single, 1, place.to_x()).wait_send()
+    for p in range(PAIRS):
+        to_ctx(p).wait_send()
+    to_d.wait_send()
+    send(lay_out.at[1 - r], d_out.at[other_rows], single, 4, place.to_x()).wait_recv()
     for copy in [hid_local, wq_local, q_local] + gives:
         copy.wait()
-    for i in range(SPAN):
-        kv_copy(jnp.int32(i)).wait()
+    for t in range(SPAN * PAIRS):
+        kv_copy(jnp.int32(t)).wait()
 
 
 def forward_attention(size, lengths, hid, qkv_weights, rest_weights, vec, cot):
@@ -722,7 +764,7 @@
             shape((rows, HALF), BF16),
             shape((2, part, HALF), BF16),
             shape((part, HALF), F32),
-            shape((2, part, HALF), BF16),
+            shape((rows, HALF), BF16),
             shape((16, D), F32),
         ),
         in_specs=[pl.BlockSpec(memory_space=pltpu.SMEM)] + [vmem] * 9,
@@ -761,11 +803,11 @@
             dma((n_col,)),
             dma((n_all,)),
             dma((n_all,)),
-            dma((8,)),
-            dma((8,)),
-            dma((4,)),
-            dma((4,)),
-            dma((20,)),
+            dma((SPAN * PAIRS,)),
+            dma((SPAN * PAIRS,)),
+            dma((7,)),
+            dma((7,)),
+            dma((12 + SPAN * PAIRS,)),
             dma((2,)),
         ],
         compiler_params=pltpu.CompilerParams(
@@ -777,7 +819,7 @@
 
 def kernel_c(
     size,
-    dctx,
+    d_ctx,
     qs,
     m_in,
     lse_in,
@@ -799,7 +841,6 @@
     small_out,
     bias_out,
     grad_out,
-    d_ctx,
     dtot,
     delta,
     qm,
@@ -849,7 +890,6 @@
     half = size // 2
     blk = wq_all.shape[1]
     own_rows = pl.ds(pl.multiple_of(r * part, part), part)
-    other_rows = pl.ds(pl.multiple_of((1 - r) * part, part), part)
 
     def b_block(i):
         pair, core = lax.div(i, 2), lax.rem(j + 1 + lax.rem(i, 2), 2)
@@ -884,8 +924,8 @@
 
         lax.fori_loop(0, count, step, jnp.int32(0))
 
-    needed = [(0, 1, 0), (0, 2, 0), (1, 2, 0), (0, 1, 1), (0, 3, 0), (0, 3, 1), (0, 2, 1), (1, 2, 1)]
-    needed += [(1, 1, 0), (1, 1, 1), (0, 0, 0), (0, 0, 1), (1, 3, 0), (1, 3, 1), (1, 0, 0), (1, 0, 1)]
+    needed = [(0, 2, 0), (0, 1, 0), (0, 2, 1), (1, 1, 0), (0, 3, 0), (0, 3, 1), (1, 2, 0), (1, 2, 1)]
+    needed += [(0, 1, 1), (1, 1, 1), (0, 0, 0), (0, 0, 1), (1, 3, 0), (1, 3, 1), (1, 0, 0), (1, 0, 1)]
     needed = [index(*at) for at in needed]
     p_load(jnp.int32(0), 0).start()
     for at in needed[:4]:
@@ -901,100 +941,10 @@
     acc[...] = jnp.zeros_like(acc)
     for which in range(2):
         hid_t[which] = hid_all[which].T
-    d_ctx[own_rows, :] = dctx[r]
     far[...] = jnp.zeros_like(far)
     far[own_rows, :] = dres_low[1 - r].astype(F32)
     grad_out[...] = jnp.zeros_like(grad_out)
     grad_out[own_rows, :] = dres_own[...]
-    with jax.named_scope("meet"):
-        meet(place)
-    single = (one_send, one_recv)
-    gs = (g_send, g_recv)
-    ks = (kv_send, kv_recv)
-    at_x, at_y, at_z = 4 * n, 6 * n, 8 * n
-
-    send(dctx.at[1 - r], d_ctx.at[own_rows], single, 0, place.to_x()).start()
-    send(small_in, vec_got.at[0], (v_send, v_recv), 0, place.to_x()).start()
-
-    def c_move(at):
-        return send(g_in.at[g_block(at, 1 - j)], b1.at[at], gs, at, place.to_core())
-
-    for at in needed:
-        c_move(at).start()
-
-    def fold(target, source, at):
-        total = target[at].astype(F32) + source.astype(F32)
-        target[at] = total.astype(BF16)
-
-    def pieces(p):
-        return pl.ds(2 * p, 2)
-
-    def core_send(p, pair):
-        return send(
-            big.at[2 * pair, pieces(p)], cb.at[pair, pieces(p)], ks, 4 * p + pair, place.to_core()
-        )
-
-    def core_add(p, pair):
-        core_send(p, pair).wait_recv()
-        for piece in (2 * p, 2 * p + 1):
-            fold(big, cb[pair, piece], (2 * pair + 1, piece))
-
-    def hop(p, pair):
-        peer = place.to_y() if pair == 2 else place.to_z_near()
-        number = 4 * PAIRS + 3 * p + pair
-        return send(big.at[2 * pair + 1, pieces(p)], rb.at[pair, pieces(p)], ks, number, peer)
-
-    def hop_add(p):
-        hop(p, 0).wait_recv()
-        for piece in (2 * p, 2 * p + 1):
-            fold(big, rb[0, piece], (5, piece))
-
-    def g_core_add(other, k, m):
-        at = index(other, k, m)
-        c_move(at).wait_recv()
-        g_load(at).wait()
-        fold(st, b1[at], at)
-
-    def gx(k, m):
-        at = index(0, k, m)
-        return send(st.at[at], b2.at[at], gs, at_x + at, place.to_x())
-
-    def gx_add(k, m):
-        gx(k, m).wait_recv()
-        fold(st, b2[index(0, k, m)], index(1, k, m))
-
-    def gy(k, other):
-        slot = 2 * k + other
-        return send(st.at[index(other, k, 0)], b3.at[slot], gs, at_y + slot, place.to_y())
-
-    def gy_add(k, other):
-        gy(k, other).wait_recv()
-        fold(st, b3[2 * k + other], index(other, k, 1))
-
-    def gz(k):
-        return send(st.at[index(1, k, 1)], b4.at[k - 1], gs, at_z + k - 1, place.to_z(k))
-
-    vz = (v_send, v_recv)
-
-    def vector(number):
-        level = min(number, 3)
-        step = max(number - 2, 1)
-        peer = (place.to_x(), place.to_core(), place.to_y(), place.to_z(step))[level]
-        source = small_in if level == 0 else vec_sum.at[level - 1]
-        return send(source, vec_got.at[number], vz, number, peer)
-
-    def vector_add(level):
-        vector(level).wait_recv()
-        before = small_in[...] if level == 0 else vec_sum[level - 1]
-        vec_sum[level] = before + vec_got[level]
-
-    with jax.named_scope("first_adds"):
-        g_core_add(0, 1, 0)
-        gx(1, 0).start()
-        g_core_add(0, 2, 0)
-        gy(2, 0).start()
-    with jax.named_scope("context_row"):
-        send(dctx.at[1 - r], d_ctx.at[other_rows], single, 0, place.to_x()).wait_recv()
     upper = lax.broadcasted_iota(jnp.int32, (128, rows), 0) < HEAD_DIM
     for p in range(PAIRS):
         turned = d_ctx[:, p * 128 : (p + 1) * 128].astype(F32).T
@@ -1003,9 +953,86 @@
         delta[2 * p + 1] = jnp.sum(product[HEAD_DIM:], axis=0, keepdims=True)
         dtot[2 * p] = jnp.where(upper, turned, 0.0)
         dtot[2 * p + 1] = jnp.where(upper, 0.0, turned)
-    with jax.named_scope("vector_row"):
-        vector_add(0)
-        vector(1).start()
+    with jax.named_scope("meet"):
+        meet(place)
+    single = (one_send, one_recv)
+    gs = (g_send, g_recv)
+    ks = (kv_send, kv_recv)
+    at_x, at_y, at_z = 4 * n, 6 * n, 8 * n
+
+    send(small_in, vec_got.at[0], (v_send, v_recv), 0, place.to_x()).start()
+
+    def c_move(at):
+        return send(g_in.at[g_block(at, 1 - j)], b1.at[at], gs, at, place.to_core())
+
+    for at in needed:
+        c_move(at).start()
+
+    def fold(target, source, at):
+        total = target[at].astype(F32) + source.astype(F32)
+        target[at] = total.astype(BF16)
+
+    def pieces(p):
+        return pl.ds(2 * p, 2)
+
+    def core_send(p, pair):
+        return send(
+            big.at[2 * pair, pieces(p)], cb.at[pair, pieces(p)], ks, 4 * p + pair, place.to_core()
+        )
+
+    def core_add(p, pair):
+        core_send(p, pair).wait_recv()
+        for piece in (2 * p, 2 * p + 1):
+            fold(big, cb[pair, piece], (2 * pair + 1, piece))
+
+    def hop(p, pair):
+        peer = place.to_y() if pair == 2 else place.to_z_near()
+        number = 4 * PAIRS + 3 * p + pair
+        return send(big.at[2 * pair + 1, pieces(p)], rb.at[pair, pieces(p)], ks, number, peer)
+
+    def hop_add(p):
+        hop(p, 0).wait_recv()
+        for piece in (2 * p, 2 * p + 1):
+            fold(big, rb[0, piece], (5, piece))
+
+    def g_core_add(other, k, m):
+        at = index(other, k, m)
+        c_move(at).wait_recv()
+        g_load(at).wait()
+        fold(st, b1[at], at)
+
+    def gx(k, m):
+        at = index(0, k, m)
+        return send(st.at[at], b2.at[at], gs, at_x + at, place.to_x())
+
+    def gx_add(k, m):
+        gx(k, m).wait_recv()
+        fold(st, b2[index(0, k, m)], index(1, k, m))
+
+    def gy(k, other):
+        slot = 2 * k + other
+        return send(st.at[index(other, k, 0)], b3.at[slot], gs, at_y + slot, place.to_y())
+
+    def gy_add(k, other):
+        gy(k, other).wait_recv()
+        fold(st, b3[2 * k + other], index(other, k, 1))
+
+    def gz(k):
+        return send(st.at[index(1, k, 1)], b4.at[k - 1], gs, at_z + k - 1, place.to_z(k))
+
+    vz = (v_send, v_recv)
+
+    def vector(number):
+        level = min(number, 3)
+        step = max(number - 2, 1)
+        peer = (place.to_x(), place.to_core(), place.to_y(), place.to_z(step))[level]
+        source = small_in if level == 0 else vec_sum.at[level - 1]
+        return send(source, vec_got.at[number], vz, number, peer)
+
+    def vector_add(level):
+        vector(level).wait_recv()
+        before = small_in[...] if level == 0 else vec_sum[level - 1]
+        vec_sum[level] = before + vec_got[level]
 
     qz = (q_send, q_recv)
 
@@ -1079,37 +1106,42 @@
         add(step, lambda: what(*inputs).start())
 
     bias_own[0, 2:8] = jnp.zeros((6, HALF), F32)
-    add(0, g_core_add, 0, 1, 1)
-    add(0, g_core_add, 1, 2, 0)
-    start(1, gx, 1, 1)
-    start(1, gy, 2, 1)
-    add(1, g_core_add, 0, 3, 0)
-    add(2, g_core_add, 0, 3, 1)
-    late = [(1, 1, 0), (1, 1, 1), (0, 2, 1), (1, 2, 1), (0, 0, 0), (0, 0, 1), (1, 3, 0), (1, 3, 1)]
+    add(0, g_core_add, 0, 2, 0)
+    start(0, gx, 2, 0)
+    add(0, g_core_add, 0, 1, 0)
+    start(0, gy, 1, 0)
+    add(1, g_core_add, 0, 2, 1)
+    add(1, g_core_add, 1, 1, 0)
+    start(2, gx, 2, 1)
+    start(2, gy, 1, 1)
+    add(2, g_core_add, 0, 3, 0)
+    add(3, vector_add, 0)
+    start(3, vector, 1)
+    start(3, gx, 3, 0)
+    add(3, g_core_add, 0, 3, 1)
+    late = [(1, 2, 0), (1, 2, 1), (0, 1, 1), (1, 1, 1), (0, 0, 0), (0, 0, 1), (1, 3, 0), (1, 3, 1)]
     for at, what in enumerate(late + [(1, 0, 0), (1, 0, 1)]):
-        add(3 + at, g_core_add, *what)
-    start(2, gx, 3, 0)
-    add(5, vector_add, 1)
-    start(5, vector, 2)
-    add(7, gy_add, 2, 0)
-    add(7, gx_add, 1, 0)
-    add(7, gx_add, 1, 1)
-    start(8, gy, 1, 1)
-    add(8, gy_add, 2, 1)
-    start(9, gx, 2, 1)
-    start(9, gx, 3, 1)
-    start(9, gx, 0, 0)
-    start(10, gx, 0, 1)
-    add(10, vector_add, 2)
+        add(4 + at, g_core_add, *what)
+    add(6, vector_add, 1)
+    start(6, vector, 2)
+    add(8, gx_add, 2, 0)
+    add(8, gy_add, 1, 0)
+    add(9, gx_add, 2, 1)
+    start(9, gy, 2, 1)
+    add(9, gy_add, 1, 1)
+    start(10, gx, 1, 1)
+    start(10, gx, 3, 1)
+    start(10, gx, 0, 0)
+    start(11, gx, 0, 1)
+    add(11, vector_add, 2)
     for step in range(1, n):
-        start(10, vector, 2 + step)
-    add(15, gy_add, 1, 1)
-    start(15, gz, 1)
-    add(17, gx_add, 2, 1)
-    add(18, gx_add, 3, 0)
-    add(18, gx_add, 3, 1)
-    start(18, gy, 3, 1)
-    start(22, gz, 2)
+        start(11, vector, 2 + step)
+    add(15, gy_add, 2, 1)
+    start(15, gz, 2)
+    add(18, gx_add, 1, 1)
+    add(19, gx_add, 3, 0)
+    add(19, gx_add, 3, 1)
+    start(19, gy, 3, 1)
     for p in range(PAIRS):
         base = SPAN * p
         late = 7 if p == PAIRS - 1 else 8
@@ -1131,8 +1163,6 @@
             add(base + 15, far_term, p)
             add(base + 15, own_term, p)
             add(base + 15, q_core_add, p)
-    add(23, gy_add, 3, 1)
-    start(23, gz, 3)
 
     steps = SPAN * PAIRS
 
@@ -1159,8 +1189,8 @@
 
         p_load(t, slot).wait()
         where = b_block(i)
-        key = kv[i, p]
-        value = kv[i, PAIRS + p]
+        key = kv[i, 2 * p]
+        value = kv[i, 2 * p + 1]
         key_t = key.T
         d_key = d_value = None
         for h in range(2):
@@ -1184,6 +1214,7 @@
     last = PAIRS - 1
     for call in events[steps]:
         call()
+    gz(1).start()
     q_side(0).start()
     q_side(1).start()
     with jax.named_scope("settle"):
@@ -1191,7 +1222,7 @@
     with jax.named_scope("far"):
         far_term(last)
         near[0] = far[...].astype(BF16)
-    to_near = send(near.at[0], near.at[1], single, 3, place.to_x())
+    to_near = send(near.at[0], near.at[1], single, 0, place.to_x())
     with jax.named_scope("grads"):
         grads(last)
     to_near.start()
@@ -1216,6 +1247,9 @@
         gx_add(0, 0)
         gx_add(0, 1)
     gy(0, 1).start()
+    with jax.named_scope("g_y_3"):
+        gy_add(3, 1)
+    gz(3).start()
     with jax.named_scope("q_side_0"):
         q_side_add(0)
         q_planes(0)
@@ -1275,7 +1309,7 @@
     for at in range(4 * n):
         c_move(at).wait_send()
     for k in range(n):
-        first = (2,) if k == 2 else ()
+        first = k == 1
         for m in range(2):
             if not first or m == 1:
                 gx(k, m).wait_send()
@@ -1298,7 +1332,6 @@
         for pair in range(3):
             hop(p, pair).wait_send()
     to_near.wait_send()
-    send(dctx.at[1 - r], d_ctx.at[own_rows], single, 0, place.to_x()).wait_send()
 
 
 def backward_attention(
@@ -1330,7 +1363,6 @@
         in_specs=[vmem] * 10 + [any_space] * 3,
         out_specs=[vmem] * 9,
         scratch_shapes=[
-            scratch((rows, HALF), BF16),
             scratch((2 * PAIRS, 128, rows), F32),
             scratch((2 * PAIRS, 1, rows), F32),
             scratch((2 * PAIRS, rows, 128), BF16),
@@ -1357,8 +1389,8 @@
             scratch((n + 1, 8, HALF), F32),
             scratch((3, 16, D), F32),
             scratch((n + 2, 16, D), F32),
-            dma((4,)),
-            dma((4,)),
+            dma((1,)),
+            dma((1,)),
             dma((7 * PAIRS,)),
             dma((7 * PAIRS,)),
             dma((g_count,)),

time: 222 us -> 209 us (0.941)
  Pallas kernels: 217 us -> 204 us
    pallas_call x1, Pallas kernels: 102 us -> 92.8 us  [backward_attention(): pl.pallas_call(functools.partial(kernel_c, size), out_shape=(shape((blk,...]
    pallas_call x1, Pallas kernels: 112 us -> 108 us  [forward_attention(): pl.pallas_call(functools.partial(kernel_a, size), out_shape=(shape((2, ro...]
where the time goes in v4:
time: 209 us
  Pallas kernels  204 us (98%)
  local copies, waits for them, and re-layouts  2.66 us (1%)
    pallas_call x1, Pallas kernels, forward_attention(): pl.pallas_call(functools.partial(kernel_a, size), out_shape=(shape((2, ro...  108 us
    pallas_call x1, Pallas kernels, backward_attention(): pl.pallas_call(functools.partial(kernel_c, size), out_shape=(shape((blk,...  92.8 us

profile of v4, /device:TPU:0, one launch (start us, length us, event | category | flops | bytes accessed | tf_op | source)
XLA Modules:
  0.0 208.6 jit_solution(18349970216701568963)
XLA Ops:
  0.7 1.4 pad_add_fusion.vec_in
  2.1 108.2 %forward_attention.1 = (bf16[2,512,384]{2,1,0:T(8,128)(2,1)}, bf16[16,48,1152]{2,1,0:T(8,128)(2,1)}, bf16[3,512,128]{2,1,0:T(8,128)(2,1)}, bf16[8,6,512,128]{3,2...) custom-call(s32[2]{0:T(128)} %lengths.1, ...), custom_call_target="tpu_custom_call" | custom-call | tf_op jit(solution)/shard_map/forward_attention/pallas_call | solution.py:752
  110.3 92.8 %backward_attention.1 = (f32[48,384]{1,0:T(8,128)}, f32[48,384]{1,0:T(8,128)}, f32[48,384]{1,0:T(8,128)}, f32[48,384]{1,0:T(8,128)}, f32[48,1536]{1,0:T(8,128)},...) custom-call(bf16[512,384]{1,0:T(8,128)(2,1)} %get-tuple-element.49.d_ctx, ...), custom_call_target="tpu_custom_call" | custom-call | tf_op jit(solution)/shard_map/backward_attention/pallas_call | solution.py:1350
  203.1 2.7 %finish.1 = (f32[48,384]{1,0:T(8,128)}, f32[48,384]{1,0:T(8,128)}, f32[48,384]{1,0:T(8,128)}, f32[48,384]{1,0:T(8,128)}, f32[48,1536]{1,0:T(8,128)}, /*index=5*/...) custom-call(f32[16,768]{1,0:T(8,128)} %get-tuple-element.62.refs_0_, ...), custom_call_target="tpu_custom_call" | custom-call | tf_op jit(solution)/shard_map/finish/pallas_call | solution.py:1450
  205.8 1.2 slice_bitcast_fusion.5
  207.0 1.5 slice_bitcast_fusion

commit v5 on v4

--- a/solution.py
+++ b/solution.py
@@ -212,8 +212,24 @@
     return result, sums, jnp.sum(incoming, axis=0, keepdims=True)
 
 
+def staged(kernel, size, inputs, outputs, picks, *refs):
+    results, rest = list(refs[inputs : inputs + outputs]), refs[inputs + outputs :]
+    held, sems, rest = rest[: len(picks)], rest[len(picks)], rest[len(picks) + 1 :]
+    targets = [results[at] for at in picks]
+    for at, ref in zip(picks, held):
+        results[at] = ref
+
+    def leave(number):
+        return pltpu.make_async_copy(held[number], targets[number], sems.at[number])
+
+    kernel(size, leave, *refs[:inputs], *results, *rest)
+    for number in range(len(picks)):
+        leave(number).wait()
+
+
 def kernel_a(
     size,
+    leave,
     lengths,
     hid,
     w_query,
@@ -445,21 +461,21 @@
         events.setdefault(step, []).append(functools.partial(what, *inputs))
 
     add(1, kv_here, 1, 0)
-    add(1, vec_rows)
-    add(2, rest_x, one, 1)
     add(2, kv_here, 2, 0)
     add(2, kv_start, 3, 0)
     add(2, kv_start, 6, 0)
     add(3, kv_here, 3, 0)
+    add(3, rest_x, one, 1)
     add(3, rest_y, one, 2)
+    add(3, two_start)
     add(4, kv_here, 4, 0)
     add(4, kv_start, 5, 0)
     add(4, rest_y, one, 3)
     add(5, kv_here, 5, 0)
-    add(5, two_start)
     add(5, kv_start, 2, 1)
     add(5, kv_start, 4, 1)
     add(5, kv_start, 1, 1)
+    add(5, vec_rows)
     add(6, kv_here, 6, 0)
     add(6, kv_start, 7, 0)
     add(6, rest_x, two, 0)
@@ -594,6 +610,8 @@
     lax.fori_loop(0, steps, attend, jnp.int32(0))
 
     context(PAIRS - 1)
+    for number in range(3):
+        leave(number).start()
     for t in (steps - 2, steps - 1):
         p_copy(jnp.int32(t), t % 2).wait()
     with jax.named_scope("one_all"):
@@ -700,6 +718,8 @@
             low_out[h] = d_attn[:, h * HALF : (h + 1) * HALF]
         normed_ref[...] = d_one
         own_out[...] = normed_ref[:, own_col]
+        for number in (4, 5, 7):
+            leave(number).start()
     with jax.named_scope("d_context"):
         to_lay.wait_send()
         final_out[own_rows, :] = lay_out[r]
@@ -726,12 +746,14 @@
             kv_move(number, p).wait_send()
     send(lay_far.at[r], lay_far.at[1 - r], single, 3, place.to_x()).wait_recv()
     final_out[other_rows, :] = lay_far[1 - r]
+    leave(3).start()
     send(hid, hid, single, 0, place.to_x()).wait_send()
     send(ctx_in.at[0], ctx_in.at[0], single, 1, place.to_x()).wait_send()
     for p in range(PAIRS):
         to_ctx(p).wait_send()
     to_d.wait_send()
     send(lay_out.at[1 - r], d_out.at[other_rows], single, 4, place.to_x()).wait_recv()
+    leave(6).start()
     for copy in [hid_local, wq_local, q_local] + gives:
         copy.wait()
     for t in range(SPAN * PAIRS):
@@ -749,27 +771,31 @@
     n_col, n_all = (n - 1) + n + 2 * n, (n - 1) + n + 2 * n + 4 * n
     dma = pltpu.SemaphoreType.DMA
     scratch = pltpu.VMEM
+    results = (
+        shape((2, rows, HALF), BF16),
+        shape((size, blk, QKV), BF16),
+        shape((PAIRS, rows, 128), BF16),
+        shape((SPAN, 2 * PAIRS, rows, 128), BF16),
+        shape((SPAN, 2 * PAIRS, rows, rows), BF16),
+        shape((SPAN, 2 * PAIRS, 1, rows), F32),
+        shape((2 * PAIRS, 1, rows), F32),
+        shape((PAIRS, 128, rows), F32),
+        shape((2 * size, blk, REST), BF16),
+        shape((rows, HALF), BF16),
+        shape((2, part, HALF), BF16),
+        shape((part, HALF), F32),
+        shape((rows, HALF), BF16),
+        shape((16, D), F32),
+    )
+    picks = (5, 6, 7, 9, 10, 11, 12, 13)
     return pl.pallas_call(
-        functools.partial(kernel_a, size),
-        out_shape=(
-            shape((2, rows, HALF), BF16),
-            shape((size, blk, QKV), BF16),
-            shape((PAIRS, rows, 128), BF16),
-            shape((SPAN, 2 * PAIRS, rows, 128), BF16),
-            shape((SPAN, 2 * PAIRS, rows, rows), BF16),
-            shape((SPAN, 2 * PAIRS, 1, rows), F32),
-            shape((2 * PAIRS, 1, rows), F32),
-            shape((PAIRS, 128, rows), F32),
-            shape((2 * size, blk, REST), BF16),
-            shape((rows, HALF), BF16),
-            shape((2, part, HALF), BF16),
-            shape((part, HALF), F32),
-            shape((rows, HALF), BF16),
-            shape((16, D), F32),
-        ),
+        functools.partial(staged, kernel_a, size, 10, len(results), picks),
+        out_shape=results,
         in_specs=[pl.BlockSpec(memory_space=pltpu.SMEM)] + [vmem] * 9,
-        out_specs=[any_space] * 5 + [vmem] * 3 + [any_space] + [vmem] * 5,
-        scratch_shapes=[
+        out_specs=[any_space] * len(results),
+        scratch_shapes=[scratch(results[at].shape, results[at].dtype) for at in picks]
+        + [dma((len(picks),))]
+        + [
             scratch((2, rows, HALF), BF16),
             scratch((blk, QKV), BF16),
             scratch((size, blk, QKV), BF16),
@@ -819,6 +845,7 @@
 
 def kernel_c(
     size,
+    leave,
     d_ctx,
     qs,
     m_in,
@@ -1269,6 +1296,7 @@
             vector(2 + step).wait_recv()
             total = total + vec_got[2 + step]
         small_out[...] = total
+        leave(6).start()
 
     def q_out(p):
         total = gq[p, j, y, place.z].astype(F32)
@@ -1285,6 +1313,7 @@
     with jax.named_scope("near_wait"):
         to_near.wait_recv()
         grad_out[...] = grad_out[...] + near[1].astype(F32)
+        leave(8).start()
     with jax.named_scope("g_z"):
         total = None
         for k in range(1, n):
@@ -1297,14 +1326,19 @@
         wo_out[...] = total[:, :HALF]
         wi_out[...] = total[:, HALF:FIRST]
         wu_out[...] = total[:, FIRST:]
+        for number in (3, 4, 5):
+            leave(number).start()
     with jax.named_scope("q_out"):
         q_out(1)
         q_out(last)
+        for number in range(3):
+            leave(number).start()
         total = bias_own[2]
         for step in range(1, n):
             small(1 + step).wait_recv()
             total = total + bias_got[1 + step]
         bias_out[...] = total
+        leave(7).start()
 
     for at in range(4 * n):
         c_move(at).wait_send()
@@ -1347,22 +1381,25 @@
     dma = pltpu.SemaphoreType.DMA
     scratch = pltpu.VMEM
     g_count, q_count = 4 * n + 2 * n + 2 * n + n - 1, PAIRS * (n + 1)
+    results = (
+        shape((blk, HALF), F32),
+        shape((blk, HALF), F32),
+        shape((blk, HALF), F32),
+        shape((blk, HALF), F32),
+        shape((blk, FF_HALF), F32),
+        shape((blk, FF_HALF), F32),
+        shape((16, D), F32),
+        shape((8, HALF), F32),
+        shape((rows, HALF), F32),
+    )
     return pl.pallas_call(
-        functools.partial(kernel_c, size),
-        out_shape=(
-            shape((blk, HALF), F32),
-            shape((blk, HALF), F32),
-            shape((blk, HALF), F32),
-            shape((blk, HALF), F32),
-            shape((blk, FF_HALF), F32),
-            shape((blk, FF_HALF), F32),
-            shape((16, D), F32),
-            shape((8, HALF), F32),
-            shape((rows, HALF), F32),
-        ),
+        functools.partial(staged, kernel_c, size, 13, len(results), range(len(results))),
+        out_shape=results,
         in_specs=[vmem] * 10 + [any_space] * 3,
-        out_specs=[vmem] * 9,
-        scratch_shapes=[
+        out_specs=[any_space] * len(results),
+        scratch_shapes=[scratch(a.shape, a.dtype) for a in results]
+        + [dma((len(results),))]
+        + [
             scratch((2 * PAIRS, 128, rows), F32),
             scratch((2 * PAIRS, 1, rows), F32),
             scratch((2 * PAIRS, rows, 128), BF16),
@@ -1412,12 +1449,12 @@
 
 
 def kernel_d(size, per, count, *refs):
-    sources, targets = refs[:count], refs[count : 2 * count - 1]
-    held, tile, come, go = refs[2 * count - 1 : 3 * count - 1], refs[-3], refs[-2], refs[-1]
+    sources, targets = refs[:count], refs[count : 2 * count - 2]
+    vectors = refs[2 * count - 2 : 2 * count + 7]
+    held, come, go = refs[2 * count + 7 : 3 * count + 7], refs[-2], refs[-1]
     small, bias = held[0], held[1]
     loads = [pltpu.make_async_copy(s, h, come.at[at]) for at, (s, h) in enumerate(zip(sources, held))]
-    done = list(held[2:]) + [tile]
-    stores = [pltpu.make_async_copy(h, t, go.at[at]) for at, (h, t) in enumerate(zip(done, targets))]
+    stores = [pltpu.make_async_copy(h, t, go.at[at]) for at, (h, t) in enumerate(zip(held[2:], targets))]
     for copy in loads:
         copy.start()
     loads[0].wait()
@@ -1426,15 +1463,17 @@
     inside = lax.rem(lax.axis_index("col"), size)
     start = row * HALF + inside * per
     lines = small[...]
-    tile[0:6] = pltpu.roll(lines, D - start, 1)[0:6, :128]
+    turned = pltpu.roll(lines, D - start, 1)
+    for at in range(6):
+        vectors[at][...] = turned[at, :per]
     spot = inside * 4 * per
     hidden = pltpu.roll(lines, D - lax.rem(spot, D), 1)[:, :128]
     wanted = 6 + 2 * row + lax.div(spot, D)
     line = lax.broadcasted_iota(jnp.int32, hidden.shape, 0)
-    tile[6:7] = jnp.sum(jnp.where(line == wanted, hidden, 0.0), axis=0, keepdims=True)
-    tile[7:9] = pltpu.roll(bias[...], HALF - inside * per, 1)[0:2, :128]
-    tile[9:16] = jnp.zeros((7, 128), F32)
-    stores[-1].start()
+    vectors[6][...] = jnp.sum(jnp.where(line == wanted, hidden, 0.0), axis=0)[: 4 * per]
+    turned = pltpu.roll(bias[...], HALF - inside * per, 1)
+    for at in range(2):
+        vectors[7 + at][...] = turned[at, :per]
     for load, store in zip(loads[2:], stores):
         load.wait()
         store.start()
@@ -1449,11 +1488,11 @@
     count = len(arrays)
     return pl.pallas_call(
         functools.partial(kernel_d, size, HALF // size, count),
-        out_shape=shapes + [jax.ShapeDtypeStruct((16, 128), F32)],
+        out_shape=shapes
+        + [jax.ShapeDtypeStruct((HALF // size * (4 if at == 6 else 1),), F32) for at in range(9)],
         in_specs=[space] * count,
-        out_specs=[space] * (count - 1),
+        out_specs=[space] * (count - 2) + [pl.BlockSpec(memory_space=pltpu.VMEM)] * 9,
         scratch_shapes=[pltpu.VMEM(a.shape, a.dtype) for a in arrays]
-        + [pltpu.VMEM((16, 128), F32)]
         + [pltpu.SemaphoreType.DMA((count,))] * 2,
         compiler_params=pltpu.CompilerParams(vmem_limit_bytes=63 * 2**20),
         name="finish",
@@ -1515,10 +1554,9 @@
         return lax.psum_scatter(whole, "col", scatter_dimension=0, tiled=True)
 
     arrays = [g_query, g_key, g_value, g_output, g_inner, g_outer, grad_in, layer_out]
-    *arrays, tile = finish(size, g_small, g_bias, arrays)
-    g_query, g_key, g_value, g_output, g_inner, g_outer, grad_in, layer_out = arrays
-    per = HALF // size
-    pieces = [spread(tile[at, : 4 * per if at == 6 else per]) for at in range(9)]
+    arrays = finish(size, g_small, g_bias, arrays)
+    g_query, g_key, g_value, g_output, g_inner, g_outer, grad_in, layer_out = arrays[:8]
+    pieces = [spread(piece) for piece in arrays[8:]]
     g_b_output, g_b_outer, g_gain_one, g_shift_one, g_gain_two, g_shift_two = pieces[:6]
     g_b_inner, g_b_query, g_b_value = pieces[6:]
     return (

time: 209 us -> 205 us (0.981)
  local copies, waits for them, and re-layouts: 2.66 us -> 0 us
    squeeze x2 -> x0, local copies, waits for them, and re-layouts: 2.66 us -> none  [per_device(): pieces = [spread(tile[at, :4 * per if at == 6 else per]) for at in range(9)]]
where the time goes in v5:
time: 205 us
  Pallas kernels  202 us (99%)
    pallas_call x1, Pallas kernels, forward_attention(): pl.pallas_call(functools.partial(staged, kernel_a, size, 10, len(results)...  109 us
    pallas_call x1, Pallas kernels, backward_attention(): pl.pallas_call(functools.partial(staged, kernel_c, size, 13, len(results)...  90.4 us

profile of v5, /device:TPU:0, one launch (start us, length us, event | category | flops | bytes accessed | tf_op | source)
XLA Modules:
  0.0 204.5 jit_solution(16033168927732835424)
XLA Ops:
  0.7 1.4 pad_add_fusion.refs_8_
  2.1 108.6 %forward_attention.1 = (bf16[2,512,384]{2,1,0:T(8,128)(2,1)}, bf16[16,48,1152]{2,1,0:T(8,128)(2,1)}, bf16[3,512,128]{2,1,0:T(8,128)(2,1)}, bf16[8,6,512,128]{3,2...) custom-call(s32[2]{0:T(128)} %refs_0_.1, ...), custom_call_target="tpu_custom_call" | custom-call | tf_op jit(solution)/shard_map/forward_attention/pallas_call | solution.py:791
  110.7 90.4 %backward_attention.1 = (f32[48,384]{1,0:T(8,128)}, f32[48,384]{1,0:T(8,128)}, f32[48,384]{1,0:T(8,128)}, f32[48,384]{1,0:T(8,128)}, f32[48,1536]{1,0:T(8,128)},...) custom-call(bf16[512,384]{1,0:T(8,128)(2,1)} %get-tuple-element.57.refs_0_, ...), custom_call_target="tpu_custom_call" | custom-call | tf_op jit(solution)/shard_map/backward_attention/pallas_call | solution.py:1395
  201.1 3.2 %finish.1 = (f32[48,384]{1,0:T(8,128)}, f32[48,384]{1,0:T(8,128)}, f32[48,384]{1,0:T(8,128)}, f32[48,384]{1,0:T(8,128)}, f32[48,1536]{1,0:T(8,128)}, /*index=5*/...) custom-call(f32[16,768]{1,0:T(8,128)} %get-tuple-element.70.refs_0_,, ...), custom_call_target="tpu_custom_call" | custom-call | tf_op jit(solution)/shard_map/finish/pallas_call | solution.py:1489

commit v6 on v5

--- a/solution.py
+++ b/solution.py
@@ -852,7 +852,7 @@
     lse_in,
     ctxt,
     hid_all,
-    wq_all,
+    wq_in,
     dres_low,
     dres_own,
     small_in,
@@ -868,6 +868,7 @@
     small_out,
     bias_out,
     grad_out,
+    wq_all,
     dtot,
     delta,
     qm,
@@ -960,6 +961,8 @@
     loop(SPAN, lambda i: kv_load(i).start())
     for at in needed[4:]:
         g_load(at).start()
+    wq_load = pltpu.make_async_copy(wq_in, wq_all, load.at[8 + 4 * n])
+    wq_load.start()
     lane = lax.broadcasted_iota(jnp.int32, (rows, 128), 1)
     for p in range(PAIRS):
         piece = qs[p]
@@ -1133,6 +1136,7 @@
         add(step, lambda: what(*inputs).start())
 
     bias_own[0, 2:8] = jnp.zeros((6, HALF), F32)
+    add(14, wq_load.wait)
     add(0, g_core_add, 0, 2, 0)
     start(0, gx, 2, 0)
     add(0, g_core_add, 0, 1, 0)
@@ -1395,11 +1399,12 @@
     return pl.pallas_call(
         functools.partial(staged, kernel_c, size, 13, len(results), range(len(results))),
         out_shape=results,
-        in_specs=[vmem] * 10 + [any_space] * 3,
+        in_specs=[vmem] * 6 + [any_space] + [vmem] * 3 + [any_space] * 3,
         out_specs=[any_space] * len(results),
         scratch_shapes=[scratch(a.shape, a.dtype) for a in results]
         + [dma((len(results),))]
         + [
+            scratch(wq_all.shape, BF16),
             scratch((2 * PAIRS, 128, rows), F32),
             scratch((2 * PAIRS, 1, rows), F32),
             scratch((2 * PAIRS, rows, 128), BF16),

time: 205 us -> 204 us (level)
  no operation moved by 1% of the time
where the time goes in v6:
time: 204 us
  Pallas kernels  202 us (99%)
    pallas_call x1, Pallas kernels, forward_attention(): pl.pallas_call(functools.partial(staged, kernel_a, size, 10, len(results)...  109 us
    pallas_call x1, Pallas kernels, backward_attention(): pl.pallas_call(functools.partial(staged, kernel_c, size, 13, len(results)...  89.9 us

profile of v6, /device:TPU:0, one launch (start us, length us, event | category | flops | bytes accessed | tf_op | source)
XLA Modules:
  0.0 204.0 jit_solution(8257764328263573862)
XLA Ops:
  0.7 1.4 pad_add_fusion.refs_8_
  2.1 108.6 %forward_attention.1 = (bf16[2,512,384]{2,1,0:T(8,128)(2,1)}, bf16[16,48,1152]{2,1,0:T(8,128)(2,1)}, bf16[3,512,128]{2,1,0:T(8,128)(2,1)}, bf16[8,6,512,128]{3,2...) custom-call(s32[2]{0:T(128)} %refs_0_.1, ...), custom_call_target="tpu_custom_call" | custom-call | tf_op jit(solution)/shard_map/forward_attention/pallas_call | solution.py:791
  110.7 89.9 %backward_attention.1 = (f32[48,384]{1,0:T(8,128)}, f32[48,384]{1,0:T(8,128)}, f32[48,384]{1,0:T(8,128)}, f32[48,384]{1,0:T(8,128)}, f32[48,1536]{1,0:T(8,128)},...) custom-call(bf16[512,384]{1,0:T(8,128)(2,1)} %get-tuple-element.57.refs_0_, ...), custom_call_target="tpu_custom_call" | custom-call | tf_op jit(solution)/shard_map/backward_attention/pallas_call | solution.py:1399
  200.5 3.2 %finish.1 = (f32[48,384]{1,0:T(8,128)}, f32[48,384]{1,0:T(8,128)}, f32[48,384]{1,0:T(8,128)}, f32[48,384]{1,0:T(8,128)}, f32[48,1536]{1,0:T(8,128)}, /*index=5*/...) custom-call(f32[16,768]{1,0:T(8,128)} %get-tuple-element.70.refs_0_,, ...), custom_call_target="tpu_custom_call" | custom-call | tf_op jit(solution)/shard_map/finish/pallas_call | solution.py:1494
